TPU v7x, 32 devices: a whole 2x2x4 slice. The times are simulated.
32 devices in a mesh: dp: 16 (over z, y, x), tensor: 2 (over core).
Axes of the slice: x: 2, y: 2, z: 4, core: 2. Of those that a mesh axis runs over, the one named last changes fastest.
Arguments:
- hidden_in: bfloat16 [2, 8192, 768], P(None, 'dp'), may hold values from -6 to 6
- positions: int32 [2, 8192], P(None, 'dp'), may hold values from 0 to 1999, as said below
- out_grad: bfloat16 [2, 8192, 768], P(None, 'dp'), may hold values from -6 to 6
- norm1_gain: float32 [768], replicated, may hold values from 0.5 to 1.5
- norm1_bias: float32 [768], replicated, may hold values from -3 to 3
- norm2_gain: float32 [768], replicated, may hold values from 0.5 to 1.5
- norm2_bias: float32 [768], replicated, may hold values from -3 to 3
- query_weight: bfloat16 [768, 768], P('dp', 'tensor'), may hold values from -0.21875 to 0.21875
- query_bias: float32 [768], P('tensor'), may hold values from -3 to 3
- keyval_weight: bfloat16 [768, 128], P('dp', 'tensor'), may hold values from -0.21875 to 0.21875
- keyval_bias: float32 [128], P('tensor'), may hold values from -3 to 3
- attn_out_weight: bfloat16 [768, 768], P('tensor', 'dp'), may hold values from -4 to 4
- attn_out_bias: float32 [768], replicated, may hold values from -2 to 2
- up_weight: bfloat16 [768, 3072], P('dp', 'tensor'), may hold values from -0.21875 to 0.21875
- up_bias: float32 [3072], P('tensor'), may hold values from -3 to 3
- down_weight: bfloat16 [3072, 768], P('tensor', 'dp'), may hold values from -0.109375 to 0.109375
- down_bias: float32 [768], replicated, may hold values from -2 to 2
Outputs:
- layer_out: bfloat16 [2, 8192, 768], P(None, 'dp')
- keyval_out: bfloat16 [2, 8192, 128], P(None, 'dp')
- input_grad: bfloat16 [2, 8192, 768], P(None, 'dp')
- grad_norm1_gain: float32 [768], replicated
- grad_norm1_bias: float32 [768], replicated
- grad_norm2_gain: float32 [768], replicated
- grad_norm2_bias: float32 [768], replicated
- grad_query_weight: float32 [768, 768], P('dp', 'tensor')
- grad_query_bias: float32 [768], P('tensor')
- grad_keyval_weight: float32 [768, 128], P('dp', 'tensor')
- grad_keyval_bias: float32 [128], P('tensor')
- grad_attn_out_weight: float32 [768, 768], P('tensor', 'dp')
- grad_attn_out_bias: float32 [768], replicated
- grad_up_weight: float32 [768, 3072], P('dp', 'tensor')
- grad_up_bias: float32 [3072], P('tensor')
- grad_down_weight: float32 [3072, 768], P('tensor', 'dp')
- grad_down_bias: float32 [768], replicated
Inputs may be any that keep to these rules, and one draw needn't show every extreme that they name: In each micro-batch's stream of 8192 tokens, positions count 0, 1, 2, ... within a document and restart at 0 where a new document begins; the stream begins with a document; every document except the last of a stream has 200 to 2000 tokens, and every stream holds a document of exactly 2000 tokens.
All inputs are finite; a program needn't handle non-finite values.
Results may differ from a plain program's by a relative error of at most 0.015.
Values may be sent and summed in bfloat16 or wider, within the bound.
A program may use at most 128 MiB of HBM per device.

v0:
```python
import jax
import jax.numpy as jnp
from jax import lax
from jax.sharding import PartitionSpec as P

HDIM = 64
ROT = 16
REACH = 4


epsilon = 1e-05


def shifted(value, axis, steps):
    count = lax.axis_size(axis)
    initial, last = (max(0, -steps), min(count, count - steps))
    return lax.ppermute(value, axis, [(source, source + steps) for source in range(initial, last)])


def norm_forward(stream):
    average = jnp.mean(stream, axis=-1, keepdims=True)
    centered = stream - average
    spread = jnp.mean(centered * centered, axis=-1, keepdims=True)
    scaling = lax.rsqrt(spread + epsilon)
    normed = centered * scaling
    return (normed, scaling)


def norm_backward(upstream, normed, scaling, norm_gain):
    weighted = upstream * norm_gain
    return scaling * (
        weighted
        - jnp.mean(weighted, axis=-1, keepdims=True)
        - normed * jnp.mean(weighted * normed, axis=-1, keepdims=True)
    )


def rotary_tables(places):
    inverse = 10000.0 ** (-(jnp.arange(ROT // 2, dtype=jnp.float32) * 2.0) / ROT)
    angles = places.astype(jnp.float32)[:, None] * inverse[None, :]
    angles = jnp.concatenate([angles, angles], axis=-1)
    return (jnp.cos(angles), jnp.sin(angles))


def rotate(values, cos_table, sine_table):
    head_part = values[..., :ROT]
    first_half = head_part[..., : ROT // 2]
    second_half = head_part[..., ROT // 2 :]
    turned = jnp.concatenate([-second_half, first_half], axis=-1)
    spun_part = head_part * cos_table[:, None, :] + turned * sine_table[:, None, :]
    return jnp.concatenate([spun_part, values[..., ROT:]], axis=-1)


def gelu_exact(values):
    return jax.nn.gelu(values, approximate=False)


def fetch_weights(shard_weights):
    return (
        lax.all_gather(shard_weights[0], "dp", axis=0, tiled=True),
        lax.all_gather(shard_weights[1], "dp", axis=0, tiled=True),
        lax.all_gather(shard_weights[2], "dp", axis=1, tiled=True),
        lax.all_gather(shard_weights[3], "dp", axis=0, tiled=True),
        lax.all_gather(shard_weights[4], "dp", axis=1, tiled=True),
    )


def score_block(queries, key_rows, places, reach_step):
    tokens_here = queries.shape[1]
    scores = jnp.einsum("htd,kd->htk", queries, key_rows, preferred_element_type=jnp.float32)
    row_ids = jnp.arange(tokens_here, dtype=jnp.int32)
    offsets = reach_step * tokens_here + row_ids[:, None] - row_ids[None, :]
    visible = (offsets >= 0) & (offsets <= places[:, None])
    return (scores, visible[None])


def attend_forward(queries, blocks, places):
    heads_here, tokens_here = (queries.shape[0], queries.shape[1])
    top_score = jnp.full((heads_here, tokens_here), -1e30, jnp.float32)
    totals = jnp.zeros((heads_here, tokens_here), jnp.float32)
    for reach_step, kv_block in enumerate(blocks):
        scores, visible = score_block(queries, kv_block[:, :HDIM], places, reach_step)
        masked = jnp.where(visible, scores, -1e30)
        new_top = jnp.maximum(top_score, jnp.max(masked, axis=-1))
        totals = totals * jnp.exp(top_score - new_top) + jnp.sum(
            jnp.where(visible, jnp.exp(masked - new_top[..., None]), 0.0), axis=-1
        )
        top_score = new_top
    log_sum = top_score + jnp.log(totals)
    mixture = jnp.zeros((heads_here, tokens_here, HDIM), jnp.float32)
    for reach_step, kv_block in enumerate(blocks):
        scores, visible = score_block(queries, kv_block[:, :HDIM], places, reach_step)
        weights_low = jnp.where(visible, jnp.exp(scores - log_sum[..., None]), 0.0).astype(
            jnp.bfloat16
        )
        mixture = mixture + jnp.einsum(
            "htk,kd->htd", weights_low, kv_block[:, HDIM:], preferred_element_type=jnp.float32
        )
    return (mixture, log_sum)


def attend_backward(queries, blocks, places, log_sum, grad_mixture, row_dots):
    grad_queries = jnp.zeros(queries.shape, jnp.float32)
    key_terms = []
    for reach_step, kv_block in enumerate(blocks):
        key_rows = kv_block[:, :HDIM]
        value_rows = kv_block[:, HDIM:]
        scores, visible = score_block(queries, key_rows, places, reach_step)
        weights_full = jnp.where(visible, jnp.exp(scores - log_sum[..., None]), 0.0)
        weights_low = weights_full.astype(jnp.bfloat16)
        grad_weights = jnp.einsum(
            "htd,kd->htk", grad_mixture, value_rows, preferred_element_type=jnp.float32
        )
        grad_scores = (weights_full * (grad_weights - row_dots[..., None])).astype(jnp.bfloat16)
        grad_queries = grad_queries + jnp.einsum(
            "htk,kd->htd", grad_scores, key_rows, preferred_element_type=jnp.float32
        )
        grad_keys = jnp.einsum(
            "htk,htd->kd", grad_scores, queries, preferred_element_type=jnp.float32
        )
        grad_values = jnp.einsum(
            "htk,htd->kd", weights_low, grad_mixture, preferred_element_type=jnp.float32
        )
        key_terms.append(jnp.concatenate([grad_keys, grad_values], axis=-1))
    return (grad_queries, key_terms)


def on_device(
    hidden_in,
    positions,
    out_grad,
    norm1_gain,
    norm1_bias,
    norm2_gain,
    norm2_bias,
    query_weight,
    query_bias,
    keyval_weight,
    keyval_bias,
    attn_out_weight,
    attn_out_bias,
    up_weight,
    up_bias,
    down_weight,
    down_bias,
):
    micro_count = hidden_in.shape[0]
    tokens_here = hidden_in.shape[1]
    width = hidden_in.shape[2]
    dp_count = lax.axis_size("dp")
    first_core = lax.axis_index("tensor") == 0
    heads_here = query_bias.shape[0] // HDIM
    query_scale = HDIM ** (-0.5)
    shard_weights = (query_weight, keyval_weight, attn_out_weight, up_weight, down_weight)
    gathered = None
    grad_query_w = jnp.zeros((width, query_weight.shape[1]), jnp.float32)
    grad_keyval_w = jnp.zeros((width, keyval_weight.shape[1]), jnp.float32)
    grad_out_w = jnp.zeros(
        (attn_out_weight.shape[0], attn_out_weight.shape[1] * dp_count), jnp.float32
    )
    grad_up_w = jnp.zeros((width, up_weight.shape[1]), jnp.float32)
    grad_down_w = jnp.zeros((down_weight.shape[0], down_weight.shape[1] * dp_count), jnp.float32)
    grad_n1_gain = jnp.zeros((width,), jnp.float32)
    grad_n1_bias = jnp.zeros((width,), jnp.float32)
    grad_n2_gain = jnp.zeros((width,), jnp.float32)
    grad_n2_bias = jnp.zeros((width,), jnp.float32)
    grad_row_sum = jnp.zeros((width,), jnp.float32)
    grad_query_b = jnp.zeros(query_bias.shape, jnp.float32)
    grad_keyval_b = jnp.zeros(keyval_bias.shape, jnp.float32)
    grad_up_b = jnp.zeros(up_bias.shape, jnp.float32)
    layer_rows = []
    cache_rows = []
    input_rows = []
    for micro_step in range(micro_count):
        gathered = fetch_weights(shard_weights)
        w_query, w_keyval, w_out, w_up, w_down = gathered
        stream = hidden_in[micro_step].astype(jnp.float32)
        places = positions[micro_step]
        normed, scaling = norm_forward(stream)
        low_first = (normed * norm1_gain + norm1_bias).astype(jnp.bfloat16)
        low_second = (normed * norm2_gain + norm2_bias).astype(jnp.bfloat16)
        cos_table, sine_table = rotary_tables(places)
        query_lin = jnp.dot(low_first, w_query, preferred_element_type=jnp.float32) + query_bias
        queries = (
            rotate(query_lin.reshape(tokens_here, heads_here, HDIM), cos_table, sine_table)
            * query_scale
        ).astype(jnp.bfloat16)
        query_heads = jnp.transpose(queries, (1, 0, 2))
        half_lin = jnp.dot(low_first, w_keyval, preferred_element_type=jnp.float32) + keyval_bias
        spun_half = rotate(half_lin[:, None, :], cos_table, sine_table)[:, 0, :]
        half_low = jnp.where(first_core, spun_half, half_lin).astype(jnp.bfloat16)
        keyval = lax.all_gather(half_low, "tensor", axis=1, tiled=True)
        blocks = [keyval] + [
            shifted(keyval, "dp", reach_step) for reach_step in range(1, REACH + 1)
        ]
        mixture, log_sum = attend_forward(query_heads, blocks, places)
        mixture_low = (
            jnp.transpose(mixture, (1, 0, 2))
            .reshape(tokens_here, heads_here * HDIM)
            .astype(jnp.bfloat16)
        )
        up_lin = jnp.dot(low_second, w_up, preferred_element_type=jnp.float32) + up_bias
        active_low = gelu_exact(up_lin).astype(jnp.bfloat16)
        branch_part = jnp.dot(mixture_low, w_out, preferred_element_type=jnp.float32) + jnp.dot(
            active_low, w_down, preferred_element_type=jnp.float32
        )
        branches = lax.psum(branch_part.astype(jnp.bfloat16), "tensor").astype(jnp.float32)
        layer_rows.append((stream + branches + attn_out_bias + down_bias).astype(jnp.bfloat16))
        cache_rows.append(keyval)
        grad_low = out_grad[micro_step]
        grad_rows = grad_low.astype(jnp.float32)
        grad_row_sum = grad_row_sum + jnp.sum(grad_rows, axis=0)
        grad_out_w = grad_out_w + jnp.einsum(
            "th,td->hd", mixture_low, grad_low, preferred_element_type=jnp.float32
        )
        grad_down_w = grad_down_w + jnp.einsum(
            "tf,td->fd", active_low, grad_low, preferred_element_type=jnp.float32
        )
        grad_active = jnp.einsum("td,fd->tf", grad_low, w_down, preferred_element_type=jnp.float32)
        gelu_values, gelu_pull = jax.vjp(gelu_exact, up_lin)
        grad_up_low = gelu_pull(grad_active)[0].astype(jnp.bfloat16)
        grad_up_b = grad_up_b + jnp.sum(grad_up_low.astype(jnp.float32), axis=0)
        grad_up_w = grad_up_w + jnp.einsum(
            "td,tf->df", low_second, grad_up_low, preferred_element_type=jnp.float32
        )
        second_part = jnp.einsum("tf,df->td", grad_up_low, w_up, preferred_element_type=jnp.float32)
        grad_mix_low = jnp.einsum(
            "td,hd->th", grad_low, w_out, preferred_element_type=jnp.float32
        ).astype(jnp.bfloat16)
        grad_mixture = jnp.transpose(grad_mix_low.reshape(tokens_here, heads_here, HDIM), (1, 0, 2))
        row_dots = jnp.sum(grad_mixture.astype(jnp.float32) * mixture, axis=-1)
        grad_queries, key_terms = attend_backward(
            query_heads, blocks, places, log_sum, grad_mixture, row_dots
        )
        keyval_grad = key_terms[0]
        for reach_step in range(1, REACH + 1):
            keyval_grad = keyval_grad + shifted(
                key_terms[reach_step].astype(jnp.bfloat16), "dp", -reach_step
            ).astype(jnp.float32)
        half_grad = lax.psum_scatter(
            keyval_grad.astype(jnp.bfloat16), "tensor", scatter_dimension=1, tiled=True
        ).astype(jnp.float32)
        unspun_half = rotate(half_grad[:, None, :], cos_table, -sine_table)[:, 0, :]
        half_grad_low = jnp.where(first_core, unspun_half, half_grad).astype(jnp.bfloat16)
        grad_keyval_b = grad_keyval_b + jnp.sum(half_grad_low.astype(jnp.float32), axis=0)
        grad_keyval_w = grad_keyval_w + jnp.einsum(
            "td,tk->dk", low_first, half_grad_low, preferred_element_type=jnp.float32
        )
        query_rows = jnp.transpose(grad_queries, (1, 0, 2)) * query_scale
        grad_query_low = (
            rotate(query_rows, cos_table, -sine_table)
            .reshape(tokens_here, heads_here * HDIM)
            .astype(jnp.bfloat16)
        )
        grad_query_b = grad_query_b + jnp.sum(grad_query_low.astype(jnp.float32), axis=0)
        grad_query_w = grad_query_w + jnp.einsum(
            "td,tq->dq", low_first, grad_query_low, preferred_element_type=jnp.float32
        )
        first_part = jnp.einsum(
            "tq,dq->td", grad_query_low, w_query, preferred_element_type=jnp.float32
        ) + jnp.einsum("tk,dk->td", half_grad_low, w_keyval, preferred_element_type=jnp.float32)
        grad_first, grad_second = (
            lax.psum(first_part.astype(jnp.bfloat16), "tensor").astype(jnp.float32),
            lax.psum(second_part.astype(jnp.bfloat16), "tensor").astype(jnp.float32),
        )
        grad_n1_gain = grad_n1_gain + jnp.sum(grad_first * normed, axis=0)
        grad_n1_bias = grad_n1_bias + jnp.sum(grad_first, axis=0)
        grad_n2_gain = grad_n2_gain + jnp.sum(grad_second * normed, axis=0)
        grad_n2_bias = grad_n2_bias + jnp.sum(grad_second, axis=0)
        input_total = (
            grad_rows
            + norm_backward(grad_first, normed, scaling, norm1_gain)
            + norm_backward(grad_second, normed, scaling, norm2_gain)
        )
        input_rows.append(input_total.astype(jnp.bfloat16))
    summed_query, summed_keyval, summed_out, summed_up, summed_down = (
        lax.psum_scatter(grad_query_w, "dp", scatter_dimension=0, tiled=True),
        lax.psum_scatter(grad_keyval_w, "dp", scatter_dimension=0, tiled=True),
        lax.psum_scatter(grad_out_w, "dp", scatter_dimension=1, tiled=True),
        lax.psum_scatter(grad_up_w, "dp", scatter_dimension=0, tiled=True),
        lax.psum_scatter(grad_down_w, "dp", scatter_dimension=1, tiled=True),
    )
    vector_sums = lax.psum(
        (
            grad_n1_gain,
            grad_n1_bias,
            grad_n2_gain,
            grad_n2_bias,
            grad_row_sum,
            grad_query_b,
            grad_keyval_b,
            grad_up_b,
        ),
        "dp",
    )
    (
        sum_n1_gain,
        sum_n1_bias,
        sum_n2_gain,
        sum_n2_bias,
        sum_rows,
        sum_query_b,
        sum_keyval_b,
        sum_up_b,
    ) = vector_sums
    return (
        jnp.stack(layer_rows),
        jnp.stack(cache_rows),
        jnp.stack(input_rows),
        sum_n1_gain,
        sum_n1_bias,
        sum_n2_gain,
        sum_n2_bias,
        summed_query,
        sum_query_b,
        summed_keyval,
        sum_keyval_b,
        summed_out,
        sum_rows,
        summed_up,
        sum_up_b,
        summed_down,
        sum_rows,
    )


def solution(mesh):
    return jax.shard_map(
        on_device,
        mesh=mesh,
        in_specs=(
            P(None, "dp", None),
            P(None, "dp"),
            P(None, "dp", None),
            P(),
            P(),
            P(),
            P(),
            P("dp", "tensor"),
            P("tensor"),
            P("dp", "tensor"),
            P("tensor"),
            P("tensor", "dp"),
            P(),
            P("dp", "tensor"),
            P("tensor"),
            P("tensor", "dp"),
            P(),
        ),
        out_specs=(
            P(None, "dp", None),
            P(None, "dp", None),
            P(None, "dp", None),
            P(),
            P(),
            P(),
            P(),
            P("dp", "tensor"),
            P("tensor"),
            P("dp", "tensor"),
            P("tensor"),
            P("tensor", "dp"),
            P(),
            P("dp", "tensor"),
            P("tensor"),
            P("tensor", "dp"),
            P(),
        ),
        check_vma=False,
    )
```

profile of v0, /device:TPU:0, one launch (start us, length us, event | category | flops | bytes accessed | tf_op | source)
XLA Modules:
  0.0 1191.6 jit_solution(16865282871851822811)
XLA Ops:
  11.9 43.4 %all_gather.27 = bf16[768,64]{1,0:T(8,128)(2,1)S(1)} all-gather(bf16[48,64]{1,0:T(8,128)(2,1)S(1)} %copy-done.132), channel_id=1, replica_groups=mesh['dp'=16,'tensor'=2] {'dp'}, dimensions={0}, use_global_device_ids=true | all-gather | bytes 104448 | tf_op jit(solution)/shard_map/all_gather | solution.py:61
  66.9 6.1 collective-permute-start.3
  73.0 42.1 %all_gather.26 = bf16[768,384]{1,0:T(8,128)(2,1)S(1)} all-gather(bf16[48,384]{1,0:T(8,128)(2,1)S(1)} %copy-done.127), channel_id=1, replica_groups=mesh['dp'=16,'tensor'=2] {'dp'}, dimensions={0}, use_global_device_ids=true | all-gather | bytes 626688 | tf_op jit(solution)/shard_map/all_gather | solution.py:60
  117.3 39.0 %all_gather.29 = bf16[384,768]{0,1:T(8,128)(2,1)S(1)} all-gather(bf16[384,48]{0,1:T(8,128)(2,1)S(1)} %copy-done.128), channel_id=1, replica_groups=mesh['dp'=16,'tensor'=2] {'dp'}, dimensions={1}, use_global_device_ids=true | all-gather | bytes 626688 | tf_op jit(solution)/shard_map/all_gather | solution.py:62
  157.2 2.2 fusion.146
  172.2 4.5 collective-permute-start
  177.9 4.2 select_reduce_fusion.13
  182.8 2.9 select_reduce_fusion.4
  185.7 4.7 select_reduce_fusion.2
  190.5 3.1 select_reduce_fusion
  193.7 4.6 fusion.115
  205.7 2.2 fusion.203
  209.8 4.5 select_reduce_fusion.16
  214.3 4.5 select_reduce_fusion.17
  218.9 4.6 select_reduce_fusion.18
  224.1 2.6 select_reduce_fusion.9
  226.7 6.1 select_reduce_fusion.7
  232.8 4.7 select_reduce_fusion.5
  237.7 3.0 fusion.216
  240.7 4.7 fusion.107
  245.4 4.7 fusion.109
  260.0 5.1 convolution_add_fusion.11
  265.1 4.0 multiply_reduce_fusion
  269.2 4.6 multiply_convert_fusion.4
  273.8 4.9 multiply_convert_fusion.3
  281.8 4.6 multiply_convert_fusion.2
  289.5 3.0 multiply_convert_fusion.1
  304.9 2.2 fusion.209
  307.1 2.2 fusion.206
  309.4 2.3 convolution_add_fusion.13
  311.7 3.1 multiply_reduce_fusion.1
  314.8 4.3 multiply_convert_fusion.9
  319.1 2.7 multiply_convert_fusion.8
  324.5 2.7 multiply_convert_fusion.7
  328.3 2.7 multiply_convert_fusion.6
  332.1 2.7 multiply_convert_fusion.5
  342.5 2.9 convolution_bitcast_fusion.19
  346.2 3.2 collective-permute-done.10
  349.4 3.4 collective-permute-done.11
  355.0 2.7 fusion.244
  386.2 37.2 %all-gather.3.cloned.1.call-done = bf16[768,1536]{1,0:T(8,128)(2,1)} async-done(((bf16[48,1536]{1,0:T(8,128)(2,1)}), bf16[768,1536]{1,0:T(8,128)(2,1)}) %all-gather.3.cloned.1.call-update) | async-done | bytes 2359312 | tf_op jit(solution)/shard_map/all_gather | solution.py:63
  423.4 11.8 multiply_convert_fusion.11
  435.2 51.7 %all-gather.5.cloned.1.call-done = bf16[1536,768]{0,1:T(8,128)(2,1)} async-done(((bf16[1536,48]{0,1:T(8,128)(2,1)}), bf16[1536,768]{0,1:T(8,128)(2,1)}) %all-gather.5.cloned.1.call-update) | async-done | bytes 2359312 | tf_op jit(solution)/shard_map/all_gather | solution.py:64
  486.9 3.2 fusion.315
  491.9 7.9 multiply_convert_fusion.10
  502.9 3.0 convert_reduce_fusion
  505.9 2.3 convolution_convert_fusion
  509.6 2.8 convert_reduce_fusion.1
  513.5 2.3 convolution_convert_fusion.1
  517.5 2.3 convolution_add_fusion.16
  522.0 2.6 convolution_add_fusion.5
  528.1 3.2 fusion.300
  531.3 3.9 convolution_add_fusion.1
  535.5 3.2 fusion.163
  538.7 3.8 convolution_add_fusion
  547.4 4.4 fusion.90
  551.9 2.8 convert_reduce_fusion.8
  554.8 73.9 %all-reduce = (f32[768]{0:T(1024)}, f32[768]{0:T(1024)}, f32[768]{0:T(1024)}, f32[768]{0:T(1024)}, f32[384]{0:T(512)}, /*index=5*/f32[64]{0:T(128)}, f32[768]{0:T(1024)S(1)}, f32[1536]{0:T(1024)}) all-reduce(f32[768]{0:T(1024)S(1)} %add.617, f32[768]{0:T(1024)S(1)} %add.618, ...), channel_id=1, replica_groups=mesh['dp'=16,'tensor'=2] {'dp'}, use_global_device_ids=true, to_apply=%region_44.45 | all-reduce | flops 5824 | bytes 46592 | tf_op jit(solution)/shard_map/psum | solution.py:283
  628.8 3.1 fusion.152
  634.5 7.6 reduce-scatter.14.cloned.1.call-done
  642.1 128.2 %reduce-scatter.12.cloned.1.call-done = f32[48,384]{1,0:T(8,128)} async-done(((f32[768,384]{1,0:T(8,128)}), f32[48,384]{1,0:T(8,128)}) %reduce-scatter.12.cloned.1.call-update) | async-done | bytes 73744 | tf_op jit(solution)/shard_map/reduce_scatter | solution.py:277
  770.3 128.1 %reduce-scatter.16.cloned.1.call-done = f32[384,48]{0,1:T(8,128)} async-done(((f32[384,768]{0,1:T(8,128)}), f32[384,48]{0,1:T(8,128)}) %reduce-scatter.16.cloned.1.call-update) | async-done | bytes 73744 | tf_op jit(solution)/shard_map/reduce_scatter | solution.py:279
  898.4 142.2 %reduce-scatter.18.cloned.1.call-done = f32[48,1536]{1,0:T(8,128)} async-done(((f32[768,1536]{1,0:T(8,128)}), f32[48,1536]{1,0:T(8,128)}) %reduce-scatter.18.cloned.1.call-update) | async-done | bytes 294928 | tf_op jit(solution)/shard_map/reduce_scatter | solution.py:280
  1040.6 143.1 %reduce-scatter.20.cloned.1.call-done = f32[1536,48]{0,1:T(8,128)} async-done(((f32[1536,768]{0,1:T(8,128)}), f32[1536,48]{0,1:T(8,128)}) %reduce-scatter.20.cloned.1.call-update) | async-done | bytes 294928 | tf_op jit(solution)/shard_map/reduce_scatter | solution.py:281
  (511 shorter events, 137.0 us)
Async XLA Ops:
  8.0 47.3 %copy-start.1 = (bf16[2,512,768]{2,1,0:T(8,128)(2,1)S(1)}, bf16[2,512,768]{2,1,0:T(8,128)(2,1)}, u32[]{:S(2)}) copy-start(bf16[2,512,768]{2,1,0:T(8,128)(2,1)} %param.17) | copy-start | bytes 4718596
  8.0 47.3 %copy-start.118 = (f32[768]{0:T(1024)S(1)}, f32[768]{0:T(1024)}, u32[]{:S(2)}) copy-start(f32[768]{0:T(1024)} %param.20) | copy-start | bytes 9220
  8.1 47.3 %copy-start.133 = (f32[768]{0:T(1024)S(1)}, f32[768]{0:T(1024)}, u32[]{:S(2)}) copy-start(f32[768]{0:T(1024)} %param.21) | copy-start | bytes 9220
  8.1 47.3 %copy-start.139 = (f32[64]{0:T(128)S(1)}, f32[64]{0:T(128)}, u32[]{:S(2)}) copy-start(f32[64]{0:T(128)} %param.27) | copy-start | bytes 772
  8.1 47.9 %copy-start.137 = (s32[2,512]{1,0:T(2,128)S(1)}, s32[2,512]{1,0:T(2,128)}, u32[]{:S(2)}) copy-start(s32[2,512]{1,0:T(2,128)} %param.18) | copy-start | bytes 12292
  8.1 369.0 %reduce-scatter.10.cloned.1.call-start = ((), (), s32[]{:S(2)}) async-start(), calls=%async_computation.10 | async-start | bytes 196608 | tf_op jit(solution)/shard_map/reduce_scatter | solution.py:240
  9.9 105.2 %copy-start.106 = (f32[512]{0:T(512)}, f32[512]{0:T(512)S(1)}, u32[]{:S(2)}) copy-start(f32[512]{0:T(512)S(1)} %broadcast_multiply_fusion.10) | copy-start | bytes 6148
  9.9 54.4 %copy-start.121 = (f32[512]{0:T(512)}, f32[512]{0:T(512)S(1)}, u32[]{:S(2)}) copy-start(f32[512]{0:T(512)S(1)} %broadcast_multiply_fusion.11) | copy-start | bytes 6148
  11.9 103.2 %copy-start.124 = (f32[512]{0:T(512)}, f32[512]{0:T(512)S(1)}, u32[]{:S(2)}) copy-start(f32[512]{0:T(512)S(1)} %add_rsqrt_fusion) | copy-start | bytes 6148
  55.4 9.5 copy-start.47
  55.4 17.6 %copy-start.127 = (bf16[48,384]{1,0:T(8,128)(2,1)S(1)}, bf16[48,384]{1,0:T(8,128)(2,1)}, u32[]{:S(2)}) copy-start(bf16[48,384]{1,0:T(8,128)(2,1)} %param.24) | copy-start | bytes 110596
  55.4 59.8 %copy-start.143 = (f32[384]{0:T(512)S(1)}, f32[384]{0:T(512)}, u32[]{:S(2)}) copy-start(f32[384]{0:T(512)} %param.25) | copy-start | bytes 4612
  56.1 16.9 %copy-start.99 = (f32[512,1,8]{0,2,1:T(8,128)}, f32[512,1,8]{0,2,1:T(8,128)S(1)}, u32[]{:S(2)}) copy-start(f32[512,1,8]{0,2,1:T(8,128)S(1)} %get-tuple-element.130) | copy-start | bytes 49156
  58.7 296.3 %copy-start.55 = (bf16[512,128]{0,1:T(8,128)(2,1)}, bf16[512,128]{0,1:T(8,128)(2,1)S(1)}, u32[]{:S(2)}) copy-start(bf16[512,128]{0,1:T(8,128)(2,1)S(1)} %all_gather.32) | copy-start | bytes 393220
  58.7 107.2 %collective-permute-start.7 = (bf16[512,128]{0,1:T(8,128)(2,1)S(1)}, bf16[512,128]{0,1:T(8,128)(2,1)S(1)}, u32[]{:S(2)}, u32[]{:S(2)}) collective-permute-start(bf16[512,128]{0,1:T(8,128)(2,1)S(1)} %all_gather.32), channel_id=1, source_target_pairs={{0,8},{2,10},{4,12},{6,14},{8,16},{10,18},{12,20},{14,22},{16,24},... | collective-permute-start | bytes 393224 | tf_op jit(solution)/shard_map/ppermute | solution.py:17
  60.0 108.9 %collective-permute-start.6 = (bf16[512,128]{0,1:T(8,128)(2,1)S(1)}, bf16[512,128]{0,1:T(8,128)(2,1)S(1)}, u32[]{:S(2)}, u32[]{:S(2)}) collective-permute-start(bf16[512,128]{0,1:T(8,128)(2,1)S(1)} %all_gather.32), channel_id=1, source_target_pairs={{0,6},{2,8},{4,10},{6,12},{8,14},{10,16},{12,18},{14,20},{16,22},{... | collective-permute-start | bytes 393224 | tf_op jit(solution)/shard_map/ppermute | solution.py:17
  61.3 110.9 %collective-permute-start.5 = (bf16[512,128]{0,1:T(8,128)(2,1)S(1)}, bf16[512,128]{0,1:T(8,128)(2,1)S(1)}, u32[]{:S(2)}, u32[]{:S(2)}) collective-permute-start(bf16[512,128]{0,1:T(8,128)(2,1)S(1)} %all_gather.32), channel_id=1, source_target_pairs={{0,4},{2,6},{4,8},{6,10},{8,12},{10,14},{12,16},{14,18},{16,20},{1... | collective-permute-start | bytes 393224 | tf_op jit(solution)/shard_map/ppermute | solution.py:17
  62.6 115.2 %collective-permute-start.4 = (bf16[512,128]{0,1:T(8,128)(2,1)S(1)}, bf16[512,128]{0,1:T(8,128)(2,1)S(1)}, u32[]{:S(2)}, u32[]{:S(2)}) collective-permute-start(bf16[512,128]{0,1:T(8,128)(2,1)S(1)} %all_gather.32), channel_id=1, source_target_pairs={{0,2},{2,4},{4,6},{6,8},{8,10},{10,12},{12,14},{14,16},{16,18},{18... | collective-permute-start | bytes 393224 | tf_op jit(solution)/shard_map/ppermute | solution.py:17
  64.3 51.7 %copy-start.22 = (bf16[512,768]{1,0:T(8,128)(2,1)}, bf16[512,768]{1,0:T(8,128)(2,1)S(1)}, u32[]{:S(2)}) copy-start(bf16[512,768]{1,0:T(8,128)(2,1)S(1)} %fusion.51) | copy-start | bytes 2359300
  66.9 141.0 %collective-permute-start.3 = (bf16[512,128]{0,1:T(8,128)(2,1)}, bf16[512,128]{0,1:T(8,128)(2,1)}, u32[]{:S(2)}, u32[]{:S(2)}) collective-permute-start(bf16[512,128]{0,1:T(8,128)(2,1)} %all_gather.28), channel_id=1, source_target_pairs={{0,8},{2,10},{4,12},{6,14},{8,16},{10,18},{12,20},{14,22},{16,24},... | collective-permute-start | bytes 393224 | tf_op jit(solution)/shard_map/ppermute | solution.py:17
  117.3 39.8 %copy-start.84 = (f32[512,16]{0,1:T(8,128)}, f32[512,16]{0,1:T(8,128)S(1)}, u32[]{:S(2)}) copy-start(f32[512,16]{0,1:T(8,128)S(1)} %get-tuple-element.122) | copy-start | bytes 98308
  156.3 8.3 copy-start.24
  159.4 8.4 copy-start.30
  159.4 11.7 copy-start.34
  159.5 17.3 %copy-start.37 = (pred[512,512]{0,1:T(8,128)(4,1)}, pred[512,512]{0,1:T(8,128)(4,1)S(1)}, u32[]{:S(2)}) copy-start(pred[512,512]{0,1:T(8,128)(4,1)S(1)} %get-tuple-element.138) | copy-start | bytes 786436
  159.5 18.4 %copy-start.40 = (pred[512,512]{0,1:T(8,128)(4,1)}, pred[512,512]{0,1:T(8,128)(4,1)S(1)}, u32[]{:S(2)}) copy-start(pred[512,512]{0,1:T(8,128)(4,1)S(1)} %get-tuple-element.136) | copy-start | bytes 786436
  161.3 20.8 %copy-start.88 = (f32[6,512]{1,0:T(8,128)}, f32[6,512]{1,0:T(8,128)S(1)}, u32[]{:S(2)}) copy-start(f32[6,512]{1,0:T(8,128)S(1)} %get-tuple-element.164) | copy-start | bytes 36868
  165.9 43.9 %collective-permute-start.2 = (bf16[512,128]{0,1:T(8,128)(2,1)}, bf16[512,128]{0,1:T(8,128)(2,1)}, u32[]{:S(2)}, u32[]{:S(2)}) collective-permute-start(bf16[512,128]{0,1:T(8,128)(2,1)} %all_gather.28), channel_id=1, source_target_pairs={{0,6},{2,8},{4,10},{6,12},{8,14},{10,16},{12,18},{14,20},{16,22},{... | collective-permute-start | bytes 393224 | tf_op jit(solution)/shard_map/ppermute | solution.py:17
  169.0 45.4 %collective-permute-start.1 = (bf16[512,128]{0,1:T(8,128)(2,1)}, bf16[512,128]{0,1:T(8,128)(2,1)}, u32[]{:S(2)}, u32[]{:S(2)}) collective-permute-start(bf16[512,128]{0,1:T(8,128)(2,1)} %all_gather.28), channel_id=1, source_target_pairs={{0,4},{2,6},{4,8},{6,10},{8,12},{10,14},{12,16},{14,18},{16,20},{1... | collective-permute-start | bytes 393224 | tf_op jit(solution)/shard_map/ppermute | solution.py:17
  172.2 46.6 %collective-permute-start = (bf16[512,128]{0,1:T(8,128)(2,1)}, bf16[512,128]{0,1:T(8,128)(2,1)}, u32[]{:S(2)}, u32[]{:S(2)}) collective-permute-start(bf16[512,128]{0,1:T(8,128)(2,1)} %all_gather.28), channel_id=1, source_target_pairs={{0,2},{2,4},{4,6},{6,8},{8,10},{10,12},{12,14},{14,16},{16,18},{18... | collective-permute-start | bytes 393224 | tf_op jit(solution)/shard_map/ppermute | solution.py:17
  177.8 20.4 %copy-start = (f32[6,512,512]{1,2,0:T(8,128)}, f32[6,512,512]{1,2,0:T(8,128)S(1)}, u32[]{:S(2)}) copy-start(f32[6,512,512]{1,2,0:T(8,128)S(1)} %get-tuple-element.161) | copy-start | bytes 18874372
  240.7 9.4 slice-start
  280.5 56.1 %collective-permute-start.12 = (bf16[512,128]{0,1:T(8,128)(2,1)}, bf16[512,128]{0,1:T(8,128)(2,1)}, u32[]{:S(2)}, u32[]{:S(2)}) collective-permute-start(bf16[512,128]{0,1:T(8,128)(2,1)} %pad_maximum_fusion.7), channel_id=1, source_target_pairs={{2,0},{4,2},{6,4},{8,6},{10,8},{12,10},{14,12},{16,14},{18,16},{20... | collective-permute-start | bytes 393224 | tf_op jit(solution)/shard_map/ppermute | solution.py:17
  288.2 49.7 %collective-permute-start.13 = (bf16[512,128]{0,1:T(8,128)(2,1)}, bf16[512,128]{0,1:T(8,128)(2,1)}, u32[]{:S(2)}, u32[]{:S(2)}) collective-permute-start(bf16[512,128]{0,1:T(8,128)(2,1)} %pad_maximum_fusion.8), channel_id=1, source_target_pairs={{4,0},{6,2},{8,4},{10,6},{12,8},{14,10},{16,12},{18,14},{20,16},{2... | collective-permute-start | bytes 393224 | tf_op jit(solution)/shard_map/ppermute | solution.py:17
  295.3 9.5 slice-start.2
  296.0 8.9 slice-start.3
  296.0 43.2 %collective-permute-start.14 = (bf16[512,128]{0,1:T(8,128)(2,1)}, bf16[512,128]{0,1:T(8,128)(2,1)}, u32[]{:S(2)}, u32[]{:S(2)}) collective-permute-start(bf16[512,128]{0,1:T(8,128)(2,1)} %pad_maximum_fusion.9), channel_id=1, source_target_pairs={{6,0},{8,2},{10,4},{12,6},{14,8},{16,10},{18,12},{20,14},{22,16},{... | collective-permute-start | bytes 393224 | tf_op jit(solution)/shard_map/ppermute | solution.py:17
  301.3 39.3 %collective-permute-start.15 = (bf16[512,128]{0,1:T(8,128)(2,1)}, bf16[512,128]{0,1:T(8,128)(2,1)}, u32[]{:S(2)}, u32[]{:S(2)}) collective-permute-start(bf16[512,128]{0,1:T(8,128)(2,1)} %pad_maximum_fusion.10), channel_id=1, source_target_pairs={{8,0},{10,2},{12,4},{14,6},{16,8},{18,10},{20,12},{22,14},{24,16},... | collective-permute-start | bytes 393224 | tf_op jit(solution)/shard_map/ppermute | solution.py:17
  323.0 22.5 %collective-permute-start.8 = (bf16[512,128]{0,1:T(8,128)(2,1)S(1)}, bf16[512,128]{0,1:T(8,128)(2,1)S(1)}, u32[]{:S(2)}, u32[]{:S(2)}) collective-permute-start(bf16[512,128]{0,1:T(8,128)(2,1)S(1)} %pad_maximum_fusion.3), channel_id=1, source_target_pairs={{2,0},{4,2},{6,4},{8,6},{10,8},{12,10},{14,12},{16,14},{18,16},{20... | collective-permute-start | bytes 393224 | tf_op jit(solution)/shard_map/ppermute | solution.py:17
  336.5 16.2 %copy-start.103 = (f32[512,64]{0,1:T(8,128)S(1)}, f32[512,64]{0,1:T(8,128)}, u32[]{:S(2)}) copy-start(f32[512,64]{0,1:T(8,128)} %convolution_bitcast_fusion.18) | copy-start | bytes 393220
  336.6 9.6 collective-permute-start.9
  337.9 11.5 collective-permute-start.10
  339.2 13.5 %collective-permute-start.11 = (bf16[512,128]{0,1:T(8,128)(2,1)S(1)}, bf16[512,128]{0,1:T(8,128)(2,1)S(1)}, u32[]{:S(2)}, u32[]{:S(2)}) collective-permute-start(bf16[512,128]{0,1:T(8,128)(2,1)S(1)} %pad_maximum_fusion.6), channel_id=1, source_target_pairs={{8,0},{10,2},{12,4},{14,6},{16,8},{18,10},{20,12},{22,14},{24,16},... | collective-permute-start | bytes 393224 | tf_op jit(solution)/shard_map/ppermute | solution.py:17
  342.4 36.2 %reduce-scatter.8.cloned.1.call-start = ((), (), s32[]{:S(2)}) async-start(), calls=%async_computation.9 | async-start | bytes 196608 | tf_op jit(solution)/shard_map/reduce_scatter | solution.py:240
  345.4 12.3 %copy-start.78 = (bf16[512,128]{0,1:T(8,128)(2,1)S(1)}, bf16[512,128]{0,1:T(8,128)(2,1)}, u32[]{:S(2)}) copy-start(bf16[512,128]{0,1:T(8,128)(2,1)} %copy-done.76) | copy-start | bytes 393220
  353.5 69.9 %all-gather.3.cloned.1.call-start = ((), (), s32[]{:S(2)}) async-start(), calls=%async_computation.7 | async-start | bytes 2506752 | tf_op jit(solution)/shard_map/all_gather | solution.py:63
  354.1 132.8 %all-gather.5.cloned.1.call-start = ((), (), s32[]{:S(2)}) async-start(), calls=%async_computation.8 | async-start | bytes 2506752 | tf_op jit(solution)/shard_map/all_gather | solution.py:64
  354.7 192.6 %all-reduce.4.cloned.1.call-start = ((), (), s32[]{:S(2)}) async-start(), calls=%async_computation.16 | async-start | bytes 9437184 | tf_op jit(solution)/shard_map/psum | solution.py:207
  373.7 10.0 copy-start.48
  378.6 44.9 %copy-start.87 = (f32[768]{0:T(1024)S(1)}, f32[768]{0:T(1024)}, u32[]{:S(2)}) copy-start(f32[768]{0:T(1024)} %param.22) | copy-start | bytes 9220
  378.6 44.9 %copy-start.120 = (f32[768]{0:T(1024)S(1)}, f32[768]{0:T(1024)}, u32[]{:S(2)}) copy-start(f32[768]{0:T(1024)} %param.23) | copy-start | bytes 9220
  378.6 44.9 %copy-start.122 = (f32[512]{0:T(512)S(1)}, f32[512]{0:T(512)}, u32[]{:S(2)}) copy-start(f32[512]{0:T(512)} %copy-done.121) | copy-start | bytes 6148
  378.6 44.9 %copy-start.130 = (f32[512]{0:T(512)S(1)}, f32[512]{0:T(512)}, u32[]{:S(2)}) copy-start(f32[512]{0:T(512)} %copy-done.129) | copy-start | bytes 6148
  435.2 54.8 %copy-start.54 = (bf16[512,1536]{1,0:T(8,128)(2,1)}, bf16[512,1536]{1,0:T(8,128)(2,1)S(1)}, u32[]{:S(2)}) copy-start(bf16[512,1536]{1,0:T(8,128)(2,1)S(1)} %get-tuple-element.88) | copy-start | bytes 4718596
  491.9 7.9 copy-start.141
  515.9 126.2 %reduce-scatter.14.cloned.1.call-start = ((), (), s32[]{:S(2)}) async-start(), calls=%async_computation.12 | async-start | bytes 417792 | tf_op jit(solution)/shard_map/reduce_scatter | solution.py:278
  519.8 250.5 %reduce-scatter.12.cloned.1.call-start = ((), (), s32[]{:S(2)}) async-start(), calls=%async_computation.11 | async-start | bytes 1253376 | tf_op jit(solution)/shard_map/reduce_scatter | solution.py:277
  524.6 373.8 %reduce-scatter.16.cloned.1.call-start = ((), (), s32[]{:S(2)}) async-start(), calls=%async_computation.13 | async-start | bytes 1253376 | tf_op jit(solution)/shard_map/reduce_scatter | solution.py:279
  528.0 512.6 %reduce-scatter.18.cloned.1.call-start = ((), (), s32[]{:S(2)}) async-start(), calls=%async_computation.14 | async-start | bytes 5013504 | tf_op jit(solution)/shard_map/reduce_scatter | solution.py:280
  535.2 648.5 %reduce-scatter.20.cloned.1.call-start = ((), (), s32[]{:S(2)}) async-start(), calls=%async_computation.15 | async-start | bytes 5013504 | tf_op jit(solution)/shard_map/reduce_scatter | solution.py:281
  551.8 76.9 %copy-start.131 = (f32[512]{0:T(512)S(1)}, f32[512]{0:T(512)}, u32[]{:S(2)}) copy-start(f32[512]{0:T(512)} %copy-done.129) | copy-start | bytes 6148
  551.8 76.9 %copy-start.135 = (f32[768]{0:T(1024)S(1)}, f32[768]{0:T(1024)}, u32[]{:S(2)}) copy-start(f32[768]{0:T(1024)} %param.33) | copy-start | bytes 9220
  551.8 76.9 %copy-start.136 = (f32[768]{0:T(1024)S(1)}, f32[768]{0:T(1024)}, u32[]{:S(2)}) copy-start(f32[768]{0:T(1024)} %param.29) | copy-start | bytes 9220
  628.7 555.0 %copy-start.138 = (f32[768]{0:T(1024)}, f32[768]{0:T(1024)S(1)}, u32[]{:S(2)}) copy-start(f32[768]{0:T(1024)S(1)} %get-tuple-element.215) | copy-start | bytes 9220
  (119 other events, 364.2 us)
Sparse Core Ops, SparseCore 0:
  342.6 18.7 reduce-scatter.9
  364.1 8.6 reduce-scatter.7
  516.0 28.1 all-reduce.3
Sparse Core Ops, SparseCore 1:
  356.8 66.5 all-gather.2
  426.1 60.8 all-gather.4
  522.3 119.7 reduce-scatter.13
  647.4 122.8 reduce-scatter.11
  775.6 122.7 reduce-scatter.15
  904.2 136.4 reduce-scatter.17
  1047.1 136.6 reduce-scatter.19
where the time goes:
time: 1200 us; the launch traced here: 1190 us
  waiting for transfers between devices  647 us (54%)
  matrix products  216 us (18%)
  blocking collectives  202 us (17%)
  other arithmetic  62.4 us (5%)
  starting transfers between devices  32 us (3%)
  between operations  18 us (2%)
  local copies, waits for them, and re-layouts  14.6 us (1%)
    reduce_scatter x1, waiting for transfers between devices, on_device(): lax.psum_scatter(grad_down_w, 'dp', scatter_dimension=1, tiled=True)  143 us
    reduce_scatter x1, waiting for transfers between devices, on_device(): lax.psum_scatter(grad_up_w, 'dp', scatter_dimension=0, tiled=True)  142 us
    reduce_scatter x1, waiting for transfers between devices, on_device(): lax.psum_scatter(grad_query_w, 'dp', scatter_dimension=0, tiled=True)  128 us
    reduce_scatter x1, waiting for transfers between devices, on_device(): lax.psum_scatter(grad_out_w, 'dp', scatter_dimension=1, tiled=True)  128 us
    psum x1, blocking collectives, on_device(): lax.psum((grad_n1_gain, grad_n1_bias, grad_n2_gain, grad_n2_bias, grad_ro...  73.9 us
    all_gather x1, waiting for transfers between devices, fetch_weights(): lax.all_gather(shard_weights[4], 'dp', axis=1, tiled=True)  51.7 us
    all_gather x1, blocking collectives, fetch_weights(): lax.all_gather(shard_weights[1], 'dp', axis=0, tiled=True)  43.4 us
    all_gather x1, blocking collectives, fetch_weights(): lax.all_gather(shard_weights[0], 'dp', axis=0, tiled=True)  42.1 us
  transfers between devices with their start and end apart: 26, of which 10 were waited for; matrix products, arithmetic and copies ran while one was open for 16% of the time, Pallas kernels for 0%

commit v1 on v0

--- a/solution.py
+++ b/solution.py
@@ -1,6 +1,10 @@
+import functools
+
 import jax
 import jax.numpy as jnp
 from jax import lax
+from jax.experimental import pallas as pl
+from jax.experimental.pallas import tpu as pltpu
 from jax.sharding import PartitionSpec as P
 
 HDIM = 64
@@ -55,14 +59,183 @@
     return jax.nn.gelu(values, approximate=False)
 
 
+MESH = pl.DeviceIdType.MESH
+
+
+def grid_place():
+    me = lax.axis_index("dp")
+    return me // 4, (me // 2) % 2, me % 2
+
+
+def place_id(z, y, x):
+    return {"dp": z * 4 + y * 2 + x}
+
+
+def barrier(peers):
+    b=pltpu.get_barrier_semaphore()
+    for p in peers:
+        pl.semaphore_signal(b,inc=1,device_id=p,device_id_type=MESH)
+    pl.semaphore_wait(b,len(peers))
+
+def gather_kernel(chunks, in_ref, out_ref, zs, zr, s2s, s2r, s3s, s3r):
+    z,y,x=grid_place()
+    peers=[place_id((z+d)%4,y,x) for d in (1,2,3)]+[place_id(z,1-y,x),place_id(z,y,1-x)]
+    barrier(peers)
+    def rc(src,dst,ss,rs,d):
+        return pltpu.make_async_remote_copy(src_ref=src,dst_ref=dst,send_sem=ss,recv_sem=rs,device_id=d,device_id_type=MESH)
+    C={}
+    def s1(k):
+        c0,c1=chunks[k]; cs=pl.ds(c0,c1-c0)
+        C[k,1]=[rc(in_ref.at[:,cs],out_ref.at[z,y,x,:,cs],zs.at[k,d-1],zr.at[k,d-1],place_id((z+d)%4,y,x)) for d in (1,2,3)]
+        for c in C[k,1]: c.start()
+    def s2(k):
+        for c in C[k,1]: c.wait_recv()
+        c0,c1=chunks[k]; cs=pl.ds(c0,c1-c0)
+        r=out_ref.at[:,y,x,:,cs]
+        C[k,2]=rc(r,r,s2s.at[k],s2r.at[k],place_id(z,y,1-x) if k%2==0 else place_id(z,1-y,x))
+        C[k,2].start()
+    def s3(k):
+        C[k,2].wait_recv()
+        c0,c1=chunks[k]; cs=pl.ds(c0,c1-c0)
+        if k%2==0:
+            r=out_ref.at[:,y,:,:,cs]; d=place_id(z,1-y,x)
+        else:
+            r=out_ref.at[:,:,x,:,cs]; d=place_id(z,y,1-x)
+        C[k,3]=rc(r,r,s3s.at[k],s3r.at[k],d)
+        C[k,3].start()
+    out_ref[z,y,x]=in_ref[...]
+    n=len(chunks)
+    for k in range(n): s1(k)
+    for t in range(n+1):
+        if t<n: s2(t)
+        if t>=1: s3(t-1)
+    for k in range(n):
+        C[k,3].wait_recv()
+    for k in range(n):
+        for c in C[k,1]: c.wait_send()
+        C[k,2].wait_send(); C[k,3].wait_send()
+
+def gather(shard, chunks):
+    rows,cols=shard.shape
+    n=len(chunks)
+    D=pltpu.SemaphoreType.DMA
+    return pl.pallas_call(functools.partial(gather_kernel,chunks),
+        out_shape=jax.ShapeDtypeStruct((4,2,2,rows,cols),shard.dtype),
+        in_specs=[pl.BlockSpec(memory_space=pltpu.VMEM)],
+        out_specs=pl.BlockSpec(memory_space=pltpu.VMEM),
+        scratch_shapes=[D((n,3)),D((n,3)),D((n,)),D((n,)),D((n,)),D((n,))],
+        compiler_params=pltpu.CompilerParams(collective_id=0,has_side_effects=True,vmem_limit_bytes=40<<20),
+        name="gather_w")(shard)
+
+def rs_kernel(chunks, g_ref, out_ref, r1, r2, r3, s1s,s1r,s2s,s2r,zs,zr):
+    z,y,x=grid_place()
+    peers=[place_id((z+d)%4,y,x) for d in (1,2,3)]+[place_id(z,1-y,x),place_id(z,y,1-x)]
+    barrier(peers)
+    def rc(src,dst,ss,rs,d):
+        return pltpu.make_async_remote_copy(src_ref=src,dst_ref=dst,send_sem=ss,recv_sem=rs,device_id=d,device_id_type=MESH)
+    C={}
+    def cs_of(k):
+        c0,c1=chunks[k]; return pl.ds(c0,c1-c0)
+    def a(k):
+        cs=cs_of(k)
+        if k%2==0: src=g_ref.at[:,:,1-x,:,cs]; d=place_id(z,y,1-x)
+        else: src=g_ref.at[:,1-y,:,:,cs]; d=place_id(z,1-y,x)
+        C[k,1]=rc(src,r1.at[:,:,:,cs],s1s.at[k],s1r.at[k],d); C[k,1].start()
+    def b(k):
+        C[k,1].wait_recv()
+        cs=cs_of(k)
+        def body(i,_):
+            zz=i//2; yy=i%2
+            mine=g_ref[zz,yy,x,:,cs] if k%2==0 else g_ref[zz,y,yy,:,cs]
+            r1[zz,yy,:,cs]=r1[zz,yy,:,cs]+mine
+            return 0
+        lax.fori_loop(0,8,body,0)
+        o=y if k%2==0 else x
+        d=place_id(z,1-y,x) if k%2==0 else place_id(z,y,1-x)
+        C[k,2]=rc(r1.at[:,1-o,:,cs],r2.at[:,:,cs],s2s.at[k],s2r.at[k],d); C[k,2].start()
+    def c(k):
+        C[k,2].wait_recv()
+        cs=cs_of(k)
+        o=y if k%2==0 else x
+        def body(i,_):
+            r2[i,:,cs]=r2[i,:,cs]+r1[i,o,:,cs]
+            return 0
+        lax.fori_loop(0,4,body,0)
+        C[k,3]=[rc(r2.at[(z+d)%4,:,cs],r3.at[d-1,:,cs],zs.at[k,d-1],zr.at[k,d-1],place_id((z+d)%4,y,x)) for d in (1,2,3)]
+        for q in C[k,3]: q.start()
+    def e(k):
+        cs=cs_of(k)
+        for q in C[k,3]: q.wait_recv()
+        out_ref[:,cs]=(r2[z,:,cs].astype(jnp.float32)+r3[0,:,cs].astype(jnp.float32))+(r3[1,:,cs].astype(jnp.float32)+r3[2,:,cs].astype(jnp.float32))
+    n=len(chunks)
+    for k in range(n): a(k)
+    for t in range(n+2):
+        if t<n: b(t)
+        if 0<=t-1<n: c(t-1)
+        if 0<=t-2<n: e(t-2)
+    for k in range(n):
+        C[k,1].wait_send(); C[k,2].wait_send()
+        for q in C[k,3]: q.wait_send()
+
+def rscat(g, chunks):
+    _,_,_,rows,cols=g.shape
+    n=len(chunks)
+    D=pltpu.SemaphoreType.DMA
+    V=pltpu.VMEM
+    return pl.pallas_call(functools.partial(rs_kernel,chunks),
+        out_shape=jax.ShapeDtypeStruct((rows,cols),jnp.float32),
+        in_specs=[pl.BlockSpec(memory_space=pltpu.VMEM)],
+        out_specs=pl.BlockSpec(memory_space=pltpu.VMEM),
+        scratch_shapes=[V((4,2,rows,cols),jnp.bfloat16),V((4,rows,cols),jnp.bfloat16),V((3,rows,cols),jnp.bfloat16),
+            D((n,)),D((n,)),D((n,)),D((n,)),D((n,3)),D((n,3))],
+        compiler_params=pltpu.CompilerParams(collective_id=1,has_side_effects=True,vmem_limit_bytes=40<<20),
+        name="rscat_g")(g)
+
+def column_chunks(columns, parts):
+    width = columns // 128
+    edges = [round(i * width / parts) * 128 for i in range(parts + 1)]
+    return [(edges[i], edges[i + 1]) for i in range(parts)]
+
+
+def pack_columns(query_part, keyval_part, out_part, up_part, down_part):
+    packed = jnp.concatenate([query_part, out_part, up_part, down_part, keyval_part], axis=1)
+    pad = -packed.shape[1] % 128
+    return jnp.pad(packed, ((0, 0), (0, pad)))
+
+
+def unpack_columns(packed, widths):
+    pieces = []
+    at = 0
+    for width in widths:
+        pieces.append(packed[:, at : at + width])
+        at += width
+    query_part, out_part, up_part, down_part, keyval_part = pieces
+    return query_part, keyval_part, out_part, up_part, down_part
+
+
+def gather_rows(shard):
+    count = lax.axis_size("dp")
+    if count == 16 and shard.shape[0] % 16 == 0:
+        gathered = gather(shard, column_chunks(shard.shape[1], 8))
+        return gathered.reshape(count * shard.shape[0], shard.shape[1])
+    return lax.all_gather(shard, "dp", axis=0, tiled=True)
+
+
+def scatter_rows(partial):
+    count = lax.axis_size("dp")
+    rows = partial.shape[0] // count
+    if count == 16 and rows % 16 == 0:
+        return rscat(partial.reshape(4, 2, 2, rows, partial.shape[1]), column_chunks(partial.shape[1], 8))
+    return lax.psum_scatter(partial, "dp", scatter_dimension=0, tiled=True).astype(jnp.float32)
+
+
 def fetch_weights(shard_weights):
-    return (
-        lax.all_gather(shard_weights[0], "dp", axis=0, tiled=True),
-        lax.all_gather(shard_weights[1], "dp", axis=0, tiled=True),
-        lax.all_gather(shard_weights[2], "dp", axis=1, tiled=True),
-        lax.all_gather(shard_weights[3], "dp", axis=0, tiled=True),
-        lax.all_gather(shard_weights[4], "dp", axis=1, tiled=True),
-    )
+    query_w, keyval_w, out_w, up_w, down_w = shard_weights
+    packed = pack_columns(query_w, keyval_w, out_w.T, up_w, down_w.T)
+    widths = (query_w.shape[1], out_w.shape[0], up_w.shape[1], down_w.shape[0], keyval_w.shape[1])
+    full = gather_rows(packed)
+    w_query, w_keyval, w_out, w_up, w_down = unpack_columns(full, widths)
+    return (w_query, w_keyval, w_out.T, w_up, w_down.T)
 
 
 def score_block(queries, key_rows, places, reach_step):
@@ -152,7 +325,6 @@
     heads_here = query_bias.shape[0] // HDIM
     query_scale = HDIM ** (-0.5)
     shard_weights = (query_weight, keyval_weight, attn_out_weight, up_weight, down_weight)
-    gathered = None
     grad_query_w = jnp.zeros((width, query_weight.shape[1]), jnp.float32)
     grad_keyval_w = jnp.zeros((width, keyval_weight.shape[1]), jnp.float32)
     grad_out_w = jnp.zeros(
@@ -171,8 +343,8 @@
     layer_rows = []
     cache_rows = []
     input_rows = []
+    gathered = fetch_weights(shard_weights)
     for micro_step in range(micro_count):
-        gathered = fetch_weights(shard_weights)
         w_query, w_keyval, w_out, w_up, w_down = gathered
         stream = hidden_in[micro_step].astype(jnp.float32)
         places = positions[micro_step]
@@ -273,13 +445,22 @@
             + norm_backward(grad_second, normed, scaling, norm2_gain)
         )
         input_rows.append(input_total.astype(jnp.bfloat16))
-    summed_query, summed_keyval, summed_out, summed_up, summed_down = (
-        lax.psum_scatter(grad_query_w, "dp", scatter_dimension=0, tiled=True),
-        lax.psum_scatter(grad_keyval_w, "dp", scatter_dimension=0, tiled=True),
-        lax.psum_scatter(grad_out_w, "dp", scatter_dimension=1, tiled=True),
-        lax.psum_scatter(grad_up_w, "dp", scatter_dimension=0, tiled=True),
-        lax.psum_scatter(grad_down_w, "dp", scatter_dimension=1, tiled=True),
+    packed_grads = pack_columns(
+        grad_query_w, grad_keyval_w, grad_out_w.T, grad_up_w, grad_down_w.T
+    ).astype(jnp.bfloat16)
+    own_grads = scatter_rows(packed_grads)
+    summed_query, summed_keyval, summed_out, summed_up, summed_down = unpack_columns(
+        own_grads,
+        (
+            query_weight.shape[1],
+            attn_out_weight.shape[0],
+            up_weight.shape[1],
+            down_weight.shape[0],
+            keyval_weight.shape[1],
+        ),
     )
+    summed_out = summed_out.T
+    summed_down = summed_down.T
     vector_sums = lax.psum(
         (
             grad_n1_gain,

time: 1200 us -> 612 us (0.51)
  waiting for transfers between devices: 647 us -> 24.3 us
  Pallas kernels: 0 us -> 149 us
  blocking collectives: 202 us -> 78.9 us
  local copies, waits for them, and re-layouts: 14.6 us -> 29.2 us
    reduce_scatter x5 -> x0, waiting for transfers between devices: 549 us -> none  [the longest x1 143 us: on_device(): lax.psum_scatter(grad_down_w, 'dp', scatter_dimension=1, tiled=True)]
    pallas_call x0 -> x2, Pallas kernels: none -> 149 us  [the longest x1 78.8 us: rscat(): pl.pallas_call(functools.partial(rs_kernel, chunks), out_shape=jax.ShapeD...]
    all_gather x3 -> x0, blocking collectives: 125 us -> none  [the longest x1 43.4 us: fetch_weights(): lax.all_gather(shard_weights[1], 'dp', axis=0, tiled=True)]
    all_gather x2 -> x0, waiting for transfers between devices: 88.8 us -> none  [the longest x1 51.7 us: fetch_weights(): lax.all_gather(shard_weights[4], 'dp', axis=1, tiled=True)]
    reduce_scatter x2, waiting for transfers between devices: 0.02 us -> 13.7 us  [on_device(): lax.psum_scatter(keyval_grad.astype(jnp.bfloat16), 'tensor', scatter_dime...]
  transfers between devices with their start and end apart: 26 -> 19, of which waited for: 10 -> 5; matrix products, arithmetic and copies ran while one was open for 16% -> 33% of each run, Pallas kernels for 0% -> 13%
where the time goes in v1:
time: 612 us; the launch traced here: 606 us
  matrix products  213 us (35%)
  Pallas kernels  149 us (24%)
  blocking collectives  78.9 us (13%)
  other arithmetic  58.5 us (10%)
  starting transfers between devices  36.8 us (6%)
  local copies, waits for them, and re-layouts  29.2 us (5%)
  waiting for transfers between devices  24.3 us (4%)
  between operations  16.3 us (3%)
    pallas_call x1, Pallas kernels, rscat(): pl.pallas_call(functools.partial(rs_kernel, chunks), out_shape=jax.ShapeD...  78.8 us
    psum x1, blocking collectives, on_device(): lax.psum((grad_n1_gain, grad_n1_bias, grad_n2_gain, grad_n2_bias, grad_ro...  74.8 us
    pallas_call x1, Pallas kernels, gather(): pl.pallas_call(functools.partial(gather_kernel, chunks), out_shape=jax.Sh...  70.2 us
    ppermute x16, starting transfers between devices, shifted(): lax.ppermute(value, axis, [(source, source + steps) for source in range(i...  36.7 us
    dot_general x10, matrix products, attend_backward(): jnp.einsum('htd,kd->htk', grad_mixture, value_rows, preferred_element_typ...  32.6 us
    dot_general x10, matrix products, attend_backward(): jnp.einsum('htk,htd->kd', weights_low, grad_mixture, preferred_element_ty...  26.8 us
    dot_general x10, matrix products, attend_forward(): jnp.einsum('htk,kd->htd', weights_low, kv_block[:, HDIM:], preferred_elem...  25.8 us
    dot_general x10, matrix products, score_block(): jnp.einsum('htd,kd->htk', queries, key_rows, preferred_element_type=jnp.f...  25.5 us
  transfers between devices with their start and end apart: 19, of which 5 were waited for; matrix products, arithmetic and copies ran while one was open for 33% of the time, Pallas kernels for 13%

profile of v1, /device:TPU:0, one launch (start us, length us, event | category | flops | bytes accessed | tf_op | source)
XLA Modules:
  0.0 605.8 jit_solution(16459028206009787311)
XLA Ops:
  11.3 70.2 %gather_w.1 = bf16[4,2,2,48,3968]{4,3,2,1,0:T(8,128)(2,1)S(1)} custom-call(bf16[48,3968]{1,0:T(8,128)(2,1)S(1)} %pad.9.in_ref), custom_call_target="tpu_custom_call" | custom-call | tf_op jit(solution)/shard_map/gather_w/pallas_call | solution.py:122
  87.9 5.2 collective-permute-start.3
  93.0 3.6 collective-permute-start.2
  96.7 3.0 collective-permute-start.1
  99.7 4.6 collective-permute-start
  112.4 7.9 %multiply_convert_fusion.10 = (bf16[512,1536]{1,0:T(8,128)(2,1)S(1)}, f32[512,1536]{1,0:T(8,128)S(1)}, f32[512,1536]{1,0:T(8,128)S(1)}) fusion(f32[1536]{0:T(1024)S(1)} %copy-done.121, bf16[768,3968]{1,0:T(8,128)(2,1)S(1)} %bitcast.549, f32[512]{0:T(512)S(1)} %add_rsqrt_fusion, f32[512]{0:T(512)S(1)} %broadcast_multiply_fusion.10, f32[768]{0:T(1024)S(1)} %copy-done.122, ...), kind=kOutput, calls=%fused_computation.65 | convolution fusion | flops 1262223360 | bytes 11030528 | tf_op jit(solution)/shard_map/dot_general | solution.py:374
  120.3 8.1 %multiply_convert_fusion.11 = (bf16[512,1536]{1,0:T(8,128)(2,1)S(1)}, f32[512,1536]{1,0:T(8,128)S(1)}, f32[512,1536]{1,0:T(8,128)S(1)}) fusion(f32[1536]{0:T(1024)S(1)} %copy-done.121, bf16[768,3968]{1,0:T(8,128)(2,1)S(1)} %bitcast.550, f32[768]{0:T(1024)S(1)} %copy-done.122, f32[768]{0:T(1024)S(1)} %copy-done.97, f32[512]{0:T(512)S(1)} %add_rsqrt_fusion.1, ...), kind=kOutput, calls=%fused_computation.78 | convolution fusion | flops 1262223360 | bytes 11030528 | tf_op jit(solution)/shard_map/dot_general | solution.py:374
  131.2 3.0 convert_reduce_fusion
  134.2 2.3 fusion.112
  136.5 2.6 fusion.99
  139.1 3.0 convert_reduce_fusion.1
  142.1 2.3 fusion.109
  144.4 2.6 fusion.101
  147.7 2.2 fusion.171
  154.3 2.2 collective-permute-start.6
  157.6 3.0 collective-permute-start.5
  162.5 2.5 collective-permute-start.4
  165.0 4.6 select_reduce_fusion.17
  169.6 4.6 select_reduce_fusion.18
  174.2 2.3 select_reduce_fusion.9
  176.5 3.7 select_reduce_fusion.5
  180.2 6.2 %select_reduce_fusion.7 = (f32[6,512]{1,0:T(8,128)S(1)}, f32[6,512]{1,0:T(8,128)S(1)}) fusion(f32[6,512,512]{1,2,0:T(8,128)} %get-tuple-element.174, f32[6,512]{1,0:T(8,128)S(1)} %get-tuple-element.103, pred[512,512]{0,1:T(8,128)(4,1)S(1)} %copy-done.22, f32[6,512]{1,0:T(8,128)S(1)} %get-tuple-element.104, f32[6,512,512]{1,2,0:T(8,128)} %get-tuple-element.176, ...), kind=kLoop, calls=%fused_computation.27 | loop fusion | flops 12576768 | bytes 13156352 | tf_op jit(solution)/shard_map/reduce_sum | solution.py:258
  186.5 4.6 fusion.132
  191.1 4.6 fusion.134
  202.6 2.1 fusion.238
  204.7 2.1 fusion.235
  206.9 5.1 convolution_add_fusion.11
  211.9 4.0 multiply_reduce_fusion.1
  215.9 3.0 multiply_convert_fusion.9
  218.9 3.2 multiply_convert_fusion.5
  223.8 3.7 multiply_convert_fusion.6
  232.5 4.6 multiply_convert_fusion.8
  237.1 3.1 multiply_convert_fusion.7
  259.1 4.5 select_reduce_fusion.13
  264.9 2.7 select_reduce_fusion
  267.6 4.8 select_reduce_fusion.2
  272.4 4.6 fusion.140
  284.5 2.2 fusion.232
  286.7 2.2 fusion.225
  293.2 2.5 multiply_reduce_fusion
  295.7 3.1 multiply_convert_fusion.4
  298.8 3.6 multiply_convert_fusion
  304.2 2.7 multiply_convert_fusion.1
  308.0 2.9 multiply_convert_fusion.2
  312.0 2.7 multiply_convert_fusion.3
  347.3 2.9 convolution_bitcast_fusion.11
  352.4 3.2 collective-permute-done.14
  355.6 5.1 collective-permute-done.15
  362.7 4.4 reduce-scatter.3.cloned.1.call-done
  369.2 9.3 %reduce-scatter.5.cloned.1.call-done = bf16[512,64]{0,1:T(8,128)(2,1)} async-done(((bf16[512,128]{0,1:T(8,128)(2,1)}), bf16[512,64]{0,1:T(8,128)(2,1)}) %reduce-scatter.5.cloned.1.call-update) | async-done | bytes 65552 | tf_op jit(solution)/shard_map/reduce_scatter | solution.py:412
  381.9 2.9 add_convert_fusion.5
  386.1 2.2 add_convert_fusion.4
  391.7 5.3 fusion.185
  397.1 3.9 fusion.333
  402.8 2.2 copy.144
  409.1 2.3 fusion.116
  411.3 2.2 copy.143
  416.2 5.3 fusion.10
  423.1 2.6 copy-done.13
  427.1 3.1 pad.10
  430.3 78.8 %rscat_g.1 = f32[48,3968]{1,0:T(8,128)S(1)} custom-call(bf16[4,2,2,48,3968]{4,3,2,1,0:T(8,128)(2,1)S(1)} %bitcast.542), custom_call_target="tpu_custom_call" | custom-call | tf_op jit(solution)/shard_map/rscat_g/pallas_call | solution.py:185
  511.3 4.3 fusion.93
  517.9 74.8 %all-reduce.2 = (f32[768]{0:T(1024)}, f32[768]{0:T(1024)}, f32[768]{0:T(1024)}, f32[768]{0:T(1024)}, f32[384]{0:T(512)}, /*index=5*/f32[64]{0:T(128)}, f32[768]{0:T(1024)S(1)}, f32[1536]{0:T(1024)}) all-reduce(f32[768]{0:T(1024)S(1)} %add.619, f32[768]{0:T(1024)S(1)} %add.620, ...), channel_id=1, replica_groups=mesh['dp'=16,'tensor'=2] {'dp'}, use_global_device_ids=true, to_apply=%region_44.45 | all-reduce | flops 5824 | bytes 46592 | tf_op jit(solution)/shard_map/psum | solution.py:464
  592.8 3.0 fusion.177
  (474 shorter events, 143.2 us)
Async XLA Ops:
  7.2 359.9 %reduce-scatter.3.cloned.1.call-start = ((), (), s32[]{:S(2)}) async-start(), calls=%async_computation.2 | async-start | bytes 196608 | tf_op jit(solution)/shard_map/reduce_scatter | solution.py:412
  9.0 111.2 %copy-start.93 = (f32[512]{0:T(512)}, f32[512]{0:T(512)S(1)}, u32[]{:S(2)}) copy-start(f32[512]{0:T(512)S(1)} %broadcast_multiply_fusion.11) | copy-start | bytes 6148
  9.1 103.2 %copy-start.91 = (f32[512]{0:T(512)}, f32[512]{0:T(512)S(1)}, u32[]{:S(2)}) copy-start(f32[512]{0:T(512)S(1)} %broadcast_multiply_fusion.10) | copy-start | bytes 6148
  11.0 109.2 %copy-start.102 = (f32[512]{0:T(512)}, f32[512]{0:T(512)S(1)}, u32[]{:S(2)}) copy-start(f32[512]{0:T(512)S(1)} %add_rsqrt_fusion.1) | copy-start | bytes 6148
  11.1 101.2 %copy-start.99 = (f32[512]{0:T(512)}, f32[512]{0:T(512)S(1)}, u32[]{:S(2)}) copy-start(f32[512]{0:T(512)S(1)} %add_rsqrt_fusion) | copy-start | bytes 6148
  11.3 70.2 %copy-start.2 = (bf16[2,512,768]{2,1,0:T(8,128)(2,1)S(1)}, bf16[2,512,768]{2,1,0:T(8,128)(2,1)}, u32[]{:S(2)}) copy-start(bf16[2,512,768]{2,1,0:T(8,128)(2,1)} %param.17) | copy-start | bytes 4718596
  11.3 70.2 %copy-start.89 = (f32[768]{0:T(1024)S(1)}, f32[768]{0:T(1024)}, u32[]{:S(2)}) copy-start(f32[768]{0:T(1024)} %param.20) | copy-start | bytes 9220
  11.3 70.2 %copy-start.113 = (f32[768]{0:T(1024)S(1)}, f32[768]{0:T(1024)}, u32[]{:S(2)}) copy-start(f32[768]{0:T(1024)} %param.21) | copy-start | bytes 9220
  82.2 29.4 %copy-start.14 = (bf16[512,768]{1,0:T(8,128)(2,1)}, bf16[512,768]{1,0:T(8,128)(2,1)S(1)}, u32[]{:S(2)}) copy-start(bf16[512,768]{1,0:T(8,128)(2,1)S(1)} %get-tuple-element.116) | copy-start | bytes 2359300
  82.2 29.5 %copy-start.16 = (bf16[512,768]{1,0:T(8,128)(2,1)}, bf16[512,768]{1,0:T(8,128)(2,1)S(1)}, u32[]{:S(2)}) copy-start(bf16[512,768]{1,0:T(8,128)(2,1)S(1)} %get-tuple-element.115) | copy-start | bytes 2359300
  85.0 26.6 %copy-start.1 = (bf16[4,2,2,48,3968]{4,3,2,1,0:T(8,128)(2,1)S(1)}, bf16[4,2,2,48,3968]{4,3,2,1,0:T(8,128)(2,1)}, u32[]{:S(2)}) copy-start(bf16[4,2,2,48,3968]{4,3,2,1,0:T(8,128)(2,1)} %copy-done) | copy-start | bytes 18284548
  85.1 26.6 %copy-start.125 = (f32[384]{0:T(512)S(1)}, f32[384]{0:T(512)}, u32[]{:S(2)}) copy-start(f32[384]{0:T(512)} %param.25) | copy-start | bytes 4612
  85.1 27.1 %copy-start.75 = (f32[512,1,8]{0,2,1:T(8,128)}, f32[512,1,8]{0,2,1:T(8,128)S(1)}, u32[]{:S(2)}) copy-start(f32[512,1,8]{0,2,1:T(8,128)S(1)} %get-tuple-element.168) | copy-start | bytes 49156
  87.9 143.1 %copy-start.42 = (bf16[512,128]{0,1:T(8,128)(2,1)}, bf16[512,128]{0,1:T(8,128)(2,1)S(1)}, u32[]{:S(2)}) copy-start(bf16[512,128]{0,1:T(8,128)(2,1)S(1)} %all_gather.6) | copy-start | bytes 393220
  87.9 66.4 %collective-permute-start.3 = (bf16[512,128]{0,1:T(8,128)(2,1)S(1)}, bf16[512,128]{0,1:T(8,128)(2,1)S(1)}, u32[]{:S(2)}, u32[]{:S(2)}) collective-permute-start(bf16[512,128]{0,1:T(8,128)(2,1)S(1)} %all_gather.6), channel_id=1, source_target_pairs={{0,8},{2,10},{4,12},{6,14},{8,16},{10,18},{12,20},{14,22},{16,24},... | collective-permute-start | bytes 393224 | tf_op jit(solution)/shard_map/ppermute | solution.py:21
  93.0 64.5 %collective-permute-start.2 = (bf16[512,128]{0,1:T(8,128)(2,1)S(1)}, bf16[512,128]{0,1:T(8,128)(2,1)S(1)}, u32[]{:S(2)}, u32[]{:S(2)}) collective-permute-start(bf16[512,128]{0,1:T(8,128)(2,1)S(1)} %all_gather.6), channel_id=1, source_target_pairs={{0,6},{2,8},{4,10},{6,12},{8,14},{10,16},{12,18},{14,20},{16,22},{... | collective-permute-start | bytes 393224 | tf_op jit(solution)/shard_map/ppermute | solution.py:21
  96.7 65.8 %collective-permute-start.1 = (bf16[512,128]{0,1:T(8,128)(2,1)S(1)}, bf16[512,128]{0,1:T(8,128)(2,1)}, u32[]{:S(2)}, u32[]{:S(2)}) collective-permute-start(bf16[512,128]{0,1:T(8,128)(2,1)S(1)} %all_gather.6), channel_id=1, source_target_pairs={{0,4},{2,6},{4,8},{6,10},{8,12},{10,14},{12,16},{14,18},{16,20},{1... | collective-permute-start | bytes 393224 | tf_op jit(solution)/shard_map/ppermute | solution.py:21
  99.7 69.9 %collective-permute-start = (bf16[512,128]{0,1:T(8,128)(2,1)S(1)}, bf16[512,128]{0,1:T(8,128)(2,1)}, u32[]{:S(2)}, u32[]{:S(2)}) collective-permute-start(bf16[512,128]{0,1:T(8,128)(2,1)S(1)} %all_gather.6), channel_id=1, source_target_pairs={{0,2},{2,4},{4,6},{6,8},{8,10},{10,12},{12,14},{14,16},{16,18},{18... | collective-permute-start | bytes 393224 | tf_op jit(solution)/shard_map/ppermute | solution.py:21
  107.8 138.7 %collective-permute-start.7 = (bf16[512,128]{0,1:T(8,128)(2,1)}, bf16[512,128]{0,1:T(8,128)(2,1)}, u32[]{:S(2)}, u32[]{:S(2)}) collective-permute-start(bf16[512,128]{0,1:T(8,128)(2,1)} %all_gather.7), channel_id=1, source_target_pairs={{0,8},{2,10},{4,12},{6,14},{8,16},{10,18},{12,20},{14,22},{16,24},... | collective-permute-start | bytes 393224 | tf_op jit(solution)/shard_map/ppermute | solution.py:21
  120.2 16.3 %copy-start.19 = (bf16[512,1536]{1,0:T(8,128)(2,1)}, bf16[512,1536]{1,0:T(8,128)(2,1)S(1)}, u32[]{:S(2)}) copy-start(bf16[512,1536]{1,0:T(8,128)(2,1)S(1)} %get-tuple-element.111) | copy-start | bytes 4718596
  120.3 9.6 %copy-start.4 = (bf16[2,512,768]{2,1,0:T(8,128)(2,1)S(1)}, bf16[2,512,768]{2,1,0:T(8,128)(2,1)}, u32[]{:S(2)}) copy-start(bf16[2,512,768]{2,1,0:T(8,128)(2,1)} %param.19) | copy-start | bytes 4718596
  128.4 16.1 %copy-start.41 = (bf16[512,1536]{1,0:T(8,128)(2,1)}, bf16[512,1536]{1,0:T(8,128)(2,1)S(1)}, u32[]{:S(2)}) copy-start(bf16[512,1536]{1,0:T(8,128)(2,1)S(1)} %get-tuple-element.105) | copy-start | bytes 4718596
  149.9 10.6 %copy-start.27 = (pred[512,512]{0,1:T(8,128)(4,1)}, pred[512,512]{0,1:T(8,128)(4,1)S(1)}, u32[]{:S(2)}) copy-start(pred[512,512]{0,1:T(8,128)(4,1)S(1)} %get-tuple-element.164) | copy-start | bytes 786436
  149.9 15.1 %copy-start.21 = (pred[512,512]{0,1:T(8,128)(4,1)}, pred[512,512]{0,1:T(8,128)(4,1)S(1)}, u32[]{:S(2)}) copy-start(pred[512,512]{0,1:T(8,128)(4,1)S(1)} %get-tuple-element.162) | copy-start | bytes 786436
  149.9 19.6 %copy-start.23 = (pred[512,512]{0,1:T(8,128)(4,1)}, pred[512,512]{0,1:T(8,128)(4,1)S(1)}, u32[]{:S(2)}) copy-start(pred[512,512]{0,1:T(8,128)(4,1)S(1)} %get-tuple-element.158) | copy-start | bytes 786436
  154.3 95.8 %collective-permute-start.6 = (bf16[512,128]{0,1:T(8,128)(2,1)}, bf16[512,128]{0,1:T(8,128)(2,1)}, u32[]{:S(2)}, u32[]{:S(2)}) collective-permute-start(bf16[512,128]{0,1:T(8,128)(2,1)} %all_gather.7), channel_id=1, source_target_pairs={{0,6},{2,8},{4,10},{6,12},{8,14},{10,16},{12,18},{14,20},{16,22},{... | collective-permute-start | bytes 393224 | tf_op jit(solution)/shard_map/ppermute | solution.py:21
  157.6 98.9 %collective-permute-start.5 = (bf16[512,128]{0,1:T(8,128)(2,1)}, bf16[512,128]{0,1:T(8,128)(2,1)}, u32[]{:S(2)}, u32[]{:S(2)}) collective-permute-start(bf16[512,128]{0,1:T(8,128)(2,1)} %all_gather.7), channel_id=1, source_target_pairs={{0,4},{2,6},{4,8},{6,10},{8,12},{10,14},{12,16},{14,18},{16,20},{1... | collective-permute-start | bytes 393224 | tf_op jit(solution)/shard_map/ppermute | solution.py:21
  162.5 96.5 %collective-permute-start.4 = (bf16[512,128]{0,1:T(8,128)(2,1)}, bf16[512,128]{0,1:T(8,128)(2,1)}, u32[]{:S(2)}, u32[]{:S(2)}) collective-permute-start(bf16[512,128]{0,1:T(8,128)(2,1)} %all_gather.7), channel_id=1, source_target_pairs={{0,2},{2,4},{4,6},{6,8},{8,10},{10,12},{12,14},{14,16},{16,18},{18... | collective-permute-start | bytes 393224 | tf_op jit(solution)/shard_map/ppermute | solution.py:21
  204.7 7.2 %slice-start = ((s8[6291456]{0:T(1024)(128)(4,1)}), s8[4194304]{0:T(1024)(128)(4,1)S(1)}, s32[]{:S(2)}) async-start(s8[6291456]{0:T(1024)(128)(4,1)} %bitcast.563), calls=%async_computation.5 | async-start | bytes 8388608
  222.1 10.4 %slice-start.8 = ((s8[6291456]{0:T(1024)(128)(4,1)}), s8[4194304]{0:T(1024)(128)(4,1)S(1)}, s32[]{:S(2)}) async-start(s8[6291456]{0:T(1024)(128)(4,1)} %bitcast.571), calls=%async_computation.13 | async-start | bytes 8388608
  223.8 8.7 %slice-start.9 = ((s8[6291456]{0:T(1024)(128)(4,1)}), s8[2097152]{0:T(1024)(128)(4,1)S(1)}, s32[]{:S(2)}) async-start(s8[6291456]{0:T(1024)(128)(4,1)} %bitcast.571), calls=%async_computation.14 | async-start | bytes 4194304
  284.5 6.6 %slice-start.4 = ((s8[6291456]{0:T(1024)(128)(4,1)}), s8[4194304]{0:T(1024)(128)(4,1)S(1)}, s32[]{:S(2)}) async-start(s8[6291456]{0:T(1024)(128)(4,1)} %bitcast.567), calls=%async_computation.9 | async-start | bytes 8388608
  295.7 42.4 %copy-start.34 = (bf16[6,512,64]{1,2,0:T(8,128)(2,1)}, bf16[6,512,64]{1,2,0:T(8,128)(2,1)S(1)}, u32[]{:S(2)}) copy-start(bf16[6,512,64]{1,2,0:T(8,128)(2,1)S(1)} %get-tuple-element.122) | copy-start | bytes 1179652
  298.8 17.1 %copy-start.5 = (bf16[6,512,512]{1,2,0:T(8,128)(2,1)}, bf16[6,512,512]{1,2,0:T(8,128)(2,1)S(1)}, u32[]{:S(2)}) copy-start(bf16[6,512,512]{1,2,0:T(8,128)(2,1)S(1)} %multiply_convert_fusion.4) | copy-start | bytes 9437188
  322.0 7.2 %copy-start.61 = (f32[512,6,8]{0,2,1:T(8,128)S(1)}, f32[512,6,8]{0,2,1:T(8,128)}, u32[]{:S(2)}) copy-start(f32[512,6,8]{0,2,1:T(8,128)} %get-tuple-element.124) | copy-start | bytes 294916
  322.0 7.2 %copy-start.80 = (f32[512,16]{0,1:T(8,128)S(1)}, f32[512,16]{0,1:T(8,128)}, u32[]{:S(2)}) copy-start(f32[512,16]{0,1:T(8,128)} %get-tuple-element.146) | copy-start | bytes 98308
  322.0 8.2 %copy-start.50 = (bf16[512,6,48]{0,2,1:T(8,128)(2,1)S(1)}, bf16[512,6,48]{0,2,1:T(8,128)(2,1)}, u32[]{:S(2)}) copy-start(bf16[512,6,48]{0,2,1:T(8,128)(2,1)} %slice.362) | copy-start | bytes 884740
  323.7 9.0 %copy-start.88 = (bf16[512,64]{0,1:T(8,128)(2,1)S(1)}, bf16[512,64]{0,1:T(8,128)(2,1)}, u32[]{:S(2)}) copy-start(bf16[512,64]{0,1:T(8,128)(2,1)} %fusion.140) | copy-start | bytes 196612
  323.8 11.1 %copy-start.79 = (f32[512,16]{0,1:T(8,128)S(1)}, f32[512,16]{0,1:T(8,128)}, u32[]{:S(2)}) copy-start(f32[512,16]{0,1:T(8,128)} %get-tuple-element.143) | copy-start | bytes 98308
  323.9 18.6 %collective-permute-start.8 = (bf16[512,128]{0,1:T(8,128)(2,1)S(1)}, bf16[512,128]{0,1:T(8,128)(2,1)S(1)}, u32[]{:S(2)}, u32[]{:S(2)}) collective-permute-start(bf16[512,128]{0,1:T(8,128)(2,1)S(1)} %pad_maximum_fusion.3), channel_id=1, source_target_pairs={{2,0},{4,2},{6,4},{8,6},{10,8},{12,10},{14,12},{16,14},{18,16},{20... | collective-permute-start | bytes 393224 | tf_op jit(solution)/shard_map/ppermute | solution.py:21
  325.2 18.6 %collective-permute-start.9 = (bf16[512,128]{0,1:T(8,128)(2,1)S(1)}, bf16[512,128]{0,1:T(8,128)(2,1)S(1)}, u32[]{:S(2)}, u32[]{:S(2)}) collective-permute-start(bf16[512,128]{0,1:T(8,128)(2,1)S(1)} %pad_maximum_fusion.4), channel_id=1, source_target_pairs={{4,0},{6,2},{8,4},{10,6},{12,8},{14,10},{16,12},{18,14},{20,16},{2... | collective-permute-start | bytes 393224 | tf_op jit(solution)/shard_map/ppermute | solution.py:21
  326.5 18.6 %collective-permute-start.10 = (bf16[512,128]{0,1:T(8,128)(2,1)S(1)}, bf16[512,128]{0,1:T(8,128)(2,1)S(1)}, u32[]{:S(2)}, u32[]{:S(2)}) collective-permute-start(bf16[512,128]{0,1:T(8,128)(2,1)S(1)} %pad_maximum_fusion.5), channel_id=1, source_target_pairs={{6,0},{8,2},{10,4},{12,6},{14,8},{16,10},{18,12},{20,14},{22,16},{... | collective-permute-start | bytes 393224 | tf_op jit(solution)/shard_map/ppermute | solution.py:21
  327.9 18.5 %collective-permute-start.11 = (bf16[512,128]{0,1:T(8,128)(2,1)S(1)}, bf16[512,128]{0,1:T(8,128)(2,1)S(1)}, u32[]{:S(2)}, u32[]{:S(2)}) collective-permute-start(bf16[512,128]{0,1:T(8,128)(2,1)S(1)} %pad_maximum_fusion.6), channel_id=1, source_target_pairs={{8,0},{10,2},{12,4},{14,6},{16,8},{18,10},{20,12},{22,14},{24,16},... | collective-permute-start | bytes 393224 | tf_op jit(solution)/shard_map/ppermute | solution.py:21
  330.9 7.2 %copy-start.44 = (f32[512,768]{1,0:T(8,128)S(1)}, f32[512,768]{1,0:T(8,128)}, u32[]{:S(2)}) copy-start(f32[512,768]{1,0:T(8,128)} %fusion.99) | copy-start | bytes 4718596
  333.4 16.9 %collective-permute-start.12 = (bf16[512,128]{0,1:T(8,128)(2,1)}, bf16[512,128]{0,1:T(8,128)(2,1)}, u32[]{:S(2)}, u32[]{:S(2)}) collective-permute-start(bf16[512,128]{0,1:T(8,128)(2,1)} %pad_maximum_fusion.7), channel_id=1, source_target_pairs={{2,0},{4,2},{6,4},{8,6},{10,8},{12,10},{14,12},{16,14},{18,16},{20... | collective-permute-start | bytes 393224 | tf_op jit(solution)/shard_map/ppermute | solution.py:21
  338.2 8.3 %copy-start.55 = (f32[512,64]{0,1:T(8,128)S(1)}, f32[512,64]{0,1:T(8,128)}, u32[]{:S(2)}) copy-start(f32[512,64]{0,1:T(8,128)} %convolution_bitcast_fusion.21) | copy-start | bytes 393220
  338.2 8.3 %copy-start.78 = (f32[512,64]{0,1:T(8,128)S(1)}, f32[512,64]{0,1:T(8,128)}, u32[]{:S(2)}) copy-start(f32[512,64]{0,1:T(8,128)} %convolution_bitcast_fusion.20) | copy-start | bytes 393220
  342.5 9.9 %collective-permute-start.13 = (bf16[512,128]{0,1:T(8,128)(2,1)}, bf16[512,128]{0,1:T(8,128)(2,1)}, u32[]{:S(2)}, u32[]{:S(2)}) collective-permute-start(bf16[512,128]{0,1:T(8,128)(2,1)} %pad_maximum_fusion.8), channel_id=1, source_target_pairs={{4,0},{6,2},{8,4},{10,6},{12,8},{14,10},{16,12},{18,14},{20,16},{2... | collective-permute-start | bytes 393224 | tf_op jit(solution)/shard_map/ppermute | solution.py:21
  343.8 11.8 %collective-permute-start.14 = (bf16[512,128]{0,1:T(8,128)(2,1)}, bf16[512,128]{0,1:T(8,128)(2,1)}, u32[]{:S(2)}, u32[]{:S(2)}) collective-permute-start(bf16[512,128]{0,1:T(8,128)(2,1)} %pad_maximum_fusion.9), channel_id=1, source_target_pairs={{6,0},{8,2},{10,4},{12,6},{14,8},{16,10},{18,12},{20,14},{22,16},{... | collective-permute-start | bytes 393224 | tf_op jit(solution)/shard_map/ppermute | solution.py:21
  345.1 15.6 %collective-permute-start.15 = (bf16[512,128]{0,1:T(8,128)(2,1)}, bf16[512,128]{0,1:T(8,128)(2,1)}, u32[]{:S(2)}, u32[]{:S(2)}) collective-permute-start(bf16[512,128]{0,1:T(8,128)(2,1)} %pad_maximum_fusion.10), channel_id=1, source_target_pairs={{8,0},{10,2},{12,4},{14,6},{16,8},{18,10},{20,12},{22,14},{24,16},... | collective-permute-start | bytes 393224 | tf_op jit(solution)/shard_map/ppermute | solution.py:21
  347.2 31.3 %reduce-scatter.5.cloned.1.call-start = ((), (), s32[]{:S(2)}) async-start(), calls=%async_computation.3 | async-start | bytes 196608 | tf_op jit(solution)/shard_map/reduce_scatter | solution.py:412
  350.2 34.6 %copy-start.76 = (f32[512,1,8]{0,2,1:T(8,128)S(1)}, f32[512,1,8]{0,2,1:T(8,128)}, u32[]{:S(2)}) copy-start(f32[512,1,8]{0,2,1:T(8,128)} %copy-done.75) | copy-start | bytes 49156
  350.2 35.9 %copy-start.18 = (f32[512,768]{1,0:T(8,128)S(1)}, f32[512,768]{1,0:T(8,128)}, u32[]{:S(2)}) copy-start(f32[512,768]{1,0:T(8,128)} %fusion.207) | copy-start | bytes 4718596
  362.6 148.7 %all-reduce.6.cloned.1.call-start = ((), (), s32[]{:S(2)}) async-start(), calls=%async_computation.4 | async-start | bytes 9437184 | tf_op jit(solution)/shard_map/psum | solution.py:379
  400.9 6.6 %copy-start.90 = (f32[768]{0:T(1024)S(1)}, f32[768]{0:T(1024)}, u32[]{:S(2)}) copy-start(f32[768]{0:T(1024)} %param.20) | copy-start | bytes 9220
  401.4 7.6 %copy-start.92 = (f32[512]{0:T(512)S(1)}, f32[512]{0:T(512)}, u32[]{:S(2)}) copy-start(f32[512]{0:T(512)} %copy-done.91) | copy-start | bytes 6148
  409.0 7.2 %copy-start.100 = (f32[512]{0:T(512)S(1)}, f32[512]{0:T(512)}, u32[]{:S(2)}) copy-start(f32[512]{0:T(512)} %copy-done.99) | copy-start | bytes 6148
  409.1 7.2 %copy-start.124 = (f32[768]{0:T(1024)S(1)}, f32[768]{0:T(1024)}, u32[]{:S(2)}) copy-start(f32[768]{0:T(1024)} %param.23) | copy-start | bytes 9220
  414.7 6.8 %slice-start.10 = ((s8[4718592]{0:T(1024)(128)(4,1)}), s8[4194304]{0:T(1024)(128)(4,1)S(1)}, s32[]{:S(2)}) async-start(s8[4718592]{0:T(1024)(128)(4,1)} %bitcast.573), calls=%async_computation.15 | async-start | bytes 8388608
  430.3 79.5 %copy-start.119 = (f32[64]{0:T(128)S(1)}, f32[64]{0:T(128)}, u32[]{:S(2)}) copy-start(f32[64]{0:T(128)} %get-tuple-element.95) | copy-start | bytes 772
  430.3 79.5 %copy-start.120 = (f32[64]{0:T(128)S(1)}, f32[64]{0:T(128)}, u32[]{:S(2)}) copy-start(f32[64]{0:T(128)} %get-tuple-element.93) | copy-start | bytes 772
  430.3 81.0 %copy-start.104 = (f32[512]{0:T(512)S(1)}, f32[512]{0:T(512)}, u32[]{:S(2)}) copy-start(f32[512]{0:T(512)} %copy-done.102) | copy-start | bytes 6148
  515.6 77.1 %copy-start.114 = (f32[768]{0:T(1024)S(1)}, f32[768]{0:T(1024)}, u32[]{:S(2)}) copy-start(f32[768]{0:T(1024)} %param.33) | copy-start | bytes 9220
  515.7 77.1 %copy-start.115 = (f32[768]{0:T(1024)S(1)}, f32[768]{0:T(1024)}, u32[]{:S(2)}) copy-start(f32[768]{0:T(1024)} %param.29) | copy-start | bytes 9220
  (96 other events, 336.1 us)
Sparse Core Ops, SparseCore 0:
  347.4 19.7 reduce-scatter.2
  369.9 8.6 reduce-scatter.4
  388.5 31.0 all-reduce.5

commit v2 on v0

--- a/solution.py
+++ b/solution.py
@@ -1,14 +1,19 @@
+import functools
 import jax
 import jax.numpy as jnp
 from jax import lax
+from jax.experimental import pallas as pl
+from jax.experimental.pallas import tpu as pltpu
 from jax.sharding import PartitionSpec as P
 
 HDIM = 64
 ROT = 16
 REACH = 4
-
-
 epsilon = 1e-05
+MESH = pl.DeviceIdType.MESH
+LOW = -1e30
+F32 = jnp.float32
+BF16 = jnp.bfloat16
 
 
 def shifted(value, axis, steps):
@@ -125,7 +130,7 @@
     return (grad_queries, key_terms)
 
 
-def on_device(
+def plain_layer(
     hidden_in,
     positions,
     out_grad,
@@ -324,6 +329,728 @@
     )
 
 
+def nn(a, b):
+    return jnp.dot(a, b, preferred_element_type=F32)
+
+
+def nt(a, b):
+    return lax.dot_general(a, b, (((1,), (1,)), ((), ())), preferred_element_type=F32)
+
+
+def chunk_list(q_cols, kv_cols, ff_cols, pieces):
+    sizes = [q_cols, kv_cols, q_cols] + [ff_cols // pieces] * (2 * pieces)
+    at = 0
+    out = []
+    for size in sizes:
+        out.append((at, size))
+        at += size
+    return out
+
+
+def attend_tiles(n, half):
+    own = REACH * n
+    out = [(own + a, half, a, n - a, True) for a in range(0, n, half)]
+    out += [(own - j * n, n, 0, n, False) for j in range(1, REACH)]
+    out += [(a, half, 0, min(n, a + half), False) for a in range(0, n, half)]
+    return out
+
+
+def spin(rows, cos, sine):
+    h = ROT // 2
+    a, b, rest = rows[..., :h, :], rows[..., h:ROT, :], rows[..., ROT:, :]
+    return jnp.concatenate([a * cos - b * sine, b * cos + a * sine, rest], axis=-2)
+
+
+def fused_kernel(
+    chunks, pieces,
+    x, dy, shard, kvw, kvb, g1, b1, g2, b2, bq, bu, bo, cos, sine, start,
+    layer_out, keyval_out, input_grad, grads_out, vec_out,
+    W, G, kvx, kvbx, n1T, n2, n2T, dyT, wqT, qT, doT, oT, o_nat, lse, dvec, kvwin, kvTwin,
+    m_s, l_s, acc, gbuf, dubuf, dqT, dkv, hs, hr, kvs, kvr, yp, yr, d2p, d2r,
+    r1, r2, r3, vec, vrx, vb, vry, vz, dql, dkl,
+    gzs, gzr, g2s, g2r, g3s, g3r, a1s, a1r, a2s, a2r, azs, azr,
+    hfs, hfr, hbs, hbr, xs, xr, vs, vr,
+):
+    T, D = x.shape
+    M, W_rows, KV = kvwin.shape
+    n = T // M
+    heads = qT.shape[0] // M
+    hq = heads * HDIM
+    own = REACH * n
+    piece = gbuf.shape[2]
+    scale = HDIM ** (-0.5)
+    me = lax.axis_index("dp")
+    core = lax.axis_index("tensor")
+    count = lax.axis_size("dp")
+    z, y, xx = me // 4, (me // 2) % 2, me % 2
+    shard_rows = shard.shape[0]
+    n_chunks = len(chunks)
+
+    def at(zz, yy, xo):
+        return {"dp": zz * 4 + yy * 2 + xo}
+
+    z_ids = [at((z + d) % 4, y, xx) for d in (1, 2, 3)]
+    y_id, x_id = at(z, 1 - y, xx), at(z, y, 1 - xx)
+    t_id = {"tensor": 1 - core}
+
+    def send(src, dst, ss, rs, to):
+        return pltpu.make_async_remote_copy(
+            src_ref=src, dst_ref=dst, send_sem=ss, recv_sem=rs, device_id=to, device_id_type=MESH
+        )
+
+    bar = pltpu.get_barrier_semaphore()
+    peers = z_ids + [y_id, x_id, t_id]
+    peers += [{"dp": (me + s) % count} for s in range(1, REACH + 1)]
+    peers += [{"dp": (me + count - s) % count} for s in range(1, REACH + 1)]
+    for p in peers:
+        pl.semaphore_signal(bar, inc=1, device_id=p, device_id_type=MESH)
+    pl.semaphore_wait(bar, len(peers))
+
+    def cols(k):
+        return pl.ds(chunks[k][0], chunks[k][1])
+
+    def gather1(k):
+        return [
+            send(W.at[z, y, xx, :, cols(k)], W.at[z, y, xx, :, cols(k)], gzs.at[k, j], gzr.at[k, j], z_ids[j])
+            for j in range(3)
+        ]
+
+    def gather2(k):
+        r = W.at[:, y, xx, :, cols(k)]
+        return send(r, r, g2s.at[k], g2r.at[k], x_id if k % 2 == 0 else y_id)
+
+    def gather3(k):
+        r = W.at[:, y, :, :, cols(k)] if k % 2 == 0 else W.at[:, :, xx, :, cols(k)]
+        return send(r, r, g3s.at[k], g3r.at[k], y_id if k % 2 == 0 else x_id)
+
+    def start1(k):
+        for c in gather1(k):
+            c.start()
+
+    def step2(k):
+        for c in gather1(k):
+            c.wait_recv()
+        gather2(k).start()
+
+    def step3(k):
+        gather2(k).wait_recv()
+        gather3(k).start()
+
+    def arrived(k):
+        gather3(k).wait_recv()
+
+    def weight(k):
+        c0, cn = chunks[k]
+        return W[:, :, :, :, c0 : c0 + cn].reshape(D, cn)
+
+    def red1(k):
+        if k % 2 == 0:
+            return send(G.at[:, :, 1 - xx, :, cols(k)], r1.at[:, :, :, cols(k)], a1s.at[k], a1r.at[k], x_id)
+        return send(G.at[:, 1 - y, :, :, cols(k)], r1.at[:, :, :, cols(k)], a1s.at[k], a1r.at[k], y_id)
+
+    def red2(k):
+        o = y if k % 2 == 0 else xx
+        return send(r1.at[:, 1 - o, :, cols(k)], r2.at[:, :, cols(k)], a2s.at[k], a2r.at[k], y_id if k % 2 == 0 else x_id)
+
+    def red3(k):
+        return [
+            send(r2.at[(z + j + 1) % 4, :, cols(k)], r3.at[j, :, cols(k)], azs.at[k, j], azr.at[k, j], z_ids[j])
+            for j in range(3)
+        ]
+
+    def step_a(k):
+        red1(k).start()
+
+    def step_b(k):
+        red1(k).wait_recv()
+
+        def add(i, _):
+            zz, yy = i // 2, i % 2
+            mine = G[zz, yy, xx, :, cols(k)] if k % 2 == 0 else G[zz, y, yy, :, cols(k)]
+            r1[zz, yy, :, cols(k)] = r1[zz, yy, :, cols(k)] + mine
+            return 0
+
+        lax.fori_loop(0, 8, add, 0)
+        red2(k).start()
+
+    def step_c(k):
+        red2(k).wait_recv()
+        o = y if k % 2 == 0 else xx
+
+        def add(i, _):
+            r2[i, :, cols(k)] = r2[i, :, cols(k)] + r1[i, o, :, cols(k)]
+            return 0
+
+        lax.fori_loop(0, 4, add, 0)
+        for c in red3(k):
+            c.start()
+
+    def step_e(k):
+        for c in red3(k):
+            c.wait_recv()
+        total = r2[z, :, cols(k)].astype(F32)
+        for j in range(3):
+            total = total + r3[j, :, cols(k)].astype(F32)
+        grads_out[:, cols(k)] = total
+
+    kv_copy = send(kvw, kvx, xs.at[0], xr.at[0], t_id)
+    kvb_copy = send(kvb, kvbx, xs.at[1], xr.at[1], t_id)
+    kv_copy.start()
+    kvb_copy.start()
+    W[z, y, xx] = shard[...]
+    start1(0)
+    kv_copy.wait_recv()
+    kv0 = chunks[1][0]
+    W[z, y, xx, :, kv0 : kv0 + KV] = kvw[...] + kvx[...]
+    start1(1)
+    start1(2)
+
+    R = 256
+    vec[...] = jnp.zeros_like(vec)
+
+    def xhat_of(rows):
+        v = x[rows, :].astype(F32)
+        c = v - jnp.mean(v, axis=-1, keepdims=True)
+        rstd = lax.rsqrt(jnp.mean(c * c, axis=-1, keepdims=True) + epsilon)
+        return v, c * rstd, rstd
+
+    def norm_tile(i, _):
+        rows = pl.ds(pl.multiple_of(i * R, R), R)
+        _, xh, _ = xhat_of(rows)
+        n1v = (xh * g1[...] + b1[...]).astype(BF16)
+        n2v = (xh * g2[...] + b2[...]).astype(BF16)
+        n2[rows, :] = n2v
+        n1T[:, rows] = n1v.T
+        n2T[:, rows] = n2v.T
+        d = dy[rows, :]
+        dyT[:, rows] = d.T
+        vec[4:5, :] += jnp.sum(d.astype(F32), axis=0, keepdims=True)
+        return 0
+
+    lax.fori_loop(0, T // R // 2, norm_tile, 0)
+    step2(0)
+    step2(1)
+    start1(3)
+    lax.fori_loop(T // R // 2, T // R, norm_tile, 0)
+    step3(0)
+    step3(1)
+    step2(2)
+    start1(4)
+    kvb_copy.wait_recv()
+    bkv = jnp.transpose(kvb[...] + kvbx[...])[:, 0:1]
+    arrived(0)
+    wqT[...] = weight(0).T
+    arrived(1)
+    wkvT = weight(1).T
+    for m in range(M):
+        ms = slice(m * n, (m + 1) * n)
+        lin = nn(wkvT, n1T[:, ms]) + bkv
+        low = spin(lin, cos[:, ms], sine[:, ms]).astype(BF16)
+        kvTwin[m, :, own : own + n] = low
+        natural = low.T
+        kvwin[m, own : own + n, :] = natural
+        keyval_out[m] = natural
+
+    def halo(s):
+        return send(
+            kvwin.at[:, pl.ds(own, n), :], kvwin.at[:, pl.ds((REACH - s) * n, n), :],
+            hfs.at[s - 1], hfr.at[s - 1], {"dp": (me + s) % count},
+        )
+
+    for s in range(1, REACH + 1):
+        @pl.when(me + s < count)
+        def _(s=s):
+            halo(s).start()
+
+    step3(2)
+    step2(3)
+    start1(5)
+    for m in range(M):
+        ms = slice(m * n, (m + 1) * n)
+        lin = nn(wqT[...], n1T[:, ms]) + bq[...]
+        turned = spin(lin.reshape(heads, HDIM, n), cos[:, ms], sine[:, ms]) * scale
+        qT[m * heads : (m + 1) * heads] = turned.astype(BF16)
+    arrived(2)
+    step3(3)
+    step2(4)
+    start1(6)
+    wo = weight(2).T
+    for m in range(M):
+        ms = slice(m * n, (m + 1) * n)
+        doT[m * heads : (m + 1) * heads] = nn(wo, dyT[:, ms]).astype(BF16).reshape(heads, HDIM, n)
+
+    for s in range(1, REACH + 1):
+        blk = slice((REACH - s) * n, (REACH - s + 1) * n)
+
+        @pl.when(me >= s)
+        def _(s=s):
+            halo(s).wait_recv()
+
+        @pl.when(me < s)
+        def _(blk=blk):
+            kvwin[:, blk, :] = jnp.zeros((M, n, KV), BF16)
+
+        for m in range(M):
+            kvTwin[m, :, blk] = kvwin[m, blk, :].T
+
+    tiles = attend_tiles(n, n // 2)
+
+    def visible(w0, kn, q0, qn, first, causal):
+        key = lax.broadcasted_iota(jnp.int32, (kn, 1), 0) + w0
+        seen = key >= first
+        if causal:
+            query = lax.broadcasted_iota(jnp.int32, (1, qn), 1) + (q0 + own)
+            seen = seen & (key <= query)
+        return seen
+
+    def forward(i, _):
+        m = i // heads
+        q = jnp.concatenate([qT[i], jnp.zeros((KV - HDIM, n), BF16)], axis=0)
+        first = start[m]
+        m_s[...] = jnp.full_like(m_s, LOW)
+        l_s[...] = jnp.zeros_like(l_s)
+        acc[...] = jnp.zeros_like(acc)
+        for w0, kn, q0, qn, causal in tiles:
+            qs = slice(q0, q0 + qn)
+            sc = nn(kvwin[m, w0 : w0 + kn, :], q[:, qs])
+            sc = jnp.where(visible(w0, kn, q0, qn, first[:, qs], causal), sc, LOW)
+            before = m_s[:, qs]
+            top = jnp.maximum(before, jnp.max(sc, axis=0, keepdims=True))
+            p = jnp.exp(sc - top)
+            shrink = jnp.exp(before - top)
+            l_s[:, qs] = l_s[:, qs] * shrink + jnp.sum(p, axis=0, keepdims=True)
+            m_s[:, qs] = top
+            acc[:, qs] = acc[:, qs] * shrink + nn(kvTwin[m, HDIM:KV, w0 : w0 + kn], p.astype(BF16))
+        o = acc[...] / l_s[...]
+        oT[i] = o.astype(BF16)
+        lse[i] = m_s[...] + jnp.log(l_s[...])
+        dvec[i] = jnp.sum(doT[i].astype(F32) * o, axis=0, keepdims=True)
+        gather_steps(i)
+        return 0
+
+    plan = [
+        (lambda: (step3(4), step2(5), start1(7))),
+        (lambda: None),
+        (lambda: (step3(5), step2(6), start1(8))),
+        (lambda: None),
+        (lambda: (step3(6), step2(7))),
+        (lambda: None),
+        (lambda: (step3(7), step2(8))),
+        (lambda: None),
+        (lambda: step3(8)),
+    ]
+
+    def gather_steps(i):
+        for j, act in enumerate(plan):
+            if j % 2 == 0:
+                pl.when(i == j + 1)(lambda act=act: (act(), None)[1])
+
+    lax.fori_loop(0, M * heads, forward, 0)
+
+    for m in range(M):
+        o_nat[m * n : (m + 1) * n, :] = oT[m * heads : (m + 1) * heads].reshape(hq, n).T
+
+    def put_grad(k, leftT, right):
+        c0, cn = chunks[k]
+
+        def half(i, _):
+            rows = pl.ds(pl.multiple_of(i * (D // 2), 128), D // 2)
+            part = nn(leftT[rows, :], right[...]).astype(BF16)
+            G[pl.ds(i * 2, 2), :, :, :, c0 : c0 + cn] = part.reshape(2, 2, 2, shard_rows, cn)
+            return 0
+
+        lax.fori_loop(0, 2, half, 0)
+        step_a(k)
+
+    put_grad(2, dyT, o_nat)
+
+    for c in range(pieces):
+        ku, kd = 3 + 2 * c, 4 + 2 * c
+        arrived(ku)
+        arrived(kd)
+        (u0, _), (d0, _) = chunks[ku], chunks[kd]
+
+        def rows_tile(i, _, c=c, u0=u0, d0=d0):
+            rows = pl.ds(pl.multiple_of(i * R, R), R)
+            u = nn(n2[rows, :], W[:, :, :, :, u0 : u0 + piece].reshape(D, piece)) + bu[c]
+            phi = 0.5 * (1.0 + lax.erf(u * 0.7071067811865476))
+            slope = phi + u * (jnp.exp(-0.5 * u * u) * 0.3989422804014327)
+            gbuf[c, rows, :] = (u * phi).astype(BF16)
+            dg = nn(dy[rows, :], W[:, :, :, :, d0 : d0 + piece].reshape(D, piece))
+            du = (slope * dg).astype(BF16)
+            dubuf[c, rows, :] = du
+            return 0
+
+        lax.fori_loop(0, T // R, rows_tile, 0)
+        put_grad(ku, n2T, dubuf.at[c])
+        put_grad(kd, dyT, gbuf.at[c])
+
+    def branch_tile(i, _):
+        rows = pl.ds(pl.multiple_of(i * R, R), R)
+        total = nt(o_nat[rows, :], weight(2))
+        back = jnp.zeros((R, D), F32)
+        for c in range(pieces):
+            total = total + nt(gbuf[c, rows, :], weight(4 + 2 * c))
+            back = back + nt(dubuf[c, rows, :], weight(3 + 2 * c))
+        yp[rows, :] = total.astype(BF16)
+        d2p[rows, :] = back.astype(BF16)
+        return 0
+
+    step_b(2)
+    lax.fori_loop(0, T // R, branch_tile, 0)
+    y_copy = send(yp, yr, xs.at[2], xr.at[2], t_id)
+    d2_copy = send(d2p, d2r, xs.at[3], xr.at[3], t_id)
+    y_copy.start()
+    d2_copy.start()
+    for c in range(pieces):
+        part = jnp.sum(dubuf[c].astype(F32), axis=0, keepdims=True)
+        done = 0
+        while done < piece:
+            flat = c * piece + done
+            row, col = flat // D, flat % D
+            width = min(piece - done, D - col)
+            vec[6 + row : 7 + row, col : col + width] = part[:, done : done + width]
+            done += width
+
+    dkv[...] = jnp.zeros_like(dkv)
+
+    def backward(i, _):
+        m = i // heads
+        zero = jnp.zeros((HDIM, n), BF16)
+        q = jnp.concatenate([qT[i], zero], axis=0)
+        do = jnp.concatenate([zero, doT[i]], axis=0)
+        qdo = jnp.concatenate([qT[i], doT[i]], axis=0).T
+        first, ls, dots = start[m], lse[i], dvec[i]
+        dqT[i] = jnp.zeros((HDIM, n), F32)
+        for w0, kn, q0, qn, causal in tiles:
+            qs = slice(q0, q0 + qn)
+            rows = kvwin[m, w0 : w0 + kn, :]
+            sc = nn(rows, q[:, qs])
+            sc = jnp.where(visible(w0, kn, q0, qn, first[:, qs], causal), sc, LOW)
+            p = jnp.exp(sc - ls[:, qs])
+            dp = nn(rows, do[:, qs])
+            ds = (p * (dp - dots[:, qs])).astype(BF16)
+            for_k = nn(ds, qdo[qs])
+            for_v = nn(p.astype(BF16), qdo[qs])
+            lane = lax.broadcasted_iota(jnp.int32, for_k.shape, 1)
+            dkv[m, w0 : w0 + kn, :] += jnp.where(lane < HDIM, for_k, for_v)
+            dqT[i, :, qs] += nn(kvTwin[m, 0:HDIM, w0 : w0 + kn], ds)
+        reduce_steps(i)
+        return 0
+
+    def back_copy(s, m):
+        return send(
+            hs.at[s - 1, m], hr.at[s - 1, m], hbs.at[s - 1, m], hbr.at[s - 1, m],
+            {"dp": (me + count - s) % count},
+        )
+
+    def return_halo(m):
+        for s in range(1, REACH + 1):
+            hs[s - 1, m] = dkv[m, (REACH - s) * n : (REACH - s + 1) * n, :].astype(BF16)
+
+            @pl.when(me >= s)
+            def _(s=s):
+                back_copy(s, m).start()
+
+    red_plan = {
+        0: lambda: step_b(3),
+        1: lambda: (step_c(2), step_b(4)),
+        3: lambda: (step_c(3), step_c(4), step_b(5)),
+        5: lambda: (step_e(2), step_e(3), step_b(6), step_c(5), return_halo(0)),
+        7: lambda: (step_e(4), step_b(7), step_c(6)),
+        9: lambda: (step_e(5), step_b(8), step_c(7)),
+        11: lambda: (step_e(6), step_c(8)),
+    }
+
+    def reduce_steps(i):
+        for j, act in red_plan.items():
+            pl.when(i == j)(lambda act=act: (act(), None)[1])
+
+    lax.fori_loop(0, M * heads, backward, 0)
+    for m in range(1, M):
+        return_halo(m)
+
+    for m in range(M):
+        ms = slice(m * n, (m + 1) * n)
+        rows = dqT[m * heads : (m + 1) * heads] * scale
+        low = spin(rows, cos[:, ms], -sine[:, ms]).astype(BF16)
+        dql[ms, :] = low.reshape(hq, n).T
+    put_grad(0, n1T, dql)
+    vec[5:6, 0:hq] = jnp.sum(dql[...].astype(F32), axis=0, keepdims=True)
+
+    y_copy.wait_recv()
+
+    def out_tile(i, _):
+        rows = pl.ds(pl.multiple_of(i * R, R), R)
+        both = (yp[rows, :].astype(F32) + yr[rows, :].astype(F32)) + bo[...]
+        layer_out[rows, :] = (x[rows, :].astype(F32) + both).astype(BF16)
+        return 0
+
+    lax.fori_loop(0, T // R, out_tile, 0)
+
+    y_copy.wait_send()
+    d1p, d1r = yp, n2
+
+    for m in range(M):
+        for s in range(1, REACH + 1):
+            @pl.when(me + s < count)
+            def _(s=s, m=m):
+                back_copy(s, m).wait_recv()
+                dkv[m, own : own + n, :] += hr[s - 1, m].astype(F32)
+        kvs[m] = dkv[m, own : own + n, :].astype(BF16)
+    kv_grad = send(kvs, kvr, xs.at[4], xr.at[4], t_id)
+    kv_grad.start()
+    step_b(0)
+    kv_grad.wait_recv()
+    half_row = lax.broadcasted_iota(jnp.int32, (KV, 1), 0) // HDIM
+    for m in range(M):
+        ms = slice(m * n, (m + 1) * n)
+        both = (dkv[m, own : own + n, :] + kvr[m].astype(F32)).T
+        low = spin(both, cos[:, ms], -sine[:, ms])
+        low = jnp.where(half_row == core, low, 0.0).astype(BF16)
+        dkl[ms, :] = low.T
+    put_grad(1, n1T, dkl)
+    vec[5:6, hq : hq + KV] = jnp.sum(dkl[...].astype(F32), axis=0, keepdims=True)
+    step_c(0)
+
+    def first_tile(i, _):
+        rows = pl.ds(pl.multiple_of(i * R, R), R)
+        d1p[rows, :] = (nt(dql[rows, :], weight(0)) + nt(dkl[rows, :], weight(1))).astype(BF16)
+        return 0
+
+    lax.fori_loop(0, T // R, first_tile, 0)
+    d1_copy = send(d1p, d1r, xs.at[5], xr.at[5], t_id)
+    d1_copy.start()
+    step_b(1)
+    step_e(7)
+    step_e(8)
+    d2_copy.wait_recv()
+    d1_copy.wait_recv()
+    step_c(1)
+    step_e(0)
+
+    def last_tile(i, _):
+        rows = pl.ds(pl.multiple_of(i * R, R), R)
+        _, xh, rstd = xhat_of(rows)
+        dn1 = d1p[rows, :].astype(F32) + d1r[rows, :].astype(F32)
+        dn2 = d2p[rows, :].astype(F32) + d2r[rows, :].astype(F32)
+        vec[0:1, :] += jnp.sum(dn1 * xh, axis=0, keepdims=True)
+        vec[1:2, :] += jnp.sum(dn1, axis=0, keepdims=True)
+        vec[2:3, :] += jnp.sum(dn2 * xh, axis=0, keepdims=True)
+        vec[3:4, :] += jnp.sum(dn2, axis=0, keepdims=True)
+        a = dn1 * g1[...] + dn2 * g2[...]
+        back = a - jnp.mean(a, axis=-1, keepdims=True) - xh * jnp.mean(a * xh, axis=-1, keepdims=True)
+        input_grad[rows, :] = (dy[rows, :].astype(F32) + rstd * back).astype(BF16)
+        return 0
+
+    lax.fori_loop(0, T // R, last_tile, 0)
+
+    v1 = send(vec, vrx, vs.at[0], vr.at[0], x_id)
+    v1.start()
+    v1.wait_recv()
+    vb[...] = vec[...] + vrx[...]
+    v2 = send(vb, vry, vs.at[1], vr.at[1], y_id)
+    v2.start()
+    step_e(1)
+    v2.wait_recv()
+    vz[z] = vb[...] + vry[...]
+    v3 = [send(vz.at[z], vz.at[z], vs.at[2 + j], vr.at[2 + j], z_ids[j]) for j in range(3)]
+    for c in v3:
+        c.start()
+    for c in v3:
+        c.wait_recv()
+    vec_out[...] = (vz[0] + vz[1]) + (vz[2] + vz[3])
+
+    for k in range(n_chunks):
+        for c in gather1(k):
+            c.wait_send()
+        gather2(k).wait_send()
+        gather3(k).wait_send()
+        red1(k).wait_send()
+        red2(k).wait_send()
+        for c in red3(k):
+            c.wait_send()
+    for s in range(1, REACH + 1):
+        @pl.when(me + s < count)
+        def _(s=s):
+            halo(s).wait_send()
+
+        @pl.when(me >= s)
+        def _(s=s):
+            for m in range(M):
+                back_copy(s, m).wait_send()
+    for c in [kv_copy, kvb_copy, d2_copy, kv_grad, d1_copy, v1, v2] + v3:
+        c.wait_send()
+
+
+def fused_layer(x, dy, shard, kvw, kvb, g1, b1, g2, b2, bq, bu, bo, cos, sine, start, pieces):
+    T, D = x.shape
+    M, n = start.shape[0], start.shape[2]
+    hq = bq.shape[0]
+    heads = hq // HDIM
+    KV = kvw.shape[1]
+    F = bu.shape[0] * bu.shape[2]
+    piece = F // pieces
+    rows, C = shard.shape
+    chunks = chunk_list(hq, KV, F, pieces)
+    k = len(chunks)
+    Wn = (REACH + 1) * n
+    V = pltpu.VMEM
+    S = pltpu.SemaphoreType.DMA
+    sds = jax.ShapeDtypeStruct
+    vm = pl.BlockSpec(memory_space=pltpu.VMEM)
+    mh = M * heads
+    scratch = [
+        V((4, 2, 2, rows, C), BF16), V((4, 2, 2, rows, C), BF16),
+        V((rows, KV), BF16), V((8, KV), F32),
+        V((D, T), BF16), V((T, D), BF16), V((D, T), BF16), V((D, T), BF16),
+        V((hq, D), BF16), V((mh, HDIM, n), BF16), V((mh, HDIM, n), BF16), V((mh, HDIM, n), BF16),
+        V((T, hq), BF16), V((mh, 1, n), F32), V((mh, 1, n), F32),
+        V((M, Wn, KV), BF16), V((M, KV, Wn), BF16),
+        V((1, n), F32), V((1, n), F32), V((HDIM, n), F32),
+        V((pieces, T, piece), BF16), V((pieces, T, piece), BF16),
+        V((mh, HDIM, n), F32), V((M, Wn, KV), F32),
+        V((REACH, M, n, KV), BF16), V((REACH, M, n, KV), BF16),
+        V((M, n, KV), BF16), V((M, n, KV), BF16),
+        V((T, D), BF16), V((T, D), BF16), V((T, D), BF16), V((T, D), BF16),
+        V((4, 2, rows, C), BF16), V((4, rows, C), BF16), V((3, rows, C), BF16),
+        V((8, D), F32), V((8, D), F32), V((8, D), F32), V((8, D), F32), V((4, 8, D), F32),
+        V((T, hq), BF16), V((T, KV), BF16),
+        S((k, 3)), S((k, 3)), S((k,)), S((k,)), S((k,)), S((k,)),
+        S((k,)), S((k,)), S((k,)), S((k,)), S((k, 3)), S((k, 3)),
+        S((REACH,)), S((REACH,)), S((REACH, M)), S((REACH, M)), S((6,)), S((6,)), S((5,)), S((5,)),
+    ]
+    return pl.pallas_call(
+        functools.partial(fused_kernel, chunks, pieces),
+        out_shape=(
+            sds((T, D), BF16), sds((M, n, KV), BF16), sds((T, D), BF16), sds((rows, C), F32), sds((8, D), F32),
+        ),
+        in_specs=[vm] * 15,
+        out_specs=(vm,) * 5,
+        scratch_shapes=scratch,
+        compiler_params=pltpu.CompilerParams(
+            collective_id=0, has_side_effects=True, vmem_limit_bytes=62 << 20
+        ),
+        name="fused_layer",
+    )(x, dy, shard, kvw, kvb, g1, b1, g2, b2, bq, bu, bo, cos, sine, start)
+
+
+PIECES = 3
+
+
+def fits_fused(hidden_in, query_weight):
+    rows = query_weight.shape[0]
+    return lax.axis_size("dp") == 16 and rows % 16 == 0 and hidden_in.shape[1] % 256 == 0
+
+
+def pack_columns(query_part, keyval_part, out_part, up_part, down_part, pieces):
+    columns = [query_part, keyval_part, out_part]
+    piece = up_part.shape[1] // pieces
+    for c in range(pieces):
+        columns.append(up_part[:, c * piece : (c + 1) * piece])
+        columns.append(down_part[:, c * piece : (c + 1) * piece])
+    return jnp.concatenate(columns, axis=1)
+
+
+def fused_device(
+    hidden_in,
+    positions,
+    out_grad,
+    norm1_gain,
+    norm1_bias,
+    norm2_gain,
+    norm2_bias,
+    query_weight,
+    query_bias,
+    keyval_weight,
+    keyval_bias,
+    attn_out_weight,
+    attn_out_bias,
+    up_weight,
+    up_bias,
+    down_weight,
+    down_bias,
+):
+    micro, tokens, width = hidden_in.shape
+    core = lax.axis_index("tensor")
+    hq = query_bias.shape[0]
+    ff = up_bias.shape[0]
+    piece = ff // PIECES
+    half = keyval_bias.shape[0]
+
+    def own_half(block):
+        zero = jnp.zeros_like(block)
+        return jnp.where(
+            core == 0,
+            jnp.concatenate([block, zero], axis=1),
+            jnp.concatenate([zero, block], axis=1),
+        )
+
+    keyval_own = own_half(keyval_weight)
+    bias_own = jnp.broadcast_to(own_half(keyval_bias[None, :]), (8, 2 * half))
+    shard = pack_columns(
+        query_weight, keyval_own, attn_out_weight.T, up_weight, down_weight.T, PIECES
+    )
+    flat = positions.reshape(1, micro * tokens).astype(jnp.float32)
+    inverse = 10000.0 ** (-(jnp.arange(ROT // 2, dtype=jnp.float32) * 2.0) / ROT)
+    angles = inverse[:, None] * flat
+    row_ids = jnp.arange(tokens, dtype=jnp.int32)[None, :]
+    first = (REACH * tokens + row_ids - positions)[:, None, :]
+    layer_out, keyval_out, input_grad, grads, vec = fused_layer(
+        hidden_in.reshape(micro * tokens, width),
+        out_grad.reshape(micro * tokens, width),
+        shard,
+        keyval_own,
+        bias_own,
+        norm1_gain[None, :],
+        norm1_bias[None, :],
+        norm2_gain[None, :],
+        norm2_bias[None, :],
+        query_bias[:, None],
+        up_bias.reshape(PIECES, 1, piece),
+        (attn_out_bias + down_bias)[None, :],
+        jnp.cos(angles),
+        jnp.sin(angles),
+        first,
+        PIECES,
+    )
+    chunks = chunk_list(hq, 2 * half, ff, PIECES)
+
+    def columns(k):
+        return grads[:, chunks[k][0] : chunks[k][0] + chunks[k][1]]
+
+    def own_columns(block):
+        return jnp.where(core == 0, block[..., :half], block[..., half:])
+
+    grad_up = jnp.concatenate([columns(3 + 2 * c) for c in range(PIECES)], axis=1)
+    grad_down = jnp.concatenate([columns(4 + 2 * c) for c in range(PIECES)], axis=1).T
+    return (
+        layer_out.reshape(hidden_in.shape),
+        keyval_out,
+        input_grad.reshape(hidden_in.shape),
+        vec[0],
+        vec[1],
+        vec[2],
+        vec[3],
+        columns(0),
+        vec[5, :hq],
+        own_columns(columns(1)),
+        own_columns(vec[5, hq : hq + 2 * half]),
+        columns(2).T,
+        vec[4],
+        grad_up,
+        vec[6:8].reshape(-1)[:ff],
+        grad_down,
+        vec[4],
+    )
+
+
+def on_device(*arguments):
+    if fits_fused(arguments[0], arguments[7]):
+        return fused_device(*arguments)
+    return plain_layer(*arguments)
+
+
 def solution(mesh):
     return jax.shard_map(
         on_device,

time: 1200 us -> 256 us (0.21)
  waiting for transfers between devices: 647 us -> 0 us
  Pallas kernels: 0 us -> 219 us
  matrix products: 216 us -> 0 us
  blocking collectives: 202 us -> 0 us
  other arithmetic: 62.4 us -> 8.26 us
  starting transfers between devices: 32 us -> 0 us
  between operations: 18 us -> 0.7 us
  local copies, waits for them, and re-layouts: 14.6 us -> 26.8 us
    reduce_scatter x7 -> x0, waiting for transfers between devices: 549 us -> none  [the longest x1 143 us: on_device(): lax.psum_scatter(grad_down_w, 'dp', scatter_dimension=1, tiled=True)]
    pallas_call x0 -> x1, Pallas kernels: none -> 219 us  [fused_layer(): pl.pallas_call(functools.partial(fused_kernel, chunks, pieces), out_shape...]
    dot_general x90 -> x0, matrix products: 216 us -> none  [the longest x10 34.3 us: attend_backward(): jnp.einsum('htd,kd->htk', grad_mixture, value_rows, preferred_element_typ...]
    all_gather x5 -> x0, blocking collectives: 128 us -> none  [the longest x1 43.4 us: fetch_weights(): lax.all_gather(shard_weights[1], 'dp', axis=0, tiled=True)]
    all_gather x2 -> x0, waiting for transfers between devices: 88.8 us -> none  [the longest x1 51.7 us: fetch_weights(): lax.all_gather(shard_weights[4], 'dp', axis=1, tiled=True)]
    psum x1 -> x0, blocking collectives: 73.9 us -> none  [on_device(): lax.psum((grad_n1_gain, grad_n1_bias, grad_n2_gain, grad_n2_bias, grad_ro...]
    reduce_sum x14 -> x0, other arithmetic: 39.5 us -> none  [the longest x6 24.1 us: attend_forward(): jnp.sum(jnp.where(visible, jnp.exp(masked - new_top[..., None]), 0.0), ax...]
    ppermute x16 -> x0, starting transfers between devices: 31.1 us -> none  [shifted(): lax.ppermute(value, axis, [(source, source + steps) for source in range(i...]
  transfers between devices with their start and end apart: 26 -> 0, of which waited for: 10 -> 0; matrix products, arithmetic and copies ran while one was open for 16% -> 0% of each run, Pallas kernels for 0% -> 0%
where the time goes in v2:
time: 256 us; the launch traced here: 255 us
  Pallas kernels  219 us (86%)
  local copies, waits for them, and re-layouts  26.8 us (10%)
  other arithmetic  8.26 us (3%)
    pallas_call x1, Pallas kernels, fused_layer(): pl.pallas_call(functools.partial(fused_kernel, chunks, pieces), out_shape...  219 us
    unnamed x22, local copies, waits for them, and re-layouts  9.38 us

profile of v2, /device:TPU:0, one launch (start us, length us, event | category | flops | bytes accessed | tf_op | source)
XLA Modules:
  0.0 255.0 jit_solution(15065119300717895602)
XLA Ops:
  0.7 0.8 constant_dynamic-update-slice_fusion.1
  1.4 1.5 constant_dynamic-update-slice_fusion
  2.9 0.8 bitcast_dynamic-update-slice_fusion
  3.7 0.8 slice_dynamic-update-slice_fusion.5
  4.5 0.8 slice_dynamic-update-slice_fusion.2
  5.3 0.8 slice_dynamic-update-slice_fusion.4
  6.1 0.8 slice_dynamic-update-slice_fusion.1
  6.9 0.8 slice_dynamic-update-slice_fusion.3
  7.7 0.8 slice_dynamic-update-slice_fusion.shard
  8.5 0.0 copy-start.2
  8.5 0.8 fusion
  9.3 0.6 broadcast_in_dim.37.kvb
  9.9 1.3 broadcast_in_dim.38.g1
  11.1 1.3 broadcast_in_dim.39.b1
  12.4 1.3 broadcast_in_dim.40.g2
  13.7 1.3 broadcast_in_dim.41.b2
  14.9 1.5 broadcast_in_dim.45.bq
  16.4 1.3 reshape.79.bu
  17.7 0.7 add.22
  18.4 0.6 broadcast_in_dim.43.bo
  19.0 0.8 broadcast_subtract_fusion
  19.8 0.8 multiply_sine_fusion
  20.6 0.6 broadcast_in_dim.44.start
  21.2 0.0 copy-done.2
  21.2 219.3 %fused_layer.1 = (bf16[1024,768]{1,0:T(8,128)(2,1)}, bf16[2,512,128]{2,1,0:T(8,128)(2,1)}, bf16[1024,768]{1,0:T(8,128)(2,1)}, f32[48,3968]{1,0:T(8,128)}, f32[8,768]{1,0:T(8,128)}) custom-call(bf16[1024,768]{1,0:T(8,128)(2,1)} %bitcast.19, bf16[1024,768]{1,0:T(8,128)(2,1)} %bitcast.20, bf16[48,3968]{1,0:T(8,128)(2,1)} %copy-done.2, ...), custom_call_target="tpu_custom_call" | custom-call | tf_op jit(solution)/shard_map/fused_layer/pallas_call | solution.py:923
  240.5 0.0 copy-start.1
  240.5 1.6 slice_reduce_fusion
  242.1 0.0 copy-start.4
  242.1 1.6 slice_bitcast_fusion
  243.7 1.3 slice_reduce_fusion.5
  245.0 1.5 slice_select_fusion
  246.5 1.3 fusion.1
  247.8 1.2 fusion.2
  249.0 0.9 pad_maximum_fusion
  249.8 0.7 slice.105
  250.6 0.6 reshape.82
  251.2 0.6 copy.48
  251.8 0.0 copy-done.1
  251.8 0.0 copy-start.3
  251.8 0.0 copy-start
  251.8 1.1 copy.49
  252.9 0.0 copy-done.4
  252.9 0.0 copy-done.3
  252.9 0.7 copy.50
  253.6 0.2 copy-done
  253.9 1.1 copy.51
  (3 shorter events, 0.0 us)
Async XLA Ops:
  8.5 12.8 %copy-start.2 = (bf16[48,3968]{1,0:T(8,128)(2,1)}, bf16[48,3968]{1,0:T(8,128)(2,1)S(1)}, u32[]{:S(2)}) copy-start(bf16[48,3968]{1,0:T(8,128)(2,1)S(1)} %slice_dynamic-update-slice_fusion.shard) | copy-start | bytes 1142788
  240.5 11.3 %copy-start.1 = (bf16[1024,768]{1,0:T(8,128)(2,1)S(1)}, bf16[1024,768]{1,0:T(8,128)(2,1)}, u32[]{:S(2)}) copy-start(bf16[1024,768]{1,0:T(8,128)(2,1)} %get-tuple-element.22) | copy-start | bytes 4718596
  242.1 10.9 %copy-start.4 = (f32[768]{0:T(1024)}, f32[768]{0:T(1024)S(1)}, u32[]{:S(2)}) copy-start(f32[768]{0:T(1024)S(1)} %get-tuple-element.111) | copy-start | bytes 9220
  251.8 1.2 copy-start.3
  251.8 2.1 copy-start

commit v3 on v0

--- a/solution.py
+++ b/solution.py
@@ -1,14 +1,19 @@
+import functools
 import jax
 import jax.numpy as jnp
 from jax import lax
+from jax.experimental import pallas as pl
+from jax.experimental.pallas import tpu as pltpu
 from jax.sharding import PartitionSpec as P
 
 HDIM = 64
 ROT = 16
 REACH = 4
-
-
 epsilon = 1e-05
+MESH = pl.DeviceIdType.MESH
+LOW = -1e30
+F32 = jnp.float32
+BF16 = jnp.bfloat16
 
 
 def shifted(value, axis, steps):
@@ -125,7 +130,7 @@
     return (grad_queries, key_terms)
 
 
-def on_device(
+def plain_layer(
     hidden_in,
     positions,
     out_grad,
@@ -324,6 +329,808 @@
     )
 
 
+def nn(a, b):
+    return jnp.dot(a, b, preferred_element_type=F32)
+
+
+def nt(a, b):
+    return lax.dot_general(a, b, (((1,), (1,)), ((), ())), preferred_element_type=F32)
+
+
+def chunk_list(q_cols, kv_cols, ff_cols, pieces):
+    sizes = [kv_cols, q_cols, q_cols] + [ff_cols // pieces] * (2 * pieces)
+    at = 0
+    out = []
+    for size in sizes:
+        out.append((at, size))
+        at += size
+    return out
+
+
+def near_tiles(n, half):
+    own = REACH * n
+    return [(own + a, half, a, n - a, True) for a in range(0, n, half)]
+
+
+def far_tiles(n, half):
+    own = REACH * n
+    out = [(own - j * n, n, 0, n, False) for j in range(1, REACH)]
+    return out + [(a, half, 0, min(n, a + half), False) for a in range(0, n, half)]
+
+
+def spin(rows, cos, sine):
+    h = ROT // 2
+    a, b, rest = rows[..., :h, :], rows[..., h:ROT, :], rows[..., ROT:, :]
+    return jnp.concatenate([a * cos - b * sine, b * cos + a * sine, rest], axis=-2)
+
+
+def fused_kernel(
+    chunks, pieces,
+    x, dy, positions, g1, b1, g2, b2, w_query, b_query, w_keyval, b_keyval, w_out, b_out, w_up, b_up, w_down, b_down,
+    layer_out, keyval_out, input_grad, grads_out, vec_out,
+    W, G, n1T, n2, n2T, dyT, wqT, qT, doT, oT, o_nat, lse, dvec, kvwin, kvTwin, low_kv,
+    cos, sine, start, m_s, l_s, acc, gbuf, dubuf, dqT, dkv, dkvT, turned, hs, hr, hx, hxr, kvo, yp, yr, d2p, d2r,
+    r1, r2, r3, vec, vp, vz, dql, dkl,
+    gzs, gzr, g2s, g2r, g3s, g3r, a1s, a1r, a2s, a2r, azs, azr,
+    hfs, hfr, hbs, hbr, fws, fwr, xs, xr, ts, tr, vs, vr,
+):
+    T, D = x.shape
+    M, W_rows, KV = kvwin.shape
+    n = T // M
+    heads = qT.shape[0] // M
+    hq = heads * HDIM
+    own = REACH * n
+    piece = dubuf.shape[2]
+    scale = HDIM ** (-0.5)
+    me = lax.axis_index("dp")
+    core = lax.axis_index("tensor")
+    count = lax.axis_size("dp")
+    z, y, xx = me // 4, (me // 2) % 2, me % 2
+    shard_rows = w_query.shape[0]
+    n_chunks = len(chunks)
+    kKV, kQ, kO = 0, 1, 2
+    kUp = [3 + 2 * c for c in range(pieces)]
+    kDown = [4 + 2 * c for c in range(pieces)]
+    mine = pl.ds(pl.multiple_of(core * HDIM, HDIM), HDIM)
+    other = pl.ds(pl.multiple_of((1 - core) * HDIM, HDIM), HDIM)
+
+    def at(zz, yy, xo):
+        return {"dp": zz * 4 + yy * 2 + xo}
+
+    z_ids = [at((z + d) % 4, y, xx) for d in (1, 2, 3)]
+    y_id, x_id, d_id = at(z, 1 - y, xx), at(z, y, 1 - xx), at(z, 1 - y, 1 - xx)
+    t_id = {"tensor": 1 - core}
+
+    def send(src, dst, ss, rs, to):
+        return pltpu.make_async_remote_copy(
+            src_ref=src, dst_ref=dst, send_sem=ss, recv_sem=rs, device_id=to, device_id_type=MESH
+        )
+
+    bar = pltpu.get_barrier_semaphore()
+    peers = z_ids + [y_id, x_id, d_id, t_id]
+    peers += [{"dp": (me + s) % count} for s in range(1, REACH + 1)]
+    peers += [{"dp": (me + count - s) % count} for s in range(1, REACH + 1)]
+    for p in peers:
+        pl.semaphore_signal(bar, inc=1, device_id=p, device_id_type=MESH)
+    pl.semaphore_wait(bar, len(peers))
+
+    def cols(k):
+        return pl.ds(chunks[k][0], chunks[k][1])
+
+    def halves(k):
+        c0, cn = chunks[k]
+        if cn < 256:
+            return pl.ds(c0, cn), None
+        first = cn // 256 * 128
+        return pl.ds(c0, first), pl.ds(c0 + first, cn - first)
+
+    def gather_z(k):
+        r = W.at[z, y, xx, :, cols(k)]
+        return [send(r, r, gzs.at[k, j], gzr.at[k, j], z_ids[j]) for j in range(3)]
+
+    def gather_col(k):
+        r = W.at[:, y, xx, :, cols(k)]
+        return [send(r, r, g2s.at[k, 0], g2r.at[k, 0], x_id), send(r, r, g2s.at[k, 1], g2r.at[k, 1], y_id)]
+
+    def gather_far(k):
+        first, second = halves(k)
+        r = W.at[:, y, 1 - xx, :, first]
+        out = [send(r, r, g3s.at[k, 0], g3r.at[k, 0], y_id)]
+        if second is not None:
+            r = W.at[:, 1 - y, xx, :, second]
+            out.append(send(r, r, g3s.at[k, 1], g3r.at[k, 1], x_id))
+        return out
+
+    def start1(k):
+        for c in gather_z(k):
+            c.start()
+
+    def step2(k):
+        for c in gather_z(k):
+            c.wait_recv()
+        for c in gather_col(k):
+            c.start()
+
+    def step3(k):
+        for c in gather_col(k):
+            c.wait_recv()
+        for c in gather_far(k):
+            c.start()
+
+    def arrived(k):
+        for c in gather_far(k):
+            c.wait_recv()
+
+    def weight(k):
+        c0, cn = chunks[k]
+        return W[:, :, :, :, c0 : c0 + cn].reshape(D, cn)
+
+    def red1(k):
+        first, second = halves(k)
+        out = [send(G.at[:, :, 1 - xx, :, first], r1.at[:, :, :, first], a1s.at[k, 0], a1r.at[k, 0], x_id)]
+        if second is not None:
+            out.append(send(G.at[:, 1 - y, :, :, second], r1.at[:, :, :, second], a1s.at[k, 1], a1r.at[k, 1], y_id))
+        return out
+
+    def red2(k):
+        first, second = halves(k)
+        out = [send(r1.at[:, 1 - y, :, first], r2.at[:, :, first], a2s.at[k, 0], a2r.at[k, 0], y_id)]
+        if second is not None:
+            out.append(send(r1.at[:, 1 - xx, :, second], r2.at[:, :, second], a2s.at[k, 1], a2r.at[k, 1], x_id))
+        return out
+
+    def red3(k):
+        return [
+            send(r2.at[(z + j + 1) % 4, :, cols(k)], r3.at[j, :, cols(k)], azs.at[k, j], azr.at[k, j], z_ids[j])
+            for j in range(3)
+        ]
+
+    def step_a(k):
+        for c in red1(k):
+            c.start()
+
+    def step_b(k):
+        first, second = halves(k)
+        for c in red1(k):
+            c.wait_recv()
+
+        def add(i, _):
+            zz, o = i // 2, i % 2
+            r1[zz, o, :, first] = r1[zz, o, :, first] + G[zz, o, xx, :, first]
+            if second is not None:
+                r1[zz, o, :, second] = r1[zz, o, :, second] + G[zz, y, o, :, second]
+            return 0
+
+        lax.fori_loop(0, 8, add, 0)
+        for c in red2(k):
+            c.start()
+
+    def step_c(k):
+        first, second = halves(k)
+        for c in red2(k):
+            c.wait_recv()
+
+        def add(i, _):
+            r2[i, :, first] = r2[i, :, first] + r1[i, y, :, first]
+            if second is not None:
+                r2[i, :, second] = r2[i, :, second] + r1[i, xx, :, second]
+            return 0
+
+        lax.fori_loop(0, 4, add, 0)
+        for c in red3(k):
+            c.start()
+
+    def step_e(k):
+        for c in red3(k):
+            c.wait_recv()
+        total = r2[z, :, cols(k)].astype(F32)
+        for j in range(3):
+            total = total + r3[j, :, cols(k)].astype(F32)
+        grads_out[:, cols(k)] = total
+
+    def place(k, block):
+        c0 = chunks[k][0]
+        W[z, y, xx, :, c0 : c0 + block.shape[1]] = block
+
+    place(kKV, jnp.concatenate([w_keyval[...], jnp.zeros((shard_rows, HDIM), BF16)], axis=1))
+    start1(kKV)
+    place(kQ, w_query[...])
+    start1(kQ)
+    place(kO, w_out[...])
+    for c in range(pieces):
+        place(kUp[c], w_up[:, c * piece : (c + 1) * piece])
+        place(kDown[c], w_down[:, c * piece : (c + 1) * piece])
+
+    R = 256
+    vec[...] = jnp.zeros_like(vec)
+
+    def row(ref):
+        return ref[...].reshape(1, ref.shape[0])
+
+    g1v, b1v, g2v, b2v = row(g1), row(b1), row(g2), row(b2)
+
+    def xhat_of(rows):
+        v = x[rows, :].astype(F32)
+        c = v - jnp.mean(v, axis=-1, keepdims=True)
+        rstd = lax.rsqrt(jnp.mean(c * c, axis=-1, keepdims=True) + epsilon)
+        return v, c * rstd, rstd
+
+    def norm_tile(i, _):
+        rows = pl.ds(pl.multiple_of(i * R, R), R)
+        _, xh, _ = xhat_of(rows)
+        n1v = (xh * g1v + b1v).astype(BF16)
+        n2v = (xh * g2v + b2v).astype(BF16)
+        n2[rows, :] = n2v
+        n1T[:, rows] = n1v.T
+        n2T[:, rows] = n2v.T
+        d = dy[rows, :]
+        dyT[:, rows] = d.T
+        vec[4:5, :] += jnp.sum(d.astype(F32), axis=0, keepdims=True)
+        return 0
+
+    lax.fori_loop(0, T // R, norm_tile, 0)
+    step2(kKV)
+    h = ROT // 2
+    index = lax.broadcasted_iota(jnp.int32, (h, 1), 0)
+    inverse = jnp.zeros((h, 1), F32)
+    for i in range(h):
+        inverse = jnp.where(index == i, 10000.0 ** (-(2.0 * i) / ROT), inverse)
+    for m in range(M):
+        ms = slice(m * n, (m + 1) * n)
+        place_row = positions[m : m + 1, :]
+        angle = inverse * place_row.astype(F32)
+        cos[:, ms] = jnp.cos(angle)
+        sine[:, ms] = jnp.sin(angle)
+        start[m] = lax.broadcasted_iota(jnp.int32, (1, n), 1) + own - place_row
+
+    def keyval_spin(rows, m, sign):
+        ms = slice(m * n, (m + 1) * n)
+        return spin(rows, jnp.where(core == 0, cos[:, ms], 1.0), jnp.where(core == 0, sign * sine[:, ms], 0.0))
+
+    def column(ref):
+        size = ref.shape[0]
+        return jnp.broadcast_to(ref[...].reshape(1, size), (8, size)).T[:, 0:1]
+
+    step3(kKV)
+    step2(kQ)
+    arrived(kKV)
+    wkvT = weight(kKV).T[0:HDIM]
+    bkv = column(b_keyval)
+    for m in range(M):
+        ms = slice(m * n, (m + 1) * n)
+        low_kv[m] = keyval_spin(nn(wkvT, n1T[:, ms]) + bkv, m, 1.0).astype(BF16)
+    kvTwin[:, mine, own : own + n] = low_kv[...]
+
+    def block(s):
+        return pl.ds((REACH - s) * n, n)
+
+    def halo(s):
+        return send(
+            low_kv, kvTwin.at[:, mine, block(s)], hfs.at[s - 1], hfr.at[s - 1], {"dp": (me + s) % count}
+        )
+
+    def across(s):
+        part = kvTwin.at[:, mine, block(s)]
+        return send(part, part, fws.at[s], fwr.at[s], t_id)
+
+    for s in range(1, REACH + 1):
+        @pl.when(me + s < count)
+        def _(s=s):
+            halo(s).start()
+    across(0).start()
+
+    start1(kO)
+    start1(kUp[0])
+    step3(kQ)
+    across(0).wait_recv()
+    for m in range(M):
+        natural = kvTwin[m, :, own : own + n].T
+        kvwin[m, own : own + n, :] = natural
+        keyval_out[m] = natural
+    arrived(kQ)
+    wqT[...] = weight(kQ).T
+    bq = column(b_query)
+    for m in range(M):
+        ms = slice(m * n, (m + 1) * n)
+        lin = nn(wqT[...], n1T[:, ms]) + bq
+        spun = spin(lin.reshape(heads, HDIM, n), cos[:, ms], sine[:, ms]) * scale
+        qT[m * heads : (m + 1) * heads] = spun.astype(BF16)
+    near, far = near_tiles(n, n // 2), far_tiles(n, n // 2)
+    tops, totals, sums = lse, dvec, dqT
+
+    def visible(w0, kn, q0, qn, first, causal):
+        key = lax.broadcasted_iota(jnp.int32, (kn, 1), 0) + w0
+        seen = key >= first
+        if causal:
+            query = lax.broadcasted_iota(jnp.int32, (1, qn), 1) + (q0 + own)
+            seen = seen & (key <= query)
+        return seen
+
+    def padded_query(i):
+        return jnp.concatenate([qT[i], jnp.zeros((KV - HDIM, n), BF16)], axis=0)
+
+    def forward_near(i, _):
+        m = i // heads
+        q = padded_query(i)
+        first = start[m]
+        m_s[...] = jnp.full_like(m_s, LOW)
+        l_s[...] = jnp.zeros_like(l_s)
+        acc[...] = jnp.zeros_like(acc)
+        forward_tiles(m, q, first, near)
+        tops[i], totals[i], sums[i] = m_s[...], l_s[...], acc[...]
+        return 0
+
+    def forward_tiles(m, q, first, tiles):
+        for w0, kn, q0, qn, causal in tiles:
+            qs = slice(q0, q0 + qn)
+            sc = nn(kvwin[m, w0 : w0 + kn, :], q[:, qs])
+            sc = jnp.where(visible(w0, kn, q0, qn, first[:, qs], causal), sc, LOW)
+            before = m_s[:, qs]
+            top = jnp.maximum(before, jnp.max(sc, axis=0, keepdims=True))
+            p = jnp.exp(sc - top)
+            shrink = jnp.exp(before - top)
+            l_s[:, qs] = l_s[:, qs] * shrink + jnp.sum(p, axis=0, keepdims=True)
+            m_s[:, qs] = top
+            acc[:, qs] = acc[:, qs] * shrink + nn(kvTwin[m, HDIM:KV, w0 : w0 + kn], p.astype(BF16))
+
+    def forward_far(i, _):
+        m = i // heads
+        q = padded_query(i)
+        m_s[...], l_s[...], acc[...] = tops[i], totals[i], sums[i]
+        forward_tiles(m, q, start[m], far)
+        o = acc[...] / l_s[...]
+        oT[i] = o.astype(BF16)
+        sums[i] = o
+        lse[i] = m_s[...] + jnp.log(l_s[...])
+        scheduled(far_plan, i)
+        return 0
+
+    def scheduled(plan, i):
+        for j, act in plan.items():
+            pl.when(i == j)(lambda act=act: (act(), None)[1])
+
+    def near_step(i, _):
+        forward_near(i, 0)
+        scheduled(near_plan, i)
+        return 0
+
+    near_plan = {
+        0: lambda: step2(kO),
+        4: lambda: start1(kDown[0]),
+        8: lambda: (step2(kUp[0]), step3(kO)),
+    }
+    lax.fori_loop(0, M * heads, near_step, 0)
+    for s in range(1, REACH + 1):
+        @pl.when(me >= s)
+        def _(s=s):
+            halo(s).wait_recv()
+            across(s).start()
+
+        @pl.when(me < s)
+        def _(s=s):
+            kvTwin[:, :, block(s)] = jnp.zeros((M, KV, n), BF16)
+
+    step2(kDown[0])
+    start1(kUp[1])
+    for s in range(1, REACH + 1):
+        @pl.when(me >= s)
+        def _(s=s):
+            across(s).wait_recv()
+
+        for m in range(M):
+            kvwin[m, block(s), :] = kvTwin[m, :, block(s)].T
+
+    far_plan = {
+        0: lambda: (step3(kUp[0]), start1(kDown[1])),
+        2: lambda: step3(kDown[0]),
+        4: lambda: (step2(kUp[1]), start1(kUp[2])),
+        7: lambda: (step2(kDown[1]), start1(kDown[2])),
+        9: lambda: step3(kUp[1]),
+    }
+    lax.fori_loop(0, M * heads, forward_far, 0)
+
+    arrived(kO)
+    wo = weight(kO).T
+    for m in range(M):
+        ms = slice(m * n, (m + 1) * n)
+        doT[m * heads : (m + 1) * heads] = nn(wo, dyT[:, ms]).astype(BF16).reshape(heads, HDIM, n)
+
+    def mix_dots(i, _):
+        dvec[i] = jnp.sum(doT[i].astype(F32) * sums[i], axis=0, keepdims=True)
+        return 0
+
+    lax.fori_loop(0, M * heads, mix_dots, 0)
+    for m in range(M):
+        o_nat[m * n : (m + 1) * n, :] = oT[m * heads : (m + 1) * heads].reshape(hq, n).T
+
+    def put_grad(k, leftT, right):
+        c0, cn = chunks[k]
+
+        def half(i, _):
+            rows = pl.ds(pl.multiple_of(i * (D // 2), 128), D // 2)
+            part = nn(leftT[rows, :], right[...]).astype(BF16)
+            G[pl.ds(i * 2, 2), :, :, :, c0 : c0 + cn] = part.reshape(2, 2, 2, shard_rows, cn)
+            return 0
+
+        lax.fori_loop(0, 2, half, 0)
+        step_a(k)
+
+    put_grad(kO, dyT, o_nat)
+    step3(kDown[1])
+    step2(kUp[2])
+
+    def feed_forward(c):
+        ku, kd = kUp[c], kDown[c]
+        arrived(ku)
+        arrived(kd)
+        (u0, _), (d0, _) = chunks[ku], chunks[kd]
+        up_bias = b_up[c * piece : (c + 1) * piece].reshape(1, piece)
+
+        def rows_tile(i, _):
+            rows = pl.ds(pl.multiple_of(i * R, R), R)
+            u = nn(n2[rows, :], W[:, :, :, :, u0 : u0 + piece].reshape(D, piece)) + up_bias
+            phi = 0.5 * (1.0 + lax.erf(u * 0.7071067811865476))
+            slope = phi + u * (jnp.exp(-0.5 * u * u) * 0.3989422804014327)
+            gbuf[rows, c * piece : (c + 1) * piece] = (u * phi).astype(BF16)
+            dg = nn(dy[rows, :], W[:, :, :, :, d0 : d0 + piece].reshape(D, piece))
+            dubuf[c, rows, :] = (slope * dg).astype(BF16)
+            return 0
+
+        lax.fori_loop(0, T // R, rows_tile, 0)
+        put_grad(ku, n2T, dubuf.at[c])
+        put_grad(kd, dyT, gbuf.at[:, c * piece : (c + 1) * piece])
+
+    def branch_tile(i, _):
+        rows = pl.ds(pl.multiple_of(i * R, R), R)
+        total = nt(o_nat[rows, :], weight(kO))
+        back = jnp.zeros((R, D), F32)
+        for c in range(pieces):
+            total = total + nt(gbuf[rows, c * piece : (c + 1) * piece], weight(kDown[c]))
+            back = back + nt(dubuf[c, rows, :], weight(kUp[c]))
+        yp[rows, :] = total.astype(BF16)
+        d2p[rows, :] = back.astype(BF16)
+        return 0
+
+    y_copy = send(yp, yr, xs.at[0], xr.at[0], t_id)
+    d2_copy = send(d2p, d2r, xs.at[1], xr.at[1], t_id)
+
+    def branches():
+        lax.fori_loop(0, T // R, branch_tile, 0)
+        y_copy.start()
+        d2_copy.start()
+        for c in range(pieces):
+            part = jnp.sum(dubuf[c].astype(F32), axis=0, keepdims=True)
+            done = 0
+            while done < piece:
+                flat = c * piece + done
+                line, col = flat // D, flat % D
+                width = min(piece - done, D - col)
+                vec[6 + line : 7 + line, col : col + width] = part[:, done : done + width]
+                done += width
+
+    feed_forward(0)
+    step2(kDown[2])
+
+    dkv[...] = jnp.zeros_like(dkv)
+
+    def backward_tiles(i, tiles):
+        m = i // heads
+        zero = jnp.zeros((HDIM, n), BF16)
+        q = jnp.concatenate([qT[i], zero], axis=0)
+        do = jnp.concatenate([zero, doT[i]], axis=0)
+        qdo = jnp.concatenate([qT[i], doT[i]], axis=0).T
+        first, ls, dots = start[m], lse[i], dvec[i]
+        for w0, kn, q0, qn, causal in tiles:
+            qs = slice(q0, q0 + qn)
+            rows = kvwin[m, w0 : w0 + kn, :]
+            sc = nn(rows, q[:, qs])
+            sc = jnp.where(visible(w0, kn, q0, qn, first[:, qs], causal), sc, LOW)
+            p = jnp.exp(sc - ls[:, qs])
+            dp = nn(rows, do[:, qs])
+            ds = (p * (dp - dots[:, qs])).astype(BF16)
+            for_k = nn(ds, qdo[qs])
+            for_v = nn(p.astype(BF16), qdo[qs])
+            lane = lax.broadcasted_iota(jnp.int32, for_k.shape, 1)
+            dkv[m, w0 : w0 + kn, :] += jnp.where(lane < HDIM, for_k, for_v)
+            dqT[i, :, qs] += nn(kvTwin[m, 0:HDIM, w0 : w0 + kn], ds)
+
+    def backward_far(i, _):
+        scheduled(feed_plan, i)
+        dqT[i] = jnp.zeros((HDIM, n), F32)
+        backward_tiles(i, far)
+        scheduled(back_far_plan, i)
+        return 0
+
+    def backward_near(i, _):
+        backward_tiles(i, near)
+        scheduled(back_near_plan, i)
+        return 0
+
+    def back_copy(s, m):
+        return send(
+            hs.at[s - 1, m], hr.at[s - 1, m], hbs.at[s - 1, m], hbr.at[s - 1, m],
+            {"dp": (me + count - s) % count},
+        )
+
+    def half_copy(m):
+        part = pl.ds(0, own)
+        return send(hx.at[m, :, part], hxr.at[m, :, part], xs.at[2 + m], xr.at[2 + m], t_id)
+
+    def own_copy(m):
+        part = pl.ds(own, n)
+        return send(hx.at[m, :, part], hxr.at[m, :, part], xs.at[2 + M + m], xr.at[2 + M + m], t_id)
+
+    def split(m, j):
+        js = slice(j * n, (j + 1) * n)
+        turned[...] = dkv[m, js, :].T
+        dkvT[m, :, js] = turned[mine, :]
+        hx[m, :, js] = turned[other, :].astype(BF16)
+
+    def give_half(m):
+        for j in range(REACH):
+            split(m, j)
+        half_copy(m).start()
+
+    def return_halo(m):
+        half_copy(m).wait_recv()
+        for j in range(REACH):
+            js = slice(j * n, (j + 1) * n)
+            hs[REACH - j - 1, m] = (dkvT[m, :, js] + hxr[m, :, js].astype(F32)).astype(BF16)
+        for s in range(1, REACH + 1):
+            @pl.when(me >= s)
+            def _(s=s):
+                back_copy(s, m).start()
+
+    def give_own(m):
+        split(m, REACH)
+        own_copy(m).start()
+
+    feed_plan = {
+        3: lambda: feed_forward(1),
+        6: lambda: (feed_forward(2), branches()),
+    }
+    back_far_plan = {
+        0: lambda: (step3(kUp[2]), step_b(kO)),
+        1: lambda: (step3(kDown[2]), step_b(kUp[0])),
+        2: lambda: (step_b(kDown[0]), step_c(kO)),
+        3: lambda: (step_c(kUp[0]), step_c(kDown[0])),
+        4: lambda: step_e(kO),
+        5: lambda: (give_half(0), step_b(kUp[1]), step_e(kUp[0])),
+        6: lambda: (step_b(kDown[1]), step_c(kUp[1]), step_e(kDown[0])),
+        7: lambda: (return_halo(0), step_c(kDown[1])),
+        8: lambda: (step_b(kUp[2]), step_e(kUp[1])),
+        9: lambda: step_b(kDown[2]),
+        10: lambda: (step_c(kUp[2]), step_e(kDown[1])),
+        11: lambda: (give_half(1), step_c(kDown[2])),
+    }
+    back_near_plan = {
+        2: lambda: return_halo(1),
+        5: lambda: (give_own(0), step_e(kUp[2])),
+        8: lambda: step_e(kDown[2]),
+        11: lambda: give_own(1),
+    }
+    lax.fori_loop(0, M * heads, backward_far, 0)
+    lax.fori_loop(0, M * heads, backward_near, 0)
+
+    for m in range(M):
+        ms = slice(m * n, (m + 1) * n)
+        rows = dqT[m * heads : (m + 1) * heads] * scale
+        low = spin(rows, cos[:, ms], -sine[:, ms]).astype(BF16)
+        dql[ms, :] = low.reshape(hq, n).T
+    put_grad(kQ, n1T, dql)
+    vec[5:6, 0:hq] = jnp.sum(dql[...].astype(F32), axis=0, keepdims=True)
+
+    for m in range(M):
+        ms = slice(m * n, (m + 1) * n)
+        own_copy(m).wait_recv()
+        dko = dkvT[m, :, own : own + n] + hxr[m, :, own : own + n].astype(F32)
+        kvo[...] = dko
+        for s in range(1, REACH + 1):
+            @pl.when(me + s < count)
+            def _(s=s, m=m):
+                back_copy(s, m).wait_recv()
+                kvo[...] += hr[s - 1, m].astype(F32)
+        low = keyval_spin(kvo[...], m, -1.0).astype(BF16)
+        dkl[ms, :] = jnp.concatenate([low, jnp.zeros((KV - HDIM, n), BF16)], axis=0).T
+    put_grad(kKV, n1T, dkl)
+    vec[5:6, hq : hq + KV] = jnp.sum(dkl[...].astype(F32), axis=0, keepdims=True)
+
+    def d1_copy(i):
+        rows = pl.ds(pl.multiple_of(i * R, R), R)
+        return send(gbuf.at[rows, pl.ds(0, D)], n2.at[rows], ts.at[i], tr.at[i], t_id)
+
+    def first_tile(i, _):
+        rows = pl.ds(pl.multiple_of(i * R, R), R)
+        gbuf[rows, 0:D] = (nt(dql[rows, :], weight(kQ)) + nt(dkl[rows, :], weight(kKV))).astype(BF16)
+        d1_copy(i).start()
+        return 0
+
+    lax.fori_loop(0, T // R, first_tile, 0)
+    step_b(kQ)
+    step_b(kKV)
+
+    y_copy.wait_recv()
+    both_bias = row(b_out) + row(b_down)
+
+    def out_tile(i, _):
+        rows = pl.ds(pl.multiple_of(i * R, R), R)
+        both = (yp[rows, :].astype(F32) + yr[rows, :].astype(F32)) + both_bias
+        layer_out[rows, :] = (x[rows, :].astype(F32) + both).astype(BF16)
+        return 0
+
+    lax.fori_loop(0, T // R, out_tile, 0)
+    d2_copy.wait_recv()
+    step_c(kQ)
+
+    def last_tile(i, _):
+        rows = pl.ds(pl.multiple_of(i * R, R), R)
+        _, xh, rstd = xhat_of(rows)
+        d1_copy(i).wait_recv()
+        dn1 = gbuf[rows, 0:D].astype(F32) + n2[rows, :].astype(F32)
+        dn2 = d2p[rows, :].astype(F32) + d2r[rows, :].astype(F32)
+        vec[0:1, :] += jnp.sum(dn1 * xh, axis=0, keepdims=True)
+        vec[1:2, :] += jnp.sum(dn1, axis=0, keepdims=True)
+        vec[2:3, :] += jnp.sum(dn2 * xh, axis=0, keepdims=True)
+        vec[3:4, :] += jnp.sum(dn2, axis=0, keepdims=True)
+        a = dn1 * g1v + dn2 * g2v
+        back = a - jnp.mean(a, axis=-1, keepdims=True) - xh * jnp.mean(a * xh, axis=-1, keepdims=True)
+        input_grad[rows, :] = (dy[rows, :].astype(F32) + rstd * back).astype(BF16)
+        return 0
+
+    lax.fori_loop(0, T // R, last_tile, 0)
+
+    flat = y * 2 + xx
+    vp[flat] = vec[...]
+    plane = [send(vp.at[flat], vp.at[flat], vs.at[j], vr.at[j], to) for j, to in enumerate((x_id, y_id, d_id))]
+    for c in plane:
+        c.start()
+    step_c(kKV)
+    for c in plane:
+        c.wait_recv()
+    vz[z] = (vp[0] + vp[1]) + (vp[2] + vp[3])
+    along = [send(vz.at[z], vz.at[z], vs.at[3 + j], vr.at[3 + j], z_ids[j]) for j in range(3)]
+    for c in along:
+        c.start()
+    step_e(kQ)
+    step_e(kKV)
+    for c in along:
+        c.wait_recv()
+    vec_out[...] = (vz[0] + vz[1]) + (vz[2] + vz[3])
+
+    for k in range(n_chunks):
+        for c in gather_z(k) + gather_col(k) + gather_far(k) + red1(k) + red2(k) + red3(k):
+            c.wait_send()
+    across(0).wait_send()
+    for s in range(1, REACH + 1):
+        @pl.when(me + s < count)
+        def _(s=s):
+            halo(s).wait_send()
+
+        @pl.when(me >= s)
+        def _(s=s):
+            across(s).wait_send()
+            for m in range(M):
+                back_copy(s, m).wait_send()
+    for m in range(M):
+        half_copy(m).wait_send()
+        own_copy(m).wait_send()
+    for i in range(T // R):
+        d1_copy(i).wait_send()
+    for c in [y_copy, d2_copy] + plane + along:
+        c.wait_send()
+
+
+def finish_kernel(
+    chunks, pieces, grads, vec, n1g, n1b, n2g, n2b, wq, bq, wkv, bkv, wo, bo, wu, bu, wd, bd
+):
+    hq, half, piece, D = wq.shape[1], wkv.shape[1], chunks[3][1], vec.shape[1]
+    for out, r in ((n1g, 0), (n1b, 1), (n2g, 2), (n2b, 3), (bo, 4), (bd, 4)):
+        out[...] = vec[r].reshape(D)
+    q0, o0 = chunks[1][0], chunks[2][0]
+    wq[...] = grads[:, q0 : q0 + hq]
+    wkv[...] = grads[:, 0:half]
+    wo[...] = grads[:, o0 : o0 + hq]
+    for c in range(pieces):
+        u0, d0 = chunks[3 + 2 * c][0], chunks[4 + 2 * c][0]
+        wu[:, c * piece : (c + 1) * piece] = grads[:, u0 : u0 + piece]
+        wd[:, c * piece : (c + 1) * piece] = grads[:, d0 : d0 + piece]
+    bq[...] = vec[5:6, 0:hq].reshape(hq)
+    bkv[...] = vec[5:6, hq : hq + half].reshape(half)
+    for r in range(bu.shape[0] // D):
+        bu[r * D : (r + 1) * D] = vec[6 + r].reshape(D)
+
+
+def fused_layer(arguments, pieces):
+    (hidden_in, positions, out_grad, g1, b1, g2, b2, w_query, b_query, w_keyval, b_keyval,
+     w_out, b_out, w_up, b_up, w_down, b_down) = arguments
+    M, n, D = hidden_in.shape
+    T = M * n
+    hq, F, half, rows = b_query.shape[0], b_up.shape[0], b_keyval.shape[0], w_query.shape[0]
+    heads, KV, piece = hq // HDIM, 2 * half, F // pieces
+    chunks = chunk_list(hq, KV, F, pieces)
+    C = chunks[-1][0] + chunks[-1][1]
+    k = len(chunks)
+    Wn = (REACH + 1) * n
+    V = pltpu.VMEM
+    S = pltpu.SemaphoreType.DMA
+    sds = jax.ShapeDtypeStruct
+    vm = pl.BlockSpec(memory_space=pltpu.VMEM)
+    mh = M * heads
+    scratch = [
+        V((4, 2, 2, rows, C), BF16), V((4, 2, 2, rows, C), BF16),
+        V((D, T), BF16), V((T, D), BF16), V((D, T), BF16), V((D, T), BF16),
+        V((hq, D), BF16), V((mh, HDIM, n), BF16), V((mh, HDIM, n), BF16), V((mh, HDIM, n), BF16),
+        V((T, hq), BF16), V((mh, 1, n), F32), V((mh, 1, n), F32),
+        V((M, Wn, KV), BF16), V((M, KV, Wn), BF16), V((M, HDIM, n), BF16),
+        V((ROT // 2, T), F32), V((ROT // 2, T), F32), V((M, 1, n), jnp.int32),
+        V((1, n), F32), V((1, n), F32), V((HDIM, n), F32),
+        V((T, F), BF16), V((pieces, T, piece), BF16),
+        V((mh, HDIM, n), F32), V((M, Wn, KV), F32), V((M, HDIM, Wn), F32), V((KV, n), F32),
+        V((REACH, M, HDIM, n), BF16), V((REACH, M, HDIM, n), BF16),
+        V((M, HDIM, Wn), BF16), V((M, HDIM, Wn), BF16), V((HDIM, n), F32),
+        V((T, D), BF16), V((T, D), BF16), V((T, D), BF16), V((T, D), BF16),
+        V((4, 2, rows, C), BF16), V((4, rows, C), BF16), V((3, rows, C), BF16),
+        V((8, D), F32), V((4, 8, D), F32), V((4, 8, D), F32),
+        V((T, hq), BF16), V((T, KV), BF16),
+        S((k, 3)), S((k, 3)), S((k, 2)), S((k, 2)), S((k, 2)), S((k, 2)),
+        S((k, 2)), S((k, 2)), S((k, 2)), S((k, 2)), S((k, 3)), S((k, 3)),
+        S((REACH,)), S((REACH,)), S((REACH, M)), S((REACH, M)), S((REACH + 1,)), S((REACH + 1,)),
+        S((2 + 2 * M,)), S((2 + 2 * M,)), S((T // 256,)), S((T // 256,)), S((6,)), S((6,)),
+    ]
+    y_out, kv_out, x_out, grads, vec = pl.pallas_call(
+        functools.partial(fused_kernel, chunks, pieces),
+        out_shape=(
+            sds((T, D), BF16), sds((M, n, KV), BF16), sds((T, D), BF16), sds((rows, C), F32), sds((8, D), F32),
+        ),
+        in_specs=[vm] * 17,
+        out_specs=(vm,) * 5,
+        scratch_shapes=scratch,
+        compiler_params=pltpu.CompilerParams(
+            collective_id=0, has_side_effects=True, vmem_limit_bytes=62 << 20
+        ),
+        name="fused_layer",
+    )(hidden_in.reshape(T, D), out_grad.reshape(T, D), positions, g1, b1, g2, b2, w_query, b_query,
+      w_keyval, b_keyval, w_out.T, b_out, w_up, b_up, w_down.T, b_down)
+    vector = sds((D,), F32)
+    out_shape = (
+        vector, vector, vector, vector,
+        sds(w_query.shape, F32), sds(b_query.shape, F32), sds(w_keyval.shape, F32), sds(b_keyval.shape, F32),
+        sds(w_out.shape[::-1], F32), vector, sds(w_up.shape, F32), sds(b_up.shape, F32), sds(w_down.shape[::-1], F32), vector,
+    )
+    outs = pl.pallas_call(
+        functools.partial(finish_kernel, chunks, pieces),
+        out_shape=out_shape,
+        in_specs=[vm] * 2,
+        out_specs=(vm,) * 14,
+        compiler_params=pltpu.CompilerParams(vmem_limit_bytes=60 << 20),
+        name="finish_layer",
+    )(grads, vec)
+    outs = [y_out.reshape(hidden_in.shape), kv_out, x_out.reshape(hidden_in.shape)] + list(outs)
+    outs[11], outs[15] = outs[11].T, outs[15].T
+    return tuple(outs)
+
+
+PIECES = 3
+
+
+def fits_fused(hidden_in, query_weight, up_weight):
+    rows, hq = query_weight.shape
+    return (
+        lax.axis_size("dp") == 16
+        and rows % 16 == 0
+        and hq % 384 == 0
+        and up_weight.shape[1] % (PIECES * 256) == 0
+        and up_weight.shape[1] >= hidden_in.shape[2]
+        and hidden_in.shape[1] % 256 == 0
+    )
+
+
+def on_device(*arguments):
+    if fits_fused(arguments[0], arguments[7], arguments[13]):
+        return fused_layer(arguments, PIECES)
+    return plain_layer(*arguments)
+
+
 def solution(mesh):
     return jax.shard_map(
         on_device,

time: 1200 us -> 196 us (0.16)
  waiting for transfers between devices: 647 us -> 0 us
  matrix products: 216 us -> 0 us
  blocking collectives: 202 us -> 0 us
  Pallas kernels: 0 us -> 190 us
  other arithmetic: 62.4 us -> 0 us
  starting transfers between devices: 32 us -> 0 us
  between operations: 18 us -> 0.68 us
    reduce_scatter x7 -> x0, waiting for transfers between devices: 549 us -> none  [the longest x1 143 us: on_device(): lax.psum_scatter(grad_down_w, 'dp', scatter_dimension=1, tiled=True)]
    dot_general x90 -> x0, matrix products: 216 us -> none  [the longest x10 34.3 us: attend_backward(): jnp.einsum('htd,kd->htk', grad_mixture, value_rows, preferred_element_typ...]
    pallas_call x0 -> x2, Pallas kernels: none -> 190 us  [the longest x1 188 us: fused_layer(): pl.pallas_call(functools.partial(fused_kernel, chunks, pieces), out_shape...]
    all_gather x5 -> x0, blocking collectives: 128 us -> none  [the longest x1 43.4 us: fetch_weights(): lax.all_gather(shard_weights[1], 'dp', axis=0, tiled=True)]
    all_gather x2 -> x0, waiting for transfers between devices: 88.8 us -> none  [the longest x1 51.7 us: fetch_weights(): lax.all_gather(shard_weights[4], 'dp', axis=1, tiled=True)]
    psum x1 -> x0, blocking collectives: 73.9 us -> none  [on_device(): lax.psum((grad_n1_gain, grad_n1_bias, grad_n2_gain, grad_n2_bias, grad_ro...]
    reduce_sum x14 -> x0, other arithmetic: 39.5 us -> none  [the longest x6 24.1 us: attend_forward(): jnp.sum(jnp.where(visible, jnp.exp(masked - new_top[..., None]), 0.0), ax...]
    ppermute x16 -> x0, starting transfers between devices: 31.1 us -> none  [shifted(): lax.ppermute(value, axis, [(source, source + steps) for source in range(i...]
  transfers between devices with their start and end apart: 26 -> 0, of which waited for: 10 -> 0; matrix products, arithmetic and copies ran while one was open for 16% -> 0% of each run, Pallas kernels for 0% -> 0%
where the time goes in v3:
time: 196 us
  Pallas kernels  190 us (97%)
  local copies, waits for them, and re-layouts  4.64 us (2%)
    pallas_call x1, Pallas kernels, fused_layer(): pl.pallas_call(functools.partial(fused_kernel, chunks, pieces), out_shape...  188 us
    unnamed x7, local copies, waits for them, and re-layouts  4.64 us

profile of v3, /device:TPU:0, one launch (start us, length us, event | category | flops | bytes accessed | tf_op | source)
XLA Modules:
  0.0 195.7 jit_solution(21851713050710481)
XLA Ops:
  0.7 188.4 %fused_layer.1 = (bf16[1024,768]{1,0:T(8,128)(2,1)}, bf16[2,512,128]{2,1,0:T(8,128)(2,1)}, bf16[1024,768]{1,0:T(8,128)(2,1)}, f32[48,3968]{1,0:T(8,128)}, f32[8,768]{1,0:T(8,128)}) custom-call(bf16[1024,768]{1,0:T(8,128)(2,1)} %bitcast.8, bf16[1024,768]{1,0:T(8,128)(2,1)} %bitcast.9, s32[2,512]{1,0:T(2,128)} %positions.1, f32[768]{0:T(1024)} %g1.1, f32[768]{0:T(1024)} %b1.1, ...), custom_call_target="tpu_custom_call" | custom-call | tf_op jit(solution)/shard_map/fused_layer/pallas_call | solution.py:1080
  189.0 2.0 %finish_layer.1 = (f32[768]{0:T(1024)}, f32[768]{0:T(1024)}, f32[768]{0:T(1024)}, f32[768]{0:T(1024)}, f32[48,384]{1,0:T(8,128)}, /*index=5*/f32[384]{0:T(512)},...) custom-call(f32[48,3968]{1,0:T(8,128)} %get-tuple-element.39.grads, ...), custom_call_target="tpu_custom_call" | custom-call | tf_op jit(solution)/shard_map/finish_layer/pallas_call | solution.py:1100
  191.1 0.0 copy-start.1
  191.1 0.0 copy-start
  191.1 2.8 %copy.37 = bf16[2,512,768]{2,1,0:T(8,128)(2,1)} copy(bf16[2,512,768]{2,1,0:T(8,128)(2,1)} %bitcast.11) | data formatting | bytes 3145728
  193.9 0.0 copy-done.1
  193.9 0.7 copy.38
  194.6 0.0 copy-done
  194.6 1.1 copy.39
Async XLA Ops:
  191.1 2.8 %copy-start.1 = (bf16[2,512,128]{2,1,0:T(8,128)(2,1)S(1)}, bf16[2,512,128]{2,1,0:T(8,128)(2,1)}, u32[]{:S(2)}) copy-start(bf16[2,512,128]{2,1,0:T(8,128)(2,1)} %get-tuple-element.73) | copy-start | bytes 786436
  191.1 3.5 %copy-start = (bf16[1024,768]{1,0:T(8,128)(2,1)S(1)}, bf16[1024,768]{1,0:T(8,128)(2,1)}, u32[]{:S(2)}) copy-start(bf16[1024,768]{1,0:T(8,128)(2,1)} %get-tuple-element.38) | copy-start | bytes 4718596

commit v4 on v3

--- a/solution.py
+++ b/solution.py
@@ -14,6 +14,45 @@
 LOW = -1e30
 F32 = jnp.float32
 BF16 = jnp.bfloat16
+
+
+SCHEDULE = {
+    "pro": (("z", 0), ("z", 1), ("col", 0), ("z", 3),),
+    "norm": (("far", 0),),
+    "cos": (("col", 1), ("z", 2),),
+    "kv": (("far", 1),),
+    "q": (("col", 3),),
+    "near0": (("z", 4),),
+    "near5": (("z", 5), ("col", 2),),
+    "halow": (("col", 4),),
+    "acw": (("z", 7),),
+    "far0": (("z", 6), ("far", 4), ("far", 3),),
+    "far1": (("z", 8), ("col", 5),),
+    "far2": (("col", 7), ("col", 6),),
+    "far3": (("far", 2),),
+    "far4": (("col", 8),),
+    "far5": (("far", 5),),
+    "bfar1": (("far", 6),),
+    "bfar2": (("b", 3), ("b", 4),),
+    "bfar3": (("far", 7), ("b", 2),),
+    "ffn1": (("c", 3), ("c", 4), ("c", 2),),
+    "bfar5": (("far", 8),),
+    "bfar6": (("b", 6), ("b", 5), ("ret", 0),),
+    "ffn2": (("c", 5), ("c", 6),),
+    "bfar7": (("e", 4),),
+    "bfar8": (("b", 7),),
+    "bfar9": (("b", 8), ("e", 2),),
+    "bfar10": (("c", 7), ("c", 8),),
+    "bnear1": (("e", 6),),
+    "bnear4": (("ret", 1),),
+    "bnear6": (("e", 5), ("e", 7),),
+    "bnear8": (("e", 3),),
+    "bnear11": (("e", 8),),
+    "t3": (("b", 0), ("b", 1),),
+    "t4": (("c", 0), ("c", 1), ("e", 0),),
+    "t5": (("e", 1),),
+}
+FEED_AT = (4, 7)
 
 
 def shifted(value, axis, steps):
@@ -368,8 +407,8 @@
     chunks, pieces,
     x, dy, positions, g1, b1, g2, b2, w_query, b_query, w_keyval, b_keyval, w_out, b_out, w_up, b_up, w_down, b_down,
     layer_out, keyval_out, input_grad, grads_out, vec_out,
-    W, G, n1T, n2, n2T, dyT, wqT, qT, doT, oT, o_nat, lse, dvec, kvwin, kvTwin, low_kv,
-    cos, sine, start, m_s, l_s, acc, gbuf, dubuf, dqT, dkv, dkvT, turned, hs, hr, hx, hxr, kvo, yp, yr, d2p, d2r,
+    W, G, n1T, n2, n2T, dyT, wqT, qT, doT, o_nat, lse, dvec, kvwin, kvTwin, low_kv,
+    cos, sine, start, m_s, l_s, acc, gbuf, dubuf, dqT, dkv, dkvT, turned, hs, hr, hx, hxr, kvo, yr, d2r,
     r1, r2, r3, vec, vp, vz, dql, dkl,
     gzs, gzr, g2s, g2r, g3s, g3r, a1s, a1r, a2s, a2r, azs, azr,
     hfs, hfr, hbs, hbr, fws, fwr, xs, xr, ts, tr, vs, vr,
@@ -378,6 +417,7 @@
     M, W_rows, KV = kvwin.shape
     n = T // M
     heads = qT.shape[0] // M
+    pairs = heads // 2
     hq = heads * HDIM
     own = REACH * n
     piece = dubuf.shape[2]
@@ -528,18 +568,39 @@
             total = total + r3[j, :, cols(k)].astype(F32)
         grads_out[:, cols(k)] = total
 
+    def act(place_name):
+        for move, k in SCHEDULE.get(place_name, ()):
+            if move == "z":
+                start1(k)
+            elif move == "col":
+                step2(k)
+            elif move == "far":
+                step3(k)
+            elif move == "b":
+                step_b(k)
+            elif move == "c":
+                step_c(k)
+            elif move == "e":
+                step_e(k)
+            else:
+                return_halo(k)
+
+    def act_in(loop_name, i):
+        for j in range(M * heads):
+            if loop_name + str(j) in SCHEDULE:
+                pl.when(i == j)(functools.partial(act, loop_name + str(j)))
+
     def place(k, block):
         c0 = chunks[k][0]
         W[z, y, xx, :, c0 : c0 + block.shape[1]] = block
 
     place(kKV, jnp.concatenate([w_keyval[...], jnp.zeros((shard_rows, HDIM), BF16)], axis=1))
-    start1(kKV)
     place(kQ, w_query[...])
-    start1(kQ)
     place(kO, w_out[...])
     for c in range(pieces):
         place(kUp[c], w_up[:, c * piece : (c + 1) * piece])
         place(kDown[c], w_down[:, c * piece : (c + 1) * piece])
+    act("pro")
 
     R = 256
     vec[...] = jnp.zeros_like(vec)
@@ -569,7 +630,7 @@
         return 0
 
     lax.fori_loop(0, T // R, norm_tile, 0)
-    step2(kKV)
+    act("norm")
     h = ROT // 2
     index = lax.broadcasted_iota(jnp.int32, (h, 1), 0)
     inverse = jnp.zeros((h, 1), F32)
@@ -591,8 +652,7 @@
         size = ref.shape[0]
         return jnp.broadcast_to(ref[...].reshape(1, size), (8, size)).T[:, 0:1]
 
-    step3(kKV)
-    step2(kQ)
+    act("cos")
     arrived(kKV)
     wkvT = weight(kKV).T[0:HDIM]
     bkv = column(b_keyval)
@@ -619,14 +679,13 @@
             halo(s).start()
     across(0).start()
 
-    start1(kO)
-    start1(kUp[0])
-    step3(kQ)
+    act("kv")
     across(0).wait_recv()
     for m in range(M):
         natural = kvTwin[m, :, own : own + n].T
         kvwin[m, own : own + n, :] = natural
         keyval_out[m] = natural
+    act("own")
     arrived(kQ)
     wqT[...] = weight(kQ).T
     bq = column(b_query)
@@ -635,6 +694,8 @@
         lin = nn(wqT[...], n1T[:, ms]) + bq
         spun = spin(lin.reshape(heads, HDIM, n), cos[:, ms], sine[:, ms]) * scale
         qT[m * heads : (m + 1) * heads] = spun.astype(BF16)
+    act("q")
+
     near, far = near_tiles(n, n // 2), far_tiles(n, n // 2)
     tops, totals, sums = lse, dvec, dqT
 
@@ -649,57 +710,66 @@
     def padded_query(i):
         return jnp.concatenate([qT[i], jnp.zeros((KV - HDIM, n), BF16)], axis=0)
 
+    def forward_tiles(i, tiles):
+        m = i // pairs
+        first = start[m]
+        queries = [padded_query(2 * i + t) for t in range(2)]
+
+        def scores(t, tile):
+            w0, kn, q0, qn, causal = tile
+            qs = slice(q0, q0 + qn)
+            sc = nn(kvwin[m, w0 : w0 + kn, :], queries[t][:, qs])
+            return jnp.where(visible(w0, kn, q0, qn, first[:, qs], causal), sc, LOW)
+
+        def take(t, tile, sc):
+            w0, kn, q0, qn, _ = tile
+            qs = slice(q0, q0 + qn)
+            before = m_s[t, :, qs]
+            top = jnp.maximum(before, jnp.max(sc, axis=0, keepdims=True))
+            p = jnp.exp(sc - top)
+            shrink = jnp.exp(before - top)
+            l_s[t, :, qs] = l_s[t, :, qs] * shrink + jnp.sum(p, axis=0, keepdims=True)
+            m_s[t, :, qs] = top
+            acc[t, :, qs] = acc[t, :, qs] * shrink + nn(kvTwin[m, HDIM:KV, w0 : w0 + kn], p.astype(BF16))
+
+        ready = [scores(t, tiles[0]) for t in range(2)]
+        for at_tile, tile in enumerate(tiles):
+            ahead = None
+            if at_tile + 1 < len(tiles):
+                ahead = [scores(t, tiles[at_tile + 1]) for t in range(2)]
+            for t in range(2):
+                take(t, tile, ready[t])
+            ready = ahead
+
     def forward_near(i, _):
-        m = i // heads
-        q = padded_query(i)
-        first = start[m]
         m_s[...] = jnp.full_like(m_s, LOW)
         l_s[...] = jnp.zeros_like(l_s)
         acc[...] = jnp.zeros_like(acc)
-        forward_tiles(m, q, first, near)
-        tops[i], totals[i], sums[i] = m_s[...], l_s[...], acc[...]
+        forward_tiles(i, near)
+        both = pl.ds(2 * i, 2)
+        tops[both], totals[both], sums[both] = m_s[...], l_s[...], acc[...]
         return 0
 
-    def forward_tiles(m, q, first, tiles):
-        for w0, kn, q0, qn, causal in tiles:
-            qs = slice(q0, q0 + qn)
-            sc = nn(kvwin[m, w0 : w0 + kn, :], q[:, qs])
-            sc = jnp.where(visible(w0, kn, q0, qn, first[:, qs], causal), sc, LOW)
-            before = m_s[:, qs]
-            top = jnp.maximum(before, jnp.max(sc, axis=0, keepdims=True))
-            p = jnp.exp(sc - top)
-            shrink = jnp.exp(before - top)
-            l_s[:, qs] = l_s[:, qs] * shrink + jnp.sum(p, axis=0, keepdims=True)
-            m_s[:, qs] = top
-            acc[:, qs] = acc[:, qs] * shrink + nn(kvTwin[m, HDIM:KV, w0 : w0 + kn], p.astype(BF16))
-
     def forward_far(i, _):
-        m = i // heads
-        q = padded_query(i)
-        m_s[...], l_s[...], acc[...] = tops[i], totals[i], sums[i]
-        forward_tiles(m, q, start[m], far)
+        m = i // pairs
+        both = pl.ds(2 * i, 2)
+        m_s[...], l_s[...], acc[...] = tops[both], totals[both], sums[both]
+        forward_tiles(i, far)
         o = acc[...] / l_s[...]
-        oT[i] = o.astype(BF16)
-        sums[i] = o
-        lse[i] = m_s[...] + jnp.log(l_s[...])
-        scheduled(far_plan, i)
+        sums[both] = o
+        lse[both] = m_s[...] + jnp.log(l_s[...])
+        rows = pl.ds(pl.multiple_of(m * n, n), n)
+        lanes = pl.ds(pl.multiple_of((i % pairs) * 2 * HDIM, 2 * HDIM), 2 * HDIM)
+        o_nat[rows, lanes] = o.astype(BF16).reshape(2 * HDIM, n).T
+        act_in("far", i)
         return 0
-
-    def scheduled(plan, i):
-        for j, act in plan.items():
-            pl.when(i == j)(lambda act=act: (act(), None)[1])
 
     def near_step(i, _):
         forward_near(i, 0)
-        scheduled(near_plan, i)
+        act_in("near", i)
         return 0
 
-    near_plan = {
-        0: lambda: step2(kO),
-        4: lambda: start1(kDown[0]),
-        8: lambda: (step2(kUp[0]), step3(kO)),
-    }
-    lax.fori_loop(0, M * heads, near_step, 0)
+    lax.fori_loop(0, M * pairs, near_step, 0)
     for s in range(1, REACH + 1):
         @pl.when(me >= s)
         def _(s=s):
@@ -710,8 +780,7 @@
         def _(s=s):
             kvTwin[:, :, block(s)] = jnp.zeros((M, KV, n), BF16)
 
-    step2(kDown[0])
-    start1(kUp[1])
+    act("halow")
     for s in range(1, REACH + 1):
         @pl.when(me >= s)
         def _(s=s):
@@ -720,14 +789,8 @@
         for m in range(M):
             kvwin[m, block(s), :] = kvTwin[m, :, block(s)].T
 
-    far_plan = {
-        0: lambda: (step3(kUp[0]), start1(kDown[1])),
-        2: lambda: step3(kDown[0]),
-        4: lambda: (step2(kUp[1]), start1(kUp[2])),
-        7: lambda: (step2(kDown[1]), start1(kDown[2])),
-        9: lambda: step3(kUp[1]),
-    }
-    lax.fori_loop(0, M * heads, forward_far, 0)
+    act("acw")
+    lax.fori_loop(0, M * pairs, forward_far, 0)
 
     arrived(kO)
     wo = weight(kO).T
@@ -740,8 +803,6 @@
         return 0
 
     lax.fori_loop(0, M * heads, mix_dots, 0)
-    for m in range(M):
-        o_nat[m * n : (m + 1) * n, :] = oT[m * heads : (m + 1) * heads].reshape(hq, n).T
 
     def put_grad(k, leftT, right):
         c0, cn = chunks[k]
@@ -756,8 +817,7 @@
         step_a(k)
 
     put_grad(kO, dyT, o_nat)
-    step3(kDown[1])
-    step2(kUp[2])
+    act("mix")
 
     def feed_forward(c):
         ku, kd = kUp[c], kDown[c]
@@ -787,12 +847,12 @@
         for c in range(pieces):
             total = total + nt(gbuf[rows, c * piece : (c + 1) * piece], weight(kDown[c]))
             back = back + nt(dubuf[c, rows, :], weight(kUp[c]))
-        yp[rows, :] = total.astype(BF16)
-        d2p[rows, :] = back.astype(BF16)
+        layer_out[rows, :] = total.astype(BF16)
+        input_grad[rows, :] = back.astype(BF16)
         return 0
 
-    y_copy = send(yp, yr, xs.at[0], xr.at[0], t_id)
-    d2_copy = send(d2p, d2r, xs.at[1], xr.at[1], t_id)
+    y_copy = send(layer_out, yr, xs.at[0], xr.at[0], t_id)
+    d2_copy = send(input_grad, d2r, xs.at[1], xr.at[1], t_id)
 
     def branches():
         lax.fori_loop(0, T // R, branch_tile, 0)
@@ -809,41 +869,67 @@
                 done += width
 
     feed_forward(0)
-    step2(kDown[2])
+    act("ffn0")
 
     dkv[...] = jnp.zeros_like(dkv)
 
     def backward_tiles(i, tiles):
         m = i // heads
         zero = jnp.zeros((HDIM, n), BF16)
-        q = jnp.concatenate([qT[i], zero], axis=0)
-        do = jnp.concatenate([zero, doT[i]], axis=0)
-        qdo = jnp.concatenate([qT[i], doT[i]], axis=0).T
+        query = jnp.concatenate([qT[i], zero], axis=0)
+        cotangent = jnp.concatenate([zero, doT[i]], axis=0)
+        natural = jnp.concatenate([qT[i], doT[i]], axis=0).T
         first, ls, dots = start[m], lse[i], dvec[i]
-        for w0, kn, q0, qn, causal in tiles:
+        step = n // 2
+        pieces_of = [(w0 + a, step, q0, qn, c) for w0, kn, q0, qn, c in tiles for a in range(0, kn, step)]
+
+        def products(tile):
+            w0, kn, q0, qn, causal = tile
             qs = slice(q0, q0 + qn)
             rows = kvwin[m, w0 : w0 + kn, :]
-            sc = nn(rows, q[:, qs])
+            sc = nn(rows, query[:, qs])
             sc = jnp.where(visible(w0, kn, q0, qn, first[:, qs], causal), sc, LOW)
+            return sc, nn(rows, cotangent[:, qs])
+
+        ready = products(pieces_of[0])
+        for at_tile, tile in enumerate(pieces_of):
+            ahead = products(pieces_of[at_tile + 1]) if at_tile + 1 < len(pieces_of) else None
+            w0, kn, q0, qn, _ = tile
+            qs = slice(q0, q0 + qn)
+            sc, dp = ready
             p = jnp.exp(sc - ls[:, qs])
-            dp = nn(rows, do[:, qs])
             ds = (p * (dp - dots[:, qs])).astype(BF16)
-            for_k = nn(ds, qdo[qs])
-            for_v = nn(p.astype(BF16), qdo[qs])
+            for_k = nn(ds, natural[qs])
+            for_v = nn(p.astype(BF16), natural[qs])
             lane = lax.broadcasted_iota(jnp.int32, for_k.shape, 1)
             dkv[m, w0 : w0 + kn, :] += jnp.where(lane < HDIM, for_k, for_v)
             dqT[i, :, qs] += nn(kvTwin[m, 0:HDIM, w0 : w0 + kn], ds)
+            ready = ahead
 
     def backward_far(i, _):
-        scheduled(feed_plan, i)
+        @pl.when(i == FEED_AT[0])
+        def _():
+            feed_forward(1)
+            act("ffn1")
+
+        @pl.when(i == FEED_AT[1])
+        def _():
+            feed_forward(2)
+            branches()
+            act("ffn2")
+
         dqT[i] = jnp.zeros((HDIM, n), F32)
         backward_tiles(i, far)
-        scheduled(back_far_plan, i)
+        for m in range(M):
+            pl.when(i == (m + 1) * heads - 1)(functools.partial(give_half, m))
+        act_in("bfar", i)
         return 0
 
     def backward_near(i, _):
         backward_tiles(i, near)
-        scheduled(back_near_plan, i)
+        for m in range(M):
+            pl.when(i == (m + 1) * heads - 1)(functools.partial(give_own, m))
+        act_in("bnear", i)
         return 0
 
     def back_copy(s, m):
@@ -885,30 +971,6 @@
         split(m, REACH)
         own_copy(m).start()
 
-    feed_plan = {
-        3: lambda: feed_forward(1),
-        6: lambda: (feed_forward(2), branches()),
-    }
-    back_far_plan = {
-        0: lambda: (step3(kUp[2]), step_b(kO)),
-        1: lambda: (step3(kDown[2]), step_b(kUp[0])),
-        2: lambda: (step_b(kDown[0]), step_c(kO)),
-        3: lambda: (step_c(kUp[0]), step_c(kDown[0])),
-        4: lambda: step_e(kO),
-        5: lambda: (give_half(0), step_b(kUp[1]), step_e(kUp[0])),
-        6: lambda: (step_b(kDown[1]), step_c(kUp[1]), step_e(kDown[0])),
-        7: lambda: (return_halo(0), step_c(kDown[1])),
-        8: lambda: (step_b(kUp[2]), step_e(kUp[1])),
-        9: lambda: step_b(kDown[2]),
-        10: lambda: (step_c(kUp[2]), step_e(kDown[1])),
-        11: lambda: (give_half(1), step_c(kDown[2])),
-    }
-    back_near_plan = {
-        2: lambda: return_halo(1),
-        5: lambda: (give_own(0), step_e(kUp[2])),
-        8: lambda: step_e(kDown[2]),
-        11: lambda: give_own(1),
-    }
     lax.fori_loop(0, M * heads, backward_far, 0)
     lax.fori_loop(0, M * heads, backward_near, 0)
 
@@ -919,6 +981,7 @@
         dql[ms, :] = low.reshape(hq, n).T
     put_grad(kQ, n1T, dql)
     vec[5:6, 0:hq] = jnp.sum(dql[...].astype(F32), axis=0, keepdims=True)
+    act("t0")
 
     for m in range(M):
         ms = slice(m * n, (m + 1) * n)
@@ -934,6 +997,7 @@
         dkl[ms, :] = jnp.concatenate([low, jnp.zeros((KV - HDIM, n), BF16)], axis=0).T
     put_grad(kKV, n1T, dkl)
     vec[5:6, hq : hq + KV] = jnp.sum(dkl[...].astype(F32), axis=0, keepdims=True)
+    act("t1")
 
     def d1_copy(i):
         rows = pl.ds(pl.multiple_of(i * R, R), R)
@@ -946,28 +1010,27 @@
         return 0
 
     lax.fori_loop(0, T // R, first_tile, 0)
-    step_b(kQ)
-    step_b(kKV)
-
-    y_copy.wait_recv()
+    act("t2")
+
+    y_copy.wait()
     both_bias = row(b_out) + row(b_down)
 
     def out_tile(i, _):
         rows = pl.ds(pl.multiple_of(i * R, R), R)
-        both = (yp[rows, :].astype(F32) + yr[rows, :].astype(F32)) + both_bias
+        both = (layer_out[rows, :].astype(F32) + yr[rows, :].astype(F32)) + both_bias
         layer_out[rows, :] = (x[rows, :].astype(F32) + both).astype(BF16)
         return 0
 
     lax.fori_loop(0, T // R, out_tile, 0)
-    d2_copy.wait_recv()
-    step_c(kQ)
+    act("t3")
+    d2_copy.wait()
 
     def last_tile(i, _):
         rows = pl.ds(pl.multiple_of(i * R, R), R)
         _, xh, rstd = xhat_of(rows)
         d1_copy(i).wait_recv()
         dn1 = gbuf[rows, 0:D].astype(F32) + n2[rows, :].astype(F32)
-        dn2 = d2p[rows, :].astype(F32) + d2r[rows, :].astype(F32)
+        dn2 = input_grad[rows, :].astype(F32) + d2r[rows, :].astype(F32)
         vec[0:1, :] += jnp.sum(dn1 * xh, axis=0, keepdims=True)
         vec[1:2, :] += jnp.sum(dn1, axis=0, keepdims=True)
         vec[2:3, :] += jnp.sum(dn2 * xh, axis=0, keepdims=True)
@@ -984,17 +1047,17 @@
     plane = [send(vp.at[flat], vp.at[flat], vs.at[j], vr.at[j], to) for j, to in enumerate((x_id, y_id, d_id))]
     for c in plane:
         c.start()
-    step_c(kKV)
+    act("t4")
     for c in plane:
         c.wait_recv()
     vz[z] = (vp[0] + vp[1]) + (vp[2] + vp[3])
     along = [send(vz.at[z], vz.at[z], vs.at[3 + j], vr.at[3 + j], z_ids[j]) for j in range(3)]
     for c in along:
         c.start()
-    step_e(kQ)
-    step_e(kKV)
+    act("t5")
     for c in along:
         c.wait_recv()
+    act("t6")
     vec_out[...] = (vz[0] + vz[1]) + (vz[2] + vz[3])
 
     for k in range(n_chunks):
@@ -1016,7 +1079,7 @@
         own_copy(m).wait_send()
     for i in range(T // R):
         d1_copy(i).wait_send()
-    for c in [y_copy, d2_copy] + plane + along:
+    for c in plane + along:
         c.wait_send()
 
 
@@ -1059,16 +1122,16 @@
     scratch = [
         V((4, 2, 2, rows, C), BF16), V((4, 2, 2, rows, C), BF16),
         V((D, T), BF16), V((T, D), BF16), V((D, T), BF16), V((D, T), BF16),
-        V((hq, D), BF16), V((mh, HDIM, n), BF16), V((mh, HDIM, n), BF16), V((mh, HDIM, n), BF16),
+        V((hq, D), BF16), V((mh, HDIM, n), BF16), V((mh, HDIM, n), BF16),
         V((T, hq), BF16), V((mh, 1, n), F32), V((mh, 1, n), F32),
         V((M, Wn, KV), BF16), V((M, KV, Wn), BF16), V((M, HDIM, n), BF16),
         V((ROT // 2, T), F32), V((ROT // 2, T), F32), V((M, 1, n), jnp.int32),
-        V((1, n), F32), V((1, n), F32), V((HDIM, n), F32),
+        V((2, 1, n), F32), V((2, 1, n), F32), V((2, HDIM, n), F32),
         V((T, F), BF16), V((pieces, T, piece), BF16),
         V((mh, HDIM, n), F32), V((M, Wn, KV), F32), V((M, HDIM, Wn), F32), V((KV, n), F32),
         V((REACH, M, HDIM, n), BF16), V((REACH, M, HDIM, n), BF16),
         V((M, HDIM, Wn), BF16), V((M, HDIM, Wn), BF16), V((HDIM, n), F32),
-        V((T, D), BF16), V((T, D), BF16), V((T, D), BF16), V((T, D), BF16),
+        V((T, D), BF16), V((T, D), BF16),
         V((4, 2, rows, C), BF16), V((4, rows, C), BF16), V((3, rows, C), BF16),
         V((8, D), F32), V((4, 8, D), F32), V((4, 8, D), F32),
         V((T, hq), BF16), V((T, KV), BF16),

time: 196 us -> 173 us (0.88)
  Pallas kernels: 190 us -> 167 us
    pallas_call x1, Pallas kernels: 188 us -> 165 us  [fused_layer(): pl.pallas_call(functools.partial(fused_kernel, chunks, pieces), out_shape...]
where the time goes in v4:
time: 173 us; the launch traced here: 172 us
  Pallas kernels  167 us (97%)
  local copies, waits for them, and re-layouts  4.64 us (3%)
    pallas_call x1, Pallas kernels, fused_layer(): pl.pallas_call(functools.partial(fused_kernel, chunks, pieces), out_shape...  165 us
    unnamed x7, local copies, waits for them, and re-layouts  4.64 us

profile of v4, /device:TPU:0, one launch (start us, length us, event | category | flops | bytes accessed | tf_op | source)
XLA Modules:
  0.0 172.5 jit_solution(3631219538157878018)
XLA Ops:
  0.7 165.1 %fused_layer.1 = (bf16[1024,768]{1,0:T(8,128)(2,1)}, bf16[2,512,128]{2,1,0:T(8,128)(2,1)}, bf16[1024,768]{1,0:T(8,128)(2,1)}, f32[48,3968]{1,0:T(8,128)}, f32[8,768]{1,0:T(8,128)}) custom-call(bf16[1024,768]{1,0:T(8,128)(2,1)} %bitcast.8, bf16[1024,768]{1,0:T(8,128)(2,1)} %bitcast.9, s32[2,512]{1,0:T(2,128)} %positions.1, f32[768]{0:T(1024)} %g1.1, f32[768]{0:T(1024)} %b1.1, ...), custom_call_target="tpu_custom_call" | custom-call | tf_op jit(solution)/shard_map/fused_layer/pallas_call | solution.py:1143
  165.8 2.0 %finish_layer.1 = (f32[768]{0:T(1024)}, f32[768]{0:T(1024)}, f32[768]{0:T(1024)}, f32[768]{0:T(1024)}, f32[48,384]{1,0:T(8,128)}, /*index=5*/f32[384]{0:T(512)},...) custom-call(f32[48,3968]{1,0:T(8,128)} %get-tuple-element.39.grads, ...), custom_call_target="tpu_custom_call" | custom-call | tf_op jit(solution)/shard_map/finish_layer/pallas_call | solution.py:1163
  167.8 0.0 copy-start.1
  167.8 0.0 copy-start
  167.8 2.8 %copy.37 = bf16[2,512,768]{2,1,0:T(8,128)(2,1)} copy(bf16[2,512,768]{2,1,0:T(8,128)(2,1)} %bitcast.11) | data formatting | bytes 3145728
  170.6 0.0 copy-done.1
  170.6 0.7 copy.38
  171.3 0.0 copy-done
  171.3 1.1 copy.39
Async XLA Ops:
  167.8 2.8 %copy-start.1 = (bf16[2,512,128]{2,1,0:T(8,128)(2,1)S(1)}, bf16[2,512,128]{2,1,0:T(8,128)(2,1)}, u32[]{:S(2)}) copy-start(bf16[2,512,128]{2,1,0:T(8,128)(2,1)} %get-tuple-element.73) | copy-start | bytes 786436
  167.8 3.5 %copy-start = (bf16[1024,768]{1,0:T(8,128)(2,1)S(1)}, bf16[1024,768]{1,0:T(8,128)(2,1)}, u32[]{:S(2)}) copy-start(bf16[1024,768]{1,0:T(8,128)(2,1)} %get-tuple-element.38) | copy-start | bytes 4718596

commit v5 on v4

--- a/solution.py
+++ b/solution.py
@@ -45,9 +45,10 @@
     "bfar10": (("c", 7), ("c", 8),),
     "bnear1": (("e", 6),),
     "bnear4": (("ret", 1),),
-    "bnear6": (("e", 5), ("e", 7),),
+    "bnear6": (("e", 7),),
     "bnear8": (("e", 3),),
     "bnear11": (("e", 8),),
+    "t0": (("e", 5),),
     "t3": (("b", 0), ("b", 1),),
     "t4": (("c", 0), ("c", 1), ("e", 0),),
     "t5": (("e", 1),),
@@ -405,8 +406,9 @@
 
 def fused_kernel(
     chunks, pieces,
-    x, dy, positions, g1, b1, g2, b2, w_query, b_query, w_keyval, b_keyval, w_out, b_out, w_up, b_up, w_down, b_down,
-    layer_out, keyval_out, input_grad, grads_out, vec_out,
+    x_in, dy_in, positions, g1, b1, g2, b2, w_query, b_query, w_keyval, b_keyval, w_out, b_out, w_up, b_up, w_down, b_down,
+    layer_hbm, keyval_hbm, grad_hbm, grads_out, vec_out,
+    x, dy, layer_out, keyval_out, input_grad, in_sem, out_sem,
     W, G, n1T, n2, n2T, dyT, wqT, qT, doT, o_nat, lse, dvec, kvwin, kvTwin, low_kv,
     cos, sine, start, m_s, l_s, acc, gbuf, dubuf, dqT, dkv, dkvT, turned, hs, hr, hx, hxr, kvo, yr, d2r,
     r1, r2, r3, vec, vp, vz, dql, dkl,
@@ -446,6 +448,10 @@
             src_ref=src, dst_ref=dst, send_sem=ss, recv_sem=rs, device_id=to, device_id_type=MESH
         )
 
+    loads = [pltpu.make_async_copy(a, b, in_sem.at[j]) for j, (a, b) in enumerate(((x_in, x), (dy_in, dy)))]
+    for c in loads:
+        c.start()
+
     bar = pltpu.get_barrier_semaphore()
     peers = z_ids + [y_id, x_id, d_id, t_id]
     peers += [{"dp": (me + s) % count} for s in range(1, REACH + 1)]
@@ -629,6 +635,8 @@
         vec[4:5, :] += jnp.sum(d.astype(F32), axis=0, keepdims=True)
         return 0
 
+    for c in loads:
+        c.wait()
     lax.fori_loop(0, T // R, norm_tile, 0)
     act("norm")
     h = ROT // 2
@@ -685,6 +693,11 @@
         natural = kvTwin[m, :, own : own + n].T
         kvwin[m, own : own + n, :] = natural
         keyval_out[m] = natural
+    stores = [
+        pltpu.make_async_copy(a, b, out_sem.at[j])
+        for j, (a, b) in enumerate(((keyval_out, keyval_hbm), (layer_out, layer_hbm)))
+    ]
+    stores[0].start()
     act("own")
     arrived(kQ)
     wqT[...] = weight(kQ).T
@@ -1022,8 +1035,13 @@
         return 0
 
     lax.fori_loop(0, T // R, out_tile, 0)
+    stores[1].start()
     act("t3")
     d2_copy.wait()
+
+    def grad_store(i):
+        rows = pl.ds(pl.multiple_of(i * R, R), R)
+        return pltpu.make_async_copy(input_grad.at[rows], grad_hbm.at[rows], out_sem.at[2 + i])
 
     def last_tile(i, _):
         rows = pl.ds(pl.multiple_of(i * R, R), R)
@@ -1038,6 +1056,7 @@
         a = dn1 * g1v + dn2 * g2v
         back = a - jnp.mean(a, axis=-1, keepdims=True) - xh * jnp.mean(a * xh, axis=-1, keepdims=True)
         input_grad[rows, :] = (dy[rows, :].astype(F32) + rstd * back).astype(BF16)
+        grad_store(i).start()
         return 0
 
     lax.fori_loop(0, T // R, last_tile, 0)
@@ -1079,13 +1098,35 @@
         own_copy(m).wait_send()
     for i in range(T // R):
         d1_copy(i).wait_send()
+        grad_store(i).wait()
+    for c in stores:
+        c.wait()
     for c in plane + along:
         c.wait_send()
 
 
 def finish_kernel(
-    chunks, pieces, grads, vec, n1g, n1b, n2g, n2b, wq, bq, wkv, bkv, wo, bo, wu, bu, wd, bd
+    chunks, pieces,
+    y_in, kv_in, x_in, grads, vec,
+    y_out, kv_out, x_out, n1g, n1b, n2g, n2b, wq, bq, wkv, bkv, wo, bo, wu, bu, wd, bd,
+    y_buf, kv_buf, x_buf, in_sem, out_sem,
 ):
+    loads, stores = [], []
+    half_rows = pl.ds(0, y_in.shape[0] // 2), pl.ds(y_in.shape[0] // 2, y_in.shape[0] // 2)
+    for a, buf, b in (
+        (y_in.at[half_rows[0]], y_buf.at[half_rows[0]], y_out.at[half_rows[0]]),
+        (y_in.at[half_rows[1]], y_buf.at[half_rows[1]], y_out.at[half_rows[1]]),
+        (x_in.at[half_rows[0]], x_buf.at[half_rows[0]], x_out.at[half_rows[0]]),
+        (x_in.at[half_rows[1]], x_buf.at[half_rows[1]], x_out.at[half_rows[1]]),
+        (kv_in, kv_buf, kv_out),
+    ):
+        loads.append(pltpu.make_async_copy(a, buf, in_sem.at[len(loads)]))
+        stores.append(pltpu.make_async_copy(buf, b, out_sem.at[len(stores)]))
+    for c in loads:
+        c.start()
+    for load, store in zip(loads, stores):
+        load.wait()
+        store.start()
     hq, half, piece, D = wq.shape[1], wkv.shape[1], chunks[3][1], vec.shape[1]
     for out, r in ((n1g, 0), (n1b, 1), (n2g, 2), (n2b, 3), (bo, 4), (bd, 4)):
         out[...] = vec[r].reshape(D)
@@ -1101,6 +1142,8 @@
     bkv[...] = vec[5:6, hq : hq + half].reshape(half)
     for r in range(bu.shape[0] // D):
         bu[r * D : (r + 1) * D] = vec[6 + r].reshape(D)
+    for c in stores:
+        c.wait()
 
 
 def fused_layer(arguments, pieces):
@@ -1119,7 +1162,10 @@
     sds = jax.ShapeDtypeStruct
     vm = pl.BlockSpec(memory_space=pltpu.VMEM)
     mh = M * heads
+    hbm = pl.BlockSpec(memory_space=pl.ANY)
     scratch = [
+        V((T, D), BF16), V((T, D), BF16), V((T, D), BF16), V((M, n, KV), BF16), V((T, D), BF16),
+        S((2,)), S((2 + T // 256,)),
         V((4, 2, 2, rows, C), BF16), V((4, 2, 2, rows, C), BF16),
         V((D, T), BF16), V((T, D), BF16), V((D, T), BF16), V((D, T), BF16),
         V((hq, D), BF16), V((mh, HDIM, n), BF16), V((mh, HDIM, n), BF16),
@@ -1145,8 +1191,8 @@
         out_shape=(
             sds((T, D), BF16), sds((M, n, KV), BF16), sds((T, D), BF16), sds((rows, C), F32), sds((8, D), F32),
         ),
-        in_specs=[vm] * 17,
-        out_specs=(vm,) * 5,
+        in_specs=[hbm] * 2 + [vm] * 15,
+        out_specs=(hbm,) * 3 + (vm,) * 2,
         scratch_shapes=scratch,
         compiler_params=pltpu.CompilerParams(
             collective_id=0, has_side_effects=True, vmem_limit_bytes=62 << 20
@@ -1156,19 +1202,21 @@
       w_keyval, b_keyval, w_out.T, b_out, w_up, b_up, w_down.T, b_down)
     vector = sds((D,), F32)
     out_shape = (
-        vector, vector, vector, vector,
+        sds((T, D), BF16), sds((M, n, KV), BF16), sds((T, D), BF16), vector, vector, vector, vector,
         sds(w_query.shape, F32), sds(b_query.shape, F32), sds(w_keyval.shape, F32), sds(b_keyval.shape, F32),
         sds(w_out.shape[::-1], F32), vector, sds(w_up.shape, F32), sds(b_up.shape, F32), sds(w_down.shape[::-1], F32), vector,
     )
     outs = pl.pallas_call(
         functools.partial(finish_kernel, chunks, pieces),
         out_shape=out_shape,
-        in_specs=[vm] * 2,
-        out_specs=(vm,) * 14,
+        in_specs=[hbm] * 3 + [vm] * 2,
+        out_specs=(hbm,) * 3 + (vm,) * 14,
+        scratch_shapes=[V((T, D), BF16), V((M, n, KV), BF16), V((T, D), BF16), S((5,)), S((5,))],
         compiler_params=pltpu.CompilerParams(vmem_limit_bytes=60 << 20),
         name="finish_layer",
-    )(grads, vec)
-    outs = [y_out.reshape(hidden_in.shape), kv_out, x_out.reshape(hidden_in.shape)] + list(outs)
+    )(y_out, kv_out, x_out, grads, vec)
+    outs = list(outs)
+    outs[0], outs[2] = outs[0].reshape(hidden_in.shape), outs[2].reshape(hidden_in.shape)
     outs[11], outs[15] = outs[11].T, outs[15].T
     return tuple(outs)
 

time: 173 us -> 169 us (0.977)
  local copies, waits for them, and re-layouts: 4.64 us -> 0 us
    unnamed x7 -> x0, local copies, waits for them, and re-layouts: 4.64 us -> none
    pallas_call x1, Pallas kernels: 2.05 us -> 5 us  [fused_layer(): pl.pallas_call(functools.partial(finish_kernel, chunks, pieces), out_shap...]
    pallas_call x1, Pallas kernels: 165 us -> 163 us  [fused_layer(): pl.pallas_call(functools.partial(fused_kernel, chunks, pieces), out_shape...]
where the time goes in v5:
time: 169 us
  Pallas kernels  168 us (99%)
    pallas_call x1, Pallas kernels, fused_layer(): pl.pallas_call(functools.partial(fused_kernel, chunks, pieces), out_shape...  163 us
    pallas_call x1, Pallas kernels, fused_layer(): pl.pallas_call(functools.partial(finish_kernel, chunks, pieces), out_shap...  5 us

profile of v5, /device:TPU:0, one launch (start us, length us, event | category | flops | bytes accessed | tf_op | source)
XLA Modules:
  0.0 168.9 jit_solution(14922993195863018847)
XLA Ops:
  0.7 163.0 %fused_layer.1 = (bf16[1024,768]{1,0:T(8,128)(2,1)}, bf16[2,512,128]{2,1,0:T(8,128)(2,1)}, bf16[1024,768]{1,0:T(8,128)(2,1)}, f32[48,3968]{1,0:T(8,128)}, f32[8,768]{1,0:T(8,128)}) custom-call(bf16[1024,768]{1,0:T(8,128)(2,1)} %bitcast.8, bf16[1024,768]{1,0:T(8,128)(2,1)} %bitcast.9, s32[2,512]{1,0:T(2,128)} %positions.1, f32[768]{0:T(1024)} %g1.1, f32[768]{0:T(1024)} %b1.1, ...), custom_call_target="tpu_custom_call" | custom-call | tf_op jit(solution)/shard_map/fused_layer/pallas_call | solution.py:1189
  163.7 5.0 %finish_layer.1 = (bf16[1024,768]{1,0:T(8,128)(2,1)}, bf16[2,512,128]{2,1,0:T(8,128)(2,1)}, bf16[1024,768]{1,0:T(8,128)(2,1)}, f32[768]{0:T(1024)}, f32[768]{0:T...) custom-call(bf16[1024,768]{1,0:T(8,128)(2,1)} %get-tuple-element.39., ...), custom_call_target="tpu_custom_call" | custom-call | tf_op jit(solution)/shard_map/finish_layer/pallas_call | solution.py:1209

commit v6 on v5

--- a/solution.py
+++ b/solution.py
@@ -17,43 +17,42 @@
 
 
 SCHEDULE = {
-    "pro": (("z", 0), ("z", 1), ("col", 0), ("z", 3),),
-    "norm": (("far", 0),),
-    "cos": (("col", 1), ("z", 2),),
-    "kv": (("far", 1),),
-    "q": (("col", 3),),
-    "near0": (("z", 4),),
-    "near5": (("z", 5), ("col", 2),),
-    "halow": (("col", 4),),
-    "acw": (("z", 7),),
-    "far0": (("z", 6), ("far", 4), ("far", 3),),
-    "far1": (("z", 8), ("col", 5),),
-    "far2": (("col", 7), ("col", 6),),
-    "far3": (("far", 2),),
-    "far4": (("col", 8),),
-    "far5": (("far", 5),),
-    "bfar1": (("far", 6),),
-    "bfar2": (("b", 3), ("b", 4),),
-    "bfar3": (("far", 7), ("b", 2),),
-    "ffn1": (("c", 3), ("c", 4), ("c", 2),),
-    "bfar5": (("far", 8),),
-    "bfar6": (("b", 6), ("b", 5), ("ret", 0),),
-    "ffn2": (("c", 5), ("c", 6),),
-    "bfar7": (("e", 4),),
-    "bfar8": (("b", 7),),
-    "bfar9": (("b", 8), ("e", 2),),
-    "bfar10": (("c", 7), ("c", 8),),
-    "bnear1": (("e", 6),),
-    "bnear4": (("ret", 1),),
-    "bnear6": (("e", 7),),
-    "bnear8": (("e", 3),),
-    "bnear11": (("e", 8),),
-    "t0": (("e", 5),),
-    "t3": (("b", 0), ("b", 1),),
-    "t4": (("c", 0), ("c", 1), ("e", 0),),
-    "t5": (("e", 1),),
+    "pro": (("z", 0), ("z", 2), ("col", 2), ("z", 1), ("col", 0), ("z", 3),),
+    "norm": (("z", 5), ("col", 1), ("far", 0),),
+    "cos": (("z", 4), ("far", 1), ("col", 3),),
+    "kv": (("col", 4), ("far", 3),),
+    "own": (("far", 2),),
+    "near2": (("z", 6),),
+    "near5": (("col", 5),),
+    "halow": (("z", 7),),
+    "acw": (("far", 4), ("z", 9),),
+    "far0": (("col", 6),),
+    "far1": (("z", 8), ("col", 7), ("z", 10),),
+    "far2": (("far", 5), ("col", 9),),
+    "far4": (("far", 6),),
+    "far5": (("col", 8),),
+    "ffn0": (("far", 8), ("far", 7), ("far", 9), ("col", 10),),
+    "bfar4": (("b", 4),),
+    "ffn1": (("c", 4),),
+    "bfar5": (("far", 10),),
+    "bfar6": (("b", 8), ("ret", 0),),
+    "bfar7": (("b", 6),),
+    "ffn2": (("c", 8),),
+    "bfar8": (("c", 6),),
+    "bfar9": (("b", 9),),
+    "bfar10": (("b", 5), ("c", 9),),
+    "bfar11": (("c", 5), ("b", 7),),
+    "bnear0": (("e", 4),),
+    "bnear1": (("b", 10),),
+    "bnear4": (("ret", 1), ("e", 9),),
+    "bnear7": (("e", 5), ("e", 6),),
+    "bnear11": (("c", 7),),
+    "t2": (("c", 10), ("b", 2), ("b", 1),),
+    "t3": (("b", 0), ("b", 3),),
+    "t4": (("c", 0), ("c", 3), ("e", 8),),
+    "t5": (("c", 1), ("e", 3), ("c", 2), ("e", 0), ("e", 7), ("e", 2), ("e", 10), ("e", 1),),
 }
-FEED_AT = (4, 7)
+FEED_AT = (5, 8)
 
 
 def shifted(value, axis, steps):
@@ -378,7 +377,7 @@
 
 
 def chunk_list(q_cols, kv_cols, ff_cols, pieces):
-    sizes = [kv_cols, q_cols, q_cols] + [ff_cols // pieces] * (2 * pieces)
+    sizes = [kv_cols] + [q_cols // 3] * 3 + [q_cols] + [ff_cols // pieces] * (2 * pieces)
     at = 0
     out = []
     for size in sizes:
@@ -430,9 +429,9 @@
     z, y, xx = me // 4, (me // 2) % 2, me % 2
     shard_rows = w_query.shape[0]
     n_chunks = len(chunks)
-    kKV, kQ, kO = 0, 1, 2
-    kUp = [3 + 2 * c for c in range(pieces)]
-    kDown = [4 + 2 * c for c in range(pieces)]
+    kKV, kQ, kO = 0, (1, 2, 3), 4
+    kUp = [5 + 2 * c for c in range(pieces)]
+    kDown = [6 + 2 * c for c in range(pieces)]
     mine = pl.ds(pl.multiple_of(core * HDIM, HDIM), HDIM)
     other = pl.ds(pl.multiple_of((1 - core) * HDIM, HDIM), HDIM)
 
@@ -466,7 +465,7 @@
     def halves(k):
         c0, cn = chunks[k]
         if cn < 256:
-            return pl.ds(c0, cn), None
+            return (pl.ds(c0, cn), None) if k % 2 == 0 else (None, pl.ds(c0, cn))
         first = cn // 256 * 128
         return pl.ds(c0, first), pl.ds(c0 + first, cn - first)
 
@@ -480,8 +479,10 @@
 
     def gather_far(k):
         first, second = halves(k)
-        r = W.at[:, y, 1 - xx, :, first]
-        out = [send(r, r, g3s.at[k, 0], g3r.at[k, 0], y_id)]
+        out = []
+        if first is not None:
+            r = W.at[:, y, 1 - xx, :, first]
+            out.append(send(r, r, g3s.at[k, 0], g3r.at[k, 0], y_id))
         if second is not None:
             r = W.at[:, 1 - y, xx, :, second]
             out.append(send(r, r, g3s.at[k, 1], g3r.at[k, 1], x_id))
@@ -507,20 +508,28 @@
         for c in gather_far(k):
             c.wait_recv()
 
+    def span(ks):
+        ks = ks if isinstance(ks, tuple) else (ks,)
+        return ks, chunks[ks[0]][0], sum(chunks[k][1] for k in ks)
+
     def weight(k):
-        c0, cn = chunks[k]
+        _, c0, cn = span(k)
         return W[:, :, :, :, c0 : c0 + cn].reshape(D, cn)
 
     def red1(k):
         first, second = halves(k)
-        out = [send(G.at[:, :, 1 - xx, :, first], r1.at[:, :, :, first], a1s.at[k, 0], a1r.at[k, 0], x_id)]
+        out = []
+        if first is not None:
+            out.append(send(G.at[:, :, 1 - xx, :, first], r1.at[:, :, :, first], a1s.at[k, 0], a1r.at[k, 0], x_id))
         if second is not None:
             out.append(send(G.at[:, 1 - y, :, :, second], r1.at[:, :, :, second], a1s.at[k, 1], a1r.at[k, 1], y_id))
         return out
 
     def red2(k):
         first, second = halves(k)
-        out = [send(r1.at[:, 1 - y, :, first], r2.at[:, :, first], a2s.at[k, 0], a2r.at[k, 0], y_id)]
+        out = []
+        if first is not None:
+            out.append(send(r1.at[:, 1 - y, :, first], r2.at[:, :, first], a2s.at[k, 0], a2r.at[k, 0], y_id))
         if second is not None:
             out.append(send(r1.at[:, 1 - xx, :, second], r2.at[:, :, second], a2s.at[k, 1], a2r.at[k, 1], x_id))
         return out
@@ -542,7 +551,8 @@
 
         def add(i, _):
             zz, o = i // 2, i % 2
-            r1[zz, o, :, first] = r1[zz, o, :, first] + G[zz, o, xx, :, first]
+            if first is not None:
+                r1[zz, o, :, first] = r1[zz, o, :, first] + G[zz, o, xx, :, first]
             if second is not None:
                 r1[zz, o, :, second] = r1[zz, o, :, second] + G[zz, y, o, :, second]
             return 0
@@ -557,7 +567,8 @@
             c.wait_recv()
 
         def add(i, _):
-            r2[i, :, first] = r2[i, :, first] + r1[i, y, :, first]
+            if first is not None:
+                r2[i, :, first] = r2[i, :, first] + r1[i, y, :, first]
             if second is not None:
                 r2[i, :, second] = r2[i, :, second] + r1[i, xx, :, second]
             return 0
@@ -597,7 +608,7 @@
                 pl.when(i == j)(functools.partial(act, loop_name + str(j)))
 
     def place(k, block):
-        c0 = chunks[k][0]
+        _, c0, _ = span(k)
         W[z, y, xx, :, c0 : c0 + block.shape[1]] = block
 
     place(kKV, jnp.concatenate([w_keyval[...], jnp.zeros((shard_rows, HDIM), BF16)], axis=1))
@@ -699,7 +710,8 @@
     ]
     stores[0].start()
     act("own")
-    arrived(kQ)
+    for k in kQ:
+        arrived(k)
     wqT[...] = weight(kQ).T
     bq = column(b_query)
     for m in range(M):
@@ -817,17 +829,13 @@
 
     lax.fori_loop(0, M * heads, mix_dots, 0)
 
-    def put_grad(k, leftT, right):
-        c0, cn = chunks[k]
-
-        def half(i, _):
-            rows = pl.ds(pl.multiple_of(i * (D // 2), 128), D // 2)
-            part = nn(leftT[rows, :], right[...]).astype(BF16)
-            G[pl.ds(i * 2, 2), :, :, :, c0 : c0 + cn] = part.reshape(2, 2, 2, shard_rows, cn)
-            return 0
-
-        lax.fori_loop(0, 2, half, 0)
-        step_a(k)
+    def put_grad(ks, leftT, right):
+        ks, c0, cn = span(ks)
+
+        part = nn(leftT[...], right[...]).astype(BF16)
+        G[:, :, :, :, c0 : c0 + cn] = part.reshape(4, 2, 2, shard_rows, cn)
+        for k in ks:
+            step_a(k)
 
     put_grad(kO, dyT, o_nat)
     act("mix")
@@ -840,7 +848,7 @@
         up_bias = b_up[c * piece : (c + 1) * piece].reshape(1, piece)
 
         def rows_tile(i, _):
-            rows = pl.ds(pl.multiple_of(i * R, R), R)
+            rows = pl.ds(pl.multiple_of(i * 2 * R, 2 * R), 2 * R)
             u = nn(n2[rows, :], W[:, :, :, :, u0 : u0 + piece].reshape(D, piece)) + up_bias
             phi = 0.5 * (1.0 + lax.erf(u * 0.7071067811865476))
             slope = phi + u * (jnp.exp(-0.5 * u * u) * 0.3989422804014327)
@@ -849,7 +857,7 @@
             dubuf[c, rows, :] = (slope * dg).astype(BF16)
             return 0
 
-        lax.fori_loop(0, T // R, rows_tile, 0)
+        lax.fori_loop(0, T // R // 2, rows_tile, 0)
         put_grad(ku, n2T, dubuf.at[c])
         put_grad(kd, dyT, gbuf.at[:, c * piece : (c + 1) * piece])
 
@@ -1127,15 +1135,15 @@
     for load, store in zip(loads, stores):
         load.wait()
         store.start()
-    hq, half, piece, D = wq.shape[1], wkv.shape[1], chunks[3][1], vec.shape[1]
+    hq, half, piece, D = wq.shape[1], wkv.shape[1], chunks[5][1], vec.shape[1]
     for out, r in ((n1g, 0), (n1b, 1), (n2g, 2), (n2b, 3), (bo, 4), (bd, 4)):
         out[...] = vec[r].reshape(D)
-    q0, o0 = chunks[1][0], chunks[2][0]
+    q0, o0 = chunks[1][0], chunks[4][0]
     wq[...] = grads[:, q0 : q0 + hq]
     wkv[...] = grads[:, 0:half]
     wo[...] = grads[:, o0 : o0 + hq]
     for c in range(pieces):
-        u0, d0 = chunks[3 + 2 * c][0], chunks[4 + 2 * c][0]
+        u0, d0 = chunks[5 + 2 * c][0], chunks[6 + 2 * c][0]
         wu[:, c * piece : (c + 1) * piece] = grads[:, u0 : u0 + piece]
         wd[:, c * piece : (c + 1) * piece] = grads[:, d0 : d0 + piece]
     bq[...] = vec[5:6, 0:hq].reshape(hq)
@@ -1233,6 +1241,7 @@
         and up_weight.shape[1] % (PIECES * 256) == 0
         and up_weight.shape[1] >= hidden_in.shape[2]
         and hidden_in.shape[1] % 256 == 0
+        and hidden_in.shape[0] * hidden_in.shape[1] % 512 == 0
     )
 
 

time: 169 us -> 169 us (level)
  no operation moved by 1% of the time
where the time goes in v6:
time: 169 us; the launch traced here: 168 us
  Pallas kernels  168 us (99%)
    pallas_call x1, Pallas kernels, fused_layer(): pl.pallas_call(functools.partial(fused_kernel, chunks, pieces), out_shape...  163 us
    pallas_call x1, Pallas kernels, fused_layer(): pl.pallas_call(functools.partial(finish_kernel, chunks, pieces), out_shap...  5 us

profile of v6, /device:TPU:0, one launch (start us, length us, event | category | flops | bytes accessed | tf_op | source)
XLA Modules:
  0.0 168.4 jit_solution(5895598699965268938)
XLA Ops:
  0.7 162.5 %fused_layer.1 = (bf16[1024,768]{1,0:T(8,128)(2,1)}, bf16[2,512,128]{2,1,0:T(8,128)(2,1)}, bf16[1024,768]{1,0:T(8,128)(2,1)}, f32[48,3968]{1,0:T(8,128)}, f32[8,768]{1,0:T(8,128)}) custom-call(bf16[1024,768]{1,0:T(8,128)(2,1)} %bitcast.8, bf16[1024,768]{1,0:T(8,128)(2,1)} %bitcast.9, s32[2,512]{1,0:T(2,128)} %positions.1, f32[768]{0:T(1024)} %g1.1, f32[768]{0:T(1024)} %b1.1, ...), custom_call_target="tpu_custom_call" | custom-call | tf_op jit(solution)/shard_map/fused_layer/pallas_call | solution.py:1197
  163.2 5.0 %finish_layer.1 = (bf16[1024,768]{1,0:T(8,128)(2,1)}, bf16[2,512,128]{2,1,0:T(8,128)(2,1)}, bf16[1024,768]{1,0:T(8,128)(2,1)}, f32[768]{0:T(1024)}, f32[768]{0:T...) custom-call(bf16[1024,768]{1,0:T(8,128)(2,1)} %get-tuple-element.39., ...), custom_call_target="tpu_custom_call" | custom-call | tf_op jit(solution)/shard_map/finish_layer/pallas_call | solution.py:1217
